TPU v7x, 512 devices: a whole 4x4x16 slice. The times are simulated.
512 devices in a mesh: dp: 16 (over y_lo, x, core), ctx: 32 (over y_hi, z).
Axes of the slice: x: 4, y: 4 (y_hi: 2, y_lo: 2; y = y_hi * 2 + y_lo), z: 16, core: 2. Of those that a mesh axis runs over, the one named last changes fastest.
Arguments:
- tokens: bfloat16 [16, 32, 128, 3072], P('dp', 'ctx'), may hold values from -6 to 6
- modulation: float32 [16, 3, 3072], P('dp'), may hold values from -3 to 3
- query_key_value_weight: bfloat16 [3072, 1536], P('dp'), may hold values from -0.109375 to 0.109375
- output_projection_weight: bfloat16 [512, 3072], P(None, 'dp'), may hold values from -0.25 to 0.25
- adapter_down_maps: bfloat16 [3072, 64], P('dp'), may hold values from -0.109375 to 0.109375
- adapter_up_maps: bfloat16 [64, 512], P('dp'), may hold values from -1 to 1
- output_gradient: bfloat16 [16, 32, 128, 3072], P('dp', 'ctx'), may hold values from -6 to 6
Outputs:
- mixed_out: bfloat16 [16, 32, 128, 3072], P('dp', 'ctx')
- tokens_grad: bfloat16 [16, 32, 128, 3072], P('dp', 'ctx')
- modulation_grad: float32 [16, 3, 3072], P('dp')
- down_grad: float32 [3072, 64], P('dp')
- up_grad: float32 [64, 512], P('dp')
All inputs are finite; a program needn't handle non-finite values.
Results may differ from a plain program's by a relative error of at most 0.019.
Values may be sent and summed in bfloat16 or wider, within the bound.
No kernel may reach another device: no remote copies, remote signals or barrier semaphores. Data moves between devices by JAX's collectives and lax.ppermute only.
A program may use at most 128 MiB of HBM per device.

v0:
```python
import jax
import jax.numpy as jnp
from jax import lax
from jax.sharding import PartitionSpec as P

HEAD_SIZE = 128


EPSILON = 1e-06


def side_by_side(arrays, axis, split_dim, concat_dim, along):
    both = jnp.concatenate(arrays, axis=along)
    out, at, gathered = (
        lax.all_to_all(both, axis, split_axis=split_dim, concat_axis=concat_dim, tiled=True),
        0,
        [],
    )
    for a in arrays:
        gathered.append(lax.slice_in_dim(out, at, at + a.shape[along], axis=along))
        at += a.shape[along]
    return tuple(gathered)


def in_blocks(array, dim, peers):
    lengths = array.shape
    tiles = array.reshape(*lengths[:dim], peers, lengths[dim] // peers, *lengths[dim + 1 :])
    return jnp.moveaxis(tiles, dim, 0)


def sent_and_summed(array, axis, dim):
    tiles = in_blocks(array, dim, lax.axis_size(axis))
    arrived = lax.all_to_all(tiles, axis, split_axis=0, concat_axis=0, tiled=True)
    return arrived.astype(jnp.float32).sum(axis=0)


def sent_to_all(array, axis):
    peers = lax.axis_size(axis)
    return lax.all_to_all(
        jnp.broadcast_to(array[None], (peers, *array.shape)), axis, 0, 0, tiled=True
    )


def over_copies(array, axis):
    return sent_to_all(array, axis).astype(jnp.float32).sum(axis=0)


def times_transposed(left, right):
    return lax.dot_general(
        left, right, (((1,), (1,)), ((), ())), preferred_element_type=jnp.float32
    )


def transposed_times(left, right):
    return lax.dot_general(
        left, right, (((0,), (0,)), ((), ())), preferred_element_type=jnp.float32
    )


def normalize_rows(flat_tokens, modulation_per_clip):
    values = flat_tokens.astype(jnp.float32)
    center = values - jnp.mean(values, -1, keepdims=True)
    inverse_value = lax.rsqrt(jnp.mean(center * center, -1, keepdims=True) + EPSILON)
    normalized_input = center * inverse_value
    hidden_state = (
        normalized_input * (1.0 + modulation_per_clip[1]) + modulation_per_clip[0]
    ).astype(jnp.bfloat16)
    return (normalized_input, inverse_value, hidden_state)


def projection_forward(hidden_state, qkv_full, down_full, up_full, adapter_inner_rank):
    head_size_value = up_full.shape[1]
    base_proj = jnp.dot(hidden_state, qkv_full, preferred_element_type=jnp.float32)
    low_rank_product = jnp.dot(hidden_state, down_full, preferred_element_type=jnp.float32).astype(
        jnp.bfloat16
    )
    delta_query = jnp.dot(
        low_rank_product[:, :adapter_inner_rank],
        up_full[:adapter_inner_rank],
        preferred_element_type=jnp.float32,
    )
    delta_value = jnp.dot(
        low_rank_product[:, adapter_inner_rank:],
        up_full[adapter_inner_rank:],
        preferred_element_type=jnp.float32,
    )
    query_unnormalized = base_proj[:, :head_size_value] + delta_query
    key_unnormalized = base_proj[:, head_size_value : 2 * head_size_value]
    value_row_matrix = (base_proj[:, 2 * head_size_value :] + delta_value).astype(jnp.bfloat16)
    return (low_rank_product, query_unnormalized, key_unnormalized, value_row_matrix)


def head_stats(raw_rows, head_dim):
    grouped = raw_rows.reshape(raw_rows.shape[0], -1, head_dim)
    inverse_value = lax.rsqrt(jnp.mean(grouped * grouped, -1, keepdims=True) + EPSILON)
    return (grouped, inverse_value)


def head_normed(raw_rows, head_dim):
    grouped, inverse_value = head_stats(raw_rows, head_dim)
    return (grouped * inverse_value).reshape(raw_rows.shape).astype(jnp.bfloat16)


def head_norm_back(raw_rows, incoming_grad, head_dim):
    grouped, inverse_value = head_stats(raw_rows, head_dim)
    incoming = incoming_grad.astype(jnp.float32).reshape(grouped.shape)
    inner_mean = jnp.mean(grouped * incoming, -1, keepdims=True)
    return (inverse_value * incoming - grouped * inverse_value**3 * inner_mean).reshape(
        raw_rows.shape
    )


def split_heads(rows_in, head_dim):
    frame_count, place_count, head_size_value = rows_in.shape
    return rows_in.reshape(frame_count, place_count, head_size_value // head_dim, head_dim)


def attend(query_rows, key_rows, value_row_matrix, head_dim):
    score_scale = head_dim ** (-0.5)
    query_heads = split_heads(query_rows, head_dim)
    key_heads = split_heads(key_rows, head_dim)
    value_heads = split_heads(value_row_matrix, head_dim)
    scores = (
        jnp.einsum("fphd,gphd->phfg", query_heads, key_heads, preferred_element_type=jnp.float32)
        * score_scale
    )
    expo = jnp.exp(scores)
    attention_weights = expo / jnp.sum(expo, -1, keepdims=True)
    weights_low = attention_weights.astype(jnp.bfloat16)
    attended = jnp.einsum(
        "phfg,gphd->fphd", weights_low, value_heads, preferred_element_type=jnp.float32
    ).astype(jnp.bfloat16)
    return (attended.reshape(query_rows.shape), attention_weights)


def attend_back(attended_grad, attention_weights, query_rows, key_rows, value_row_matrix, head_dim):
    score_scale = head_dim ** (-0.5)
    grad_heads = split_heads(attended_grad, head_dim)
    query_heads = split_heads(query_rows, head_dim)
    key_heads = split_heads(key_rows, head_dim)
    value_heads = split_heads(value_row_matrix, head_dim)
    weights_low = attention_weights.astype(jnp.bfloat16)
    prob_grad = jnp.einsum(
        "fphd,gphd->phfg", grad_heads, value_heads, preferred_element_type=jnp.float32
    )
    value_gradient = jnp.einsum(
        "phfg,fphd->gphd", weights_low, grad_heads, preferred_element_type=jnp.float32
    ).astype(jnp.bfloat16)
    score_grad = attention_weights * (
        prob_grad - jnp.sum(attention_weights * prob_grad, -1, keepdims=True)
    )
    score_low = (score_grad * score_scale).astype(jnp.bfloat16)
    query_grad = jnp.einsum(
        "phfg,gphd->fphd", score_low, key_heads, preferred_element_type=jnp.float32
    ).astype(jnp.bfloat16)
    key_grad = jnp.einsum(
        "phfg,fphd->gphd", score_low, query_heads, preferred_element_type=jnp.float32
    ).astype(jnp.bfloat16)
    shape_rows = query_rows.shape
    return (
        query_grad.reshape(shape_rows),
        key_grad.reshape(shape_rows),
        value_gradient.reshape(shape_rows),
    )


def projection_backward(
    query_normalized_gradient,
    key_normalized_gradient,
    value_gradient,
    query_unnormalized,
    key_unnormalized,
    hidden_state,
    low_rank_product,
    normalized_input,
    inverse_value,
    modulation_per_clip,
    qkv_full,
    down_full,
    up_full,
    adapter_inner_rank,
    head_dim,
):
    head_size_value = up_full.shape[1]
    query_back = head_norm_back(query_unnormalized, query_normalized_gradient, head_dim)
    key_back = head_norm_back(key_unnormalized, key_normalized_gradient, head_dim)
    joined_grad = jnp.concatenate(
        [query_back, key_back, value_gradient.astype(jnp.float32)], 1
    ).astype(jnp.bfloat16)
    query_block = joined_grad[:, :head_size_value]
    value_block = joined_grad[:, 2 * head_size_value :]
    up_grad = jnp.concatenate(
        [
            transposed_times(low_rank_product[:, :adapter_inner_rank], query_block),
            transposed_times(low_rank_product[:, adapter_inner_rank:], value_block),
        ],
        0,
    )
    low_grad = jnp.concatenate(
        [
            times_transposed(query_block, up_full[:adapter_inner_rank]),
            times_transposed(value_block, up_full[adapter_inner_rank:]),
        ],
        1,
    ).astype(jnp.bfloat16)
    hidden_grad = times_transposed(joined_grad, qkv_full) + times_transposed(low_grad, down_full)
    down_grad = transposed_times(hidden_state, low_grad)
    shift_gradient = jnp.sum(hidden_grad, 0)
    scale_gradient = jnp.sum(hidden_grad * normalized_input, 0)
    normed_grad = hidden_grad * (1.0 + modulation_per_clip[1])
    first_mean = jnp.mean(normed_grad, -1, keepdims=True)
    second_mean = jnp.mean(normed_grad * normalized_input, -1, keepdims=True)
    token_gradient_rows = inverse_value * (
        normed_grad - first_mean - normalized_input * second_mean
    )
    return (token_gradient_rows, shift_gradient, scale_gradient, down_grad, up_grad)


def per_device(
    tokens,
    modulation,
    query_key_value_weight,
    output_projection_weight,
    adapter_down_maps,
    adapter_up_maps,
    output_gradient,
):
    adapter_inner_rank = adapter_down_maps.shape[1] // 2
    head_dim = HEAD_SIZE
    qkv_full, out_full, down_full, up_full = (
        lax.all_gather(query_key_value_weight, "dp", axis=0, tiled=True),
        lax.all_gather(output_projection_weight, "dp", axis=1, tiled=True),
        lax.all_gather(adapter_down_maps, "dp", axis=0, tiled=True),
        lax.all_gather(adapter_up_maps, "dp", axis=0, tiled=True),
    )
    head_size_value = up_full.shape[1]
    local_shape = tokens.shape
    frame_shape = (1, local_shape[1], local_shape[2], head_size_value)
    modulation_per_clip = modulation[0]
    flat_tokens = tokens.reshape(-1, local_shape[3])
    normalized_input, inverse_value, hidden_state = normalize_rows(flat_tokens, modulation_per_clip)
    low_rank_product, query_unnormalized, key_unnormalized, value_row_matrix = projection_forward(
        hidden_state, qkv_full, down_full, up_full, adapter_inner_rank
    )
    query_rows = head_normed(query_unnormalized, head_dim)
    key_rows = head_normed(key_unnormalized, head_dim)
    upstream = output_gradient.reshape(-1, local_shape[3]).astype(jnp.float32)
    branch_grad = (upstream * modulation_per_clip[2]).astype(jnp.bfloat16)
    attended_grad = (
        times_transposed(branch_grad, out_full).astype(jnp.bfloat16).reshape(frame_shape)
    )
    query_place, key_place, value_place, grad_place = side_by_side(
        (
            query_rows.reshape(frame_shape),
            key_rows.reshape(frame_shape),
            value_row_matrix.reshape(frame_shape),
            attended_grad,
        ),
        "ctx",
        2,
        1,
        0,
    )
    attended, attention_weights = attend(query_place[0], key_place[0], value_place[0], head_dim)
    query_normalized_gradient, key_normalized_gradient, value_gradient = attend_back(
        grad_place[0], attention_weights, query_place[0], key_place[0], value_place[0], head_dim
    )
    attended_frames, query_back_frames, key_back_frames, value_back_frames = (
        lax.all_to_all(attended[None], "ctx", split_axis=1, concat_axis=2, tiled=True),
        lax.all_to_all(
            query_normalized_gradient[None], "ctx", split_axis=1, concat_axis=2, tiled=True
        ),
        lax.all_to_all(
            key_normalized_gradient[None], "ctx", split_axis=1, concat_axis=2, tiled=True
        ),
        lax.all_to_all(value_gradient[None], "ctx", split_axis=1, concat_axis=2, tiled=True),
    )
    branch_out = jnp.dot(
        attended_frames.reshape(-1, head_size_value), out_full, preferred_element_type=jnp.float32
    )
    mixed_out = (flat_tokens.astype(jnp.float32) + modulation_per_clip[2] * branch_out).astype(
        jnp.bfloat16
    )
    gate_grad = jnp.sum(upstream * branch_out, 0)
    token_gradient_rows, shift_gradient, scale_gradient, down_section, up_section = (
        projection_backward(
            query_back_frames.reshape(-1, head_size_value),
            key_back_frames.reshape(-1, head_size_value),
            value_back_frames.reshape(-1, head_size_value),
            query_unnormalized,
            key_unnormalized,
            hidden_state,
            low_rank_product,
            normalized_input,
            inverse_value,
            modulation_per_clip,
            qkv_full,
            down_full,
            up_full,
            adapter_inner_rank,
            head_dim,
        )
    )
    tokens_grad = (upstream + token_gradient_rows).astype(jnp.bfloat16)
    token_total = lax.axis_size("dp") * lax.axis_size("ctx") * flat_tokens.shape[0]
    grad_scale = token_total ** (-0.5)
    modulation_part = jnp.stack([shift_gradient, scale_gradient, gate_grad], 0)[None] * grad_scale
    down_section = down_section * grad_scale
    up_section = up_section * grad_scale
    down_share, up_share = (
        sent_and_summed(down_section.astype(jnp.bfloat16), "dp", 0),
        sent_and_summed(up_section.astype(jnp.bfloat16), "dp", 0),
    )
    down_grad, up_grad, modulation_grad = (
        over_copies(down_share.astype(jnp.bfloat16), "ctx").astype(jnp.float32),
        over_copies(up_share.astype(jnp.bfloat16), "ctx").astype(jnp.float32),
        over_copies(modulation_part.astype(jnp.bfloat16), "ctx").astype(jnp.float32),
    )
    return (
        mixed_out.reshape(local_shape),
        tokens_grad.reshape(local_shape),
        modulation_grad,
        down_grad,
        up_grad,
    )


def solution(mesh):
    return jax.shard_map(
        per_device,
        mesh=mesh,
        in_specs=(
            P("dp", "ctx", None, None),
            P("dp", None, None),
            P("dp", None),
            P(None, "dp"),
            P("dp", None),
            P("dp", None),
            P("dp", "ctx", None, None),
        ),
        out_specs=(
            P("dp", "ctx", None, None),
            P("dp", "ctx", None, None),
            P("dp", None, None),
            P("dp", None),
            P("dp", None),
        ),
        check_vma=False,
    )
```

profile of v0, /device:TPU:24, one launch (start us, length us, event | category | flops | bytes accessed | tf_op | source)
XLA Modules:
  0.0 464.9 jit_solution(1186287801281636129)
XLA Ops:
  8.7 19.4 %all-gather.1 = bf16[16,4,512]{2,1,0:T(4,128)(2,1)S(1)} all-gather(bf16[1,4,512]{2,1,0:T(4,128)(2,1)} %bitcast.182), channel_id=1, replica_groups=mesh['dp'=16,'ctx'=32] {'dp'}, dimensions={0}, use_global_device_ids=true | all-gather | bytes 69632 | tf_op jit(solution)/shard_map/all_gather | solution.py:234
  28.2 18.2 %all-gather = bf16[16,192,64]{1,2,0:T(8,128)(2,1)S(1)} all-gather(bf16[1,192,64]{1,2,0:T(8,128)(2,1)} %bitcast.178), channel_id=1, replica_groups=mesh['dp'=16,'ctx'=32] {'dp'}, dimensions={0}, use_global_device_ids=true | all-gather | bytes 417792 | tf_op jit(solution)/shard_map/all_gather | solution.py:233
  48.4 10.2 %all-gather.7.cloned.1.call-done = bf16[512,3072]{0,1:T(8,128)(2,1)} async-done(((bf16[512,192]{0,1:T(8,128)(2,1)}), bf16[512,3072]{0,1:T(8,128)(2,1)}) %all-gather.7.cloned.1.call-update) | async-done | bytes 3145744 | tf_op jit(solution)/shard_map/all_gather | solution.py:232
  58.6 2.5 fusion.32
  61.1 65.4 %all-gather.5.cloned.1.call-done = bf16[3072,1536]{1,0:T(8,128)(2,1)} async-done(((bf16[192,1536]{1,0:T(8,128)(2,1)}), bf16[3072,1536]{1,0:T(8,128)(2,1)}) %all-gather.5.cloned.1.call-update) | async-done | bytes 9437200 | tf_op jit(solution)/shard_map/all_gather | solution.py:231
  126.5 5.1 %fusion.95 = f32[128,1536]{1,0:T(8,128)S(1)} fusion(bf16[3072,1536]{1,0:T(8,128)(2,1)} %all-gather.5.cloned.1.call-done, bf16[1,1,128,3072]{3,2,1,0:T(8,128)(2,1)S(1)} %copy-done, f32[3072]{0:T(1024)S(1)} %bitcast.180, f32[3072]{0:T(1024)S(1)} %bitcast.169, f32[128]{0:T(128)S(1)} %add_rsqrt_fusion.2, f32[128]{0:T(128)S(1)} %broadcast_multiply_fusion.4), kind=kOutput, calls=%fused_computation.140 | convolution fusion | flops 1210318848 | bytes 11035648 | tf_op jit(solution)/shard_map/dot_general | solution.py:73
  137.2 45.3 %all_to_all.70 = bf16[4,1,128,512]{3,0,1,2:T(4,128)(2,1)S(1)} all-to-all(bf16[4,1,128,512]{3,0,1,2:T(4,128)(2,1)S(1)} %copy.203), channel_id=1, replica_groups=mesh['dp'=16,'ctx'=32] {'ctx'}, dimensions={2} | all-to-all | bytes 1048576 | tf_op jit(solution)/shard_map/all_to_all | solution.py:15
  182.5 2.9 slice_reduce_fusion
  190.0 1.8 fusion.62
  191.8 1.9 fusion.58
  193.8 2.1 fusion.29
  197.5 8.1 %all-to-all-start.3 = ((bf16[1,32,4,512]{3,2,0,1:T(4,128)(2,1)}), bf16[1,32,4,512]{3,2,0,1:T(4,128)(2,1)S(1)}, u32[]{:S(2)}, u32[]{:S(2)}) async-start(bf16[1,32,4,512]{3,2,0,1:T(4,128)(2,1)} %reshape.247), calls=%async_computation.3 | async-start | bytes 262144 | tf_op jit(solution)/shard_map/all_to_all | solution.py:273
  209.6 1.9 fusion.30
  213.2 7.8 %all-to-all-done.3 = bf16[1,32,4,512]{3,2,0,1:T(4,128)(2,1)S(1)} async-done(((bf16[1,32,4,512]{3,2,0,1:T(4,128)(2,1)}), bf16[1,32,4,512]{3,2,0,1:T(4,128)(2,1)S(1)}, u32[]{:S(2)}, u32[]{:S(2)}) %all-to-all-start.3) | async-done | bytes 131104 | tf_op jit(solution)/shard_map/all_to_all | solution.py:273
  221.0 6.8 %all-to-all-start.4 = ((bf16[1,32,4,512]{3,2,0,1:T(4,128)(2,1)}), bf16[1,32,4,512]{3,2,0,1:T(4,128)(2,1)S(1)}, u32[]{:S(2)}, u32[]{:S(2)}) async-start(bf16[1,32,4,512]{3,2,0,1:T(4,128)(2,1)} %reshape.248), calls=%async_computation.4 | async-start | bytes 262144 | tf_op jit(solution)/shard_map/all_to_all | solution.py:276
  227.8 2.0 fusion.27
  233.0 2.1 fusion.28
  242.6 13.0 %all-to-all-start.2 = ((bf16[1,32,4,512]{3,2,0,1:T(4,128)(2,1)}), bf16[1,32,4,512]{3,2,0,1:T(4,128)(2,1)S(1)}, u32[]{:S(2)}, u32[]{:S(2)}) async-start(bf16[1,32,4,512]{3,2,0,1:T(4,128)(2,1)} %reshape.246), calls=%async_computation.2 | async-start | bytes 262144 | tf_op jit(solution)/shard_map/all_to_all | solution.py:270
  259.5 10.4 %all-to-all-done.2 = bf16[1,32,4,512]{3,2,0,1:T(4,128)(2,1)S(1)} async-done(((bf16[1,32,4,512]{3,2,0,1:T(4,128)(2,1)}), bf16[1,32,4,512]{3,2,0,1:T(4,128)(2,1)S(1)}, u32[]{:S(2)}, u32[]{:S(2)}) %all-to-all-start.2) | async-done | bytes 131104 | tf_op jit(solution)/shard_map/all_to_all | solution.py:270
  269.9 7.3 %all-to-all-start.1 = ((bf16[1,32,4,512]{3,2,0,1:T(4,128)(2,1)}), bf16[1,32,4,512]{3,2,0,1:T(4,128)(2,1)}, u32[]{:S(2)}, u32[]{:S(2)}) async-start(bf16[1,32,4,512]{3,2,0,1:T(4,128)(2,1)} %reshape.245), calls=%async_computation.1 | async-start | bytes 262144 | tf_op jit(solution)/shard_map/all_to_all | solution.py:269
  284.6 6.8 %fusion.42 = f32[128,3072]{1,0:T(8,128)S(1)} fusion(bf16[3072,1536]{1,0:T(8,128)(2,1)} %all-gather.5.cloned.1.call-done, bf16[128,512]{1,0:T(8,128)(2,1)S(1)} %convert_element_type.165, bf16[128,512]{1,0:T(8,128)(2,1)S(1)} %fusion.49, bf16[128,512]{1,0:T(8,128)(2,1)S(1)} %fusion.51), kind=kOutput, calls=%fused_computation.62 | convolution fusion | flops 1209139200 | bytes 11403264 | tf_op jit(solution)/shard_map/dot_general | solution.py:49
  293.6 5.4 %all-to-all-start.8 = ((bf16[16,4,512]{2,1,0:T(4,128)(2,1)}), bf16[16,4,512]{2,1,0:T(4,128)(2,1)}, u32[]{:S(2)}, u32[]{:S(2)}) async-start(bf16[16,4,512]{2,1,0:T(4,128)(2,1)} %convert_element_type.172), calls=%async_computation.8 | async-start | bytes 131072 | tf_op jit(solution)/shard_map/all_to_all | solution.py:33
  301.7 2.0 copy.229
  304.6 5.7 %all-to-all-start.6 = ((bf16[16,192,64]{1,2,0:T(8,128)(2,1)}), bf16[16,192,64]{1,2,0:T(8,128)(2,1)}, u32[]{:S(2)}, u32[]{:S(2)}) async-start(bf16[16,192,64]{1,2,0:T(8,128)(2,1)} %copy.229), calls=%async_computation.6 | async-start | bytes 1048576 | tf_op jit(solution)/shard_map/all_to_all | solution.py:33
  311.3 8.7 %all-to-all-done.6 = bf16[16,192,64]{1,2,0:T(8,128)(2,1)} async-done(((bf16[16,192,64]{1,2,0:T(8,128)(2,1)}), bf16[16,192,64]{1,2,0:T(8,128)(2,1)}, u32[]{:S(2)}, u32[]{:S(2)}) %all-to-all-start.6) | async-done | bytes 393248 | tf_op jit(solution)/shard_map/all_to_all | solution.py:33
  320.7 14.6 %all-to-all-start.9 = ((bf16[32,4,512]{2,1,0:T(4,128)(2,1)}), bf16[32,4,512]{2,1,0:T(4,128)(2,1)S(1)}, u32[]{:S(2)}, u32[]{:S(2)}) async-start(bf16[32,4,512]{2,1,0:T(4,128)(2,1)} %broadcast_in_dim.8), calls=%async_computation.9 | async-start | bytes 262144 | tf_op jit(solution)/shard_map/all_to_all | solution.py:39
  335.3 4.7 %fusion.20 = (f32[3072]{0:T(1024)S(1)}, bf16[1,1,128,3072]{3,2,1,0:T(8,128)(2,1)}, bf16[1,1,128,3072]{3,2,1,0:T(8,128)(2,1)}) fusion(bf16[1,1,128,3072]{3,2,1,0:T(8,128)(2,1)S(1)} %copy-done.1, f32[3072]{0:T(1024)S(1)} %bitcast.174, bf16[1,1,128,3072]{3,2,1,0:T(8,128)(2,1)S(1)} %copy-done, f32[128]{0:T(128)S(1)} %broadcast_multiply_fusion.2, ...), kind=kOutput, calls=%fused_computation.28 | convolution fusion | flops 408941568 | bytes 8034304 | tf_op jit(solution)/shard_map/dot_general | solution.py:278
  340.1 11.0 %all-to-all-done.9 = bf16[32,4,512]{2,1,0:T(4,128)(2,1)S(1)} async-done(((bf16[32,4,512]{2,1,0:T(4,128)(2,1)}), bf16[32,4,512]{2,1,0:T(4,128)(2,1)S(1)}, u32[]{:S(2)}, u32[]{:S(2)}) %all-to-all-start.9) | async-done | bytes 131104 | tf_op jit(solution)/shard_map/all_to_all | solution.py:39
  352.2 6.7 %all-to-all-start.5 = ((bf16[32,1,3,3072]{3,2,1,0:T(4,128)(2,1)}), bf16[32,1,3,3072]{3,2,1,0:T(4,128)(2,1)S(1)}, u32[]{:S(2)}, u32[]{:S(2)}) async-start(bf16[32,1,3,3072]{3,2,1,0:T(4,128)(2,1)} %broadcast_in_dim.6), calls=%async_computation.5 | async-start | bytes 1572864 | tf_op jit(solution)/shard_map/all_to_all | solution.py:39
  360.0 37.9 %all-to-all-done.5 = bf16[32,1,3,3072]{3,2,1,0:T(4,128)(2,1)S(1)} async-done(((bf16[32,1,3,3072]{3,2,1,0:T(4,128)(2,1)}), bf16[32,1,3,3072]{3,2,1,0:T(4,128)(2,1)S(1)}, u32[]{:S(2)}, u32[]{:S(2)}) %all-to-all-start.5) | async-done | bytes 589856 | tf_op jit(solution)/shard_map/all_to_all | solution.py:39
  399.0 8.8 %all-to-all-start.7 = ((bf16[32,192,64]{1,2,0:T(8,128)(2,1)}), bf16[32,192,64]{1,2,0:T(8,128)(2,1)S(1)}, u32[]{:S(2)}, u32[]{:S(2)}) async-start(bf16[32,192,64]{1,2,0:T(8,128)(2,1)} %broadcast_in_dim.7), calls=%async_computation.7 | async-start | bytes 2097152 | tf_op jit(solution)/shard_map/all_to_all | solution.py:39
  409.4 47.8 %all-to-all-done.7 = bf16[32,192,64]{1,2,0:T(8,128)(2,1)S(1)} async-done(((bf16[32,192,64]{1,2,0:T(8,128)(2,1)}), bf16[32,192,64]{1,2,0:T(8,128)(2,1)S(1)}, u32[]{:S(2)}, u32[]{:S(2)}) %all-to-all-start.7) | async-done | bytes 786464 | tf_op jit(solution)/shard_map/all_to_all | solution.py:39
  (144 shorter events, 55.9 us)
Async XLA Ops:
  7.2 51.4 %all-gather.7.cloned.1.call-start = ((), (), s32[]{:S(2)}) async-start(), calls=%async_computation.11 | async-start | bytes 3342336 | tf_op jit(solution)/shard_map/all_gather | solution.py:232
  7.9 118.6 %all-gather.5.cloned.1.call-start = ((), (), s32[]{:S(2)}) async-start(), calls=%async_computation.10 | async-start | bytes 10027008 | tf_op jit(solution)/shard_map/all_gather | solution.py:231
  8.6 38.6 %copy-start = (bf16[1,1,128,3072]{3,2,1,0:T(8,128)(2,1)S(1)}, bf16[1,1,128,3072]{3,2,1,0:T(8,128)(2,1)}, u32[]{:S(2)}) copy-start(bf16[1,1,128,3072]{3,2,1,0:T(8,128)(2,1)} %param.7) | copy-start | bytes 2359300
  28.1 104.4 %copy-start.6 = (bf16[32,512]{1,0:T(8,128)(2,1)}, bf16[32,512]{1,0:T(8,128)(2,1)S(1)}, u32[]{:S(2)}) copy-start(bf16[32,512]{1,0:T(8,128)(2,1)S(1)} %reshape.243) | copy-start | bytes 98308
  28.1 103.5 %copy-start.8 = (bf16[32,512]{1,0:T(8,128)(2,1)}, bf16[32,512]{1,0:T(8,128)(2,1)S(1)}, u32[]{:S(2)}) copy-start(bf16[32,512]{1,0:T(8,128)(2,1)S(1)} %reshape.244) | copy-start | bytes 98308
  47.4 79.1 %copy-start.21 = (f32[128]{0:T(128)}, f32[128]{0:T(128)S(1)}, u32[]{:S(2)}) copy-start(f32[128]{0:T(128)S(1)} %broadcast_multiply_fusion.4) | copy-start | bytes 1540
  47.4 11.2 %copy-start.1 = (bf16[1,1,128,3072]{3,2,1,0:T(8,128)(2,1)S(1)}, bf16[1,1,128,3072]{3,2,1,0:T(8,128)(2,1)}, u32[]{:S(2)}) copy-start(bf16[1,1,128,3072]{3,2,1,0:T(8,128)(2,1)} %param.13) | copy-start | bytes 2359300
  47.8 78.7 %copy-start.23 = (f32[128]{0:T(128)}, f32[128]{0:T(128)S(1)}, u32[]{:S(2)}) copy-start(f32[128]{0:T(128)S(1)} %add_rsqrt_fusion.2) | copy-start | bytes 1540
  47.8 13.2 %copy-start.11 = (f32[1,1,3072]{2,0,1:T(1,128)}, f32[1,1,3072]{2,0,1:T(1,128)S(1)}, u32[]{:S(2)}) copy-start(f32[1,1,3072]{2,0,1:T(1,128)S(1)} %get-tuple-element.39) | copy-start | bytes 36868
  47.8 78.6 %copy-start.20 = (f32[1,1,3072]{2,0,1:T(1,128)}, f32[1,1,3072]{2,0,1:T(1,128)S(1)}, u32[]{:S(2)}) copy-start(f32[1,1,3072]{2,0,1:T(1,128)S(1)} %get-tuple-element.40) | copy-start | bytes 36868
  48.4 84.1 %copy-start.13 = (bf16[128,64]{0,1:T(8,128)(2,1)}, bf16[128,64]{0,1:T(8,128)(2,1)S(1)}, u32[]{:S(2)}) copy-start(bf16[128,64]{0,1:T(8,128)(2,1)S(1)} %convolution_convert_fusion.5) | copy-start | bytes 49156
  191.8 16.0 %copy-start.3 = (bf16[32,4,4,128]{3,2,1,0:T(4,128)(2,1)S(1)}, bf16[32,4,4,128]{3,2,1,0:T(4,128)(2,1)}, u32[]{:S(2)}) copy-start(bf16[32,4,4,128]{3,2,1,0:T(4,128)(2,1)} %reshape_squeeze.17) | copy-start | bytes 393220
  197.5 23.5 %all-to-all-start.3 = ((bf16[1,32,4,512]{3,2,0,1:T(4,128)(2,1)}), bf16[1,32,4,512]{3,2,0,1:T(4,128)(2,1)S(1)}, u32[]{:S(2)}, u32[]{:S(2)}) async-start(bf16[1,32,4,512]{3,2,0,1:T(4,128)(2,1)} %reshape.247), calls=%async_computation.3 | async-start | bytes 262144 | tf_op jit(solution)/shard_map/all_to_all | solution.py:273
  221.0 21.7 %all-to-all-start.4 = ((bf16[1,32,4,512]{3,2,0,1:T(4,128)(2,1)}), bf16[1,32,4,512]{3,2,0,1:T(4,128)(2,1)S(1)}, u32[]{:S(2)}, u32[]{:S(2)}) async-start(bf16[1,32,4,512]{3,2,0,1:T(4,128)(2,1)} %reshape.248), calls=%async_computation.4 | async-start | bytes 262144 | tf_op jit(solution)/shard_map/all_to_all | solution.py:276
  242.6 27.3 %all-to-all-start.2 = ((bf16[1,32,4,512]{3,2,0,1:T(4,128)(2,1)}), bf16[1,32,4,512]{3,2,0,1:T(4,128)(2,1)S(1)}, u32[]{:S(2)}, u32[]{:S(2)}) async-start(bf16[1,32,4,512]{3,2,0,1:T(4,128)(2,1)} %reshape.246), calls=%async_computation.2 | async-start | bytes 262144 | tf_op jit(solution)/shard_map/all_to_all | solution.py:270
  257.1 22.8 %copy-start.10 = (f32[128,4]{1,0:T(8,128)S(1)}, f32[128,4]{1,0:T(8,128)}, u32[]{:S(2)}) copy-start(f32[128,4]{1,0:T(8,128)} %copy.216) | copy-start | bytes 6148
  269.9 23.6 %all-to-all-start.1 = ((bf16[1,32,4,512]{3,2,0,1:T(4,128)(2,1)}), bf16[1,32,4,512]{3,2,0,1:T(4,128)(2,1)}, u32[]{:S(2)}, u32[]{:S(2)}) async-start(bf16[1,32,4,512]{3,2,0,1:T(4,128)(2,1)} %reshape.245), calls=%async_computation.1 | async-start | bytes 262144 | tf_op jit(solution)/shard_map/all_to_all | solution.py:269
  284.5 6.8 %copy-start.7 = (bf16[32,512]{1,0:T(8,128)(2,1)S(1)}, bf16[32,512]{1,0:T(8,128)(2,1)}, u32[]{:S(2)}) copy-start(bf16[32,512]{1,0:T(8,128)(2,1)} %copy-done.6) | copy-start | bytes 98308
  284.5 7.6 %copy-start.18 = (bf16[128,32]{0,1:T(8,128)(2,1)S(1)}, bf16[128,32]{0,1:T(8,128)(2,1)}, u32[]{:S(2)}) copy-start(bf16[128,32]{0,1:T(8,128)(2,1)} %convolution_convert_fusion.6) | copy-start | bytes 24580
  284.5 7.6 %copy-start.22 = (f32[128]{0:T(128)S(1)}, f32[128]{0:T(128)}, u32[]{:S(2)}) copy-start(f32[128]{0:T(128)} %copy-done.21) | copy-start | bytes 1540
  284.5 7.6 %copy-start.24 = (f32[128]{0:T(128)S(1)}, f32[128]{0:T(128)}, u32[]{:S(2)}) copy-start(f32[128]{0:T(128)} %copy-done.23) | copy-start | bytes 1540
  293.6 11.1 %all-to-all-start.8 = ((bf16[16,4,512]{2,1,0:T(4,128)(2,1)}), bf16[16,4,512]{2,1,0:T(4,128)(2,1)}, u32[]{:S(2)}, u32[]{:S(2)}) async-start(bf16[16,4,512]{2,1,0:T(4,128)(2,1)} %convert_element_type.172), calls=%async_computation.8 | async-start | bytes 131072 | tf_op jit(solution)/shard_map/all_to_all | solution.py:33
  301.7 8.7 %copy-start.27 = (f32[128]{0:T(128)S(1)}, f32[128]{0:T(128)}, u32[]{:S(2)}) copy-start(f32[128]{0:T(128)} %get-tuple-element.26) | copy-start | bytes 1540
  301.7 8.7 %copy-start.26 = (f32[128]{0:T(128)S(1)}, f32[128]{0:T(128)}, u32[]{:S(2)}) copy-start(f32[128]{0:T(128)} %get-tuple-element.27) | copy-start | bytes 1540
  301.7 33.6 %copy-start.12 = (f32[1,1,3072]{2,0,1:T(1,128)S(1)}, f32[1,1,3072]{2,0,1:T(1,128)}, u32[]{:S(2)}) copy-start(f32[1,1,3072]{2,0,1:T(1,128)} %copy-done.11) | copy-start | bytes 36868
  301.7 33.6 %copy-start.25 = (f32[128]{0:T(128)S(1)}, f32[128]{0:T(128)}, u32[]{:S(2)}) copy-start(f32[128]{0:T(128)} %copy-done.23) | copy-start | bytes 1540
  304.6 15.3 %all-to-all-start.6 = ((bf16[16,192,64]{1,2,0:T(8,128)(2,1)}), bf16[16,192,64]{1,2,0:T(8,128)(2,1)}, u32[]{:S(2)}, u32[]{:S(2)}) async-start(bf16[16,192,64]{1,2,0:T(8,128)(2,1)} %copy.229), calls=%async_computation.6 | async-start | bytes 1048576 | tf_op jit(solution)/shard_map/all_to_all | solution.py:33
  320.7 30.4 %all-to-all-start.9 = ((bf16[32,4,512]{2,1,0:T(4,128)(2,1)}), bf16[32,4,512]{2,1,0:T(4,128)(2,1)S(1)}, u32[]{:S(2)}, u32[]{:S(2)}) async-start(bf16[32,4,512]{2,1,0:T(4,128)(2,1)} %broadcast_in_dim.8), calls=%async_computation.9 | async-start | bytes 262144 | tf_op jit(solution)/shard_map/all_to_all | solution.py:39
  335.3 4.8 %copy-start.15 = (f32[3072]{0:T(1024)S(1)}, f32[3072]{0:T(1024)}, u32[]{:S(2)}) copy-start(f32[3072]{0:T(1024)} %get-tuple-element.25) | copy-start | bytes 36868
  335.3 4.7 %copy-start.16 = (f32[3072]{0:T(1024)S(1)}, f32[3072]{0:T(1024)}, u32[]{:S(2)}) copy-start(f32[3072]{0:T(1024)} %get-tuple-element.28) | copy-start | bytes 36868
  352.2 45.7 %all-to-all-start.5 = ((bf16[32,1,3,3072]{3,2,1,0:T(4,128)(2,1)}), bf16[32,1,3,3072]{3,2,1,0:T(4,128)(2,1)S(1)}, u32[]{:S(2)}, u32[]{:S(2)}) async-start(bf16[32,1,3,3072]{3,2,1,0:T(4,128)(2,1)} %broadcast_in_dim.6), calls=%async_computation.5 | async-start | bytes 1572864 | tf_op jit(solution)/shard_map/all_to_all | solution.py:39
  399.0 58.2 %all-to-all-start.7 = ((bf16[32,192,64]{1,2,0:T(8,128)(2,1)}), bf16[32,192,64]{1,2,0:T(8,128)(2,1)S(1)}, u32[]{:S(2)}, u32[]{:S(2)}) async-start(bf16[32,192,64]{1,2,0:T(8,128)(2,1)} %broadcast_in_dim.7), calls=%async_computation.7 | async-start | bytes 2097152 | tf_op jit(solution)/shard_map/all_to_all | solution.py:39
  (7 other events, 12.0 us)
Sparse Core Ops, SparseCore 0:
  10.1 48.4 all-gather.6
  60.7 65.6 all-gather.4
where the time goes:
time: 473 us; the launch traced here: 465 us
  waiting for transfers between devices  202 us (43%)
  blocking collectives  82.9 us (18%)
  starting transfers between devices  76.6 us (16%)
  matrix products  39.8 us (8%)
  local copies, waits for them, and re-layouts  34.9 us (7%)
  between operations  14.6 us (3%)
  other arithmetic  14 us (3%)
    all_to_all x3, waiting for transfers between devices, sent_to_all(): lax.all_to_all(jnp.broadcast_to(array[None], (peers, *array.shape)), axis...  96.7 us
    all_gather x1, waiting for transfers between devices, per_device(): lax.all_gather(query_key_value_weight, 'dp', axis=0, tiled=True)  65.4 us
    all_to_all x1, blocking collectives, side_by_side(): lax.all_to_all(both, axis, split_axis=split_dim, concat_axis=concat_dim,...  45.3 us
    all_to_all x3, starting transfers between devices, sent_to_all(): lax.all_to_all(jnp.broadcast_to(array[None], (peers, *array.shape)), axis...  30.1 us
    all_gather x1, blocking collectives, per_device(): lax.all_gather(adapter_up_maps, 'dp', axis=0, tiled=True)  19.4 us
    all_gather x1, blocking collectives, per_device(): lax.all_gather(adapter_down_maps, 'dp', axis=0, tiled=True)  18.2 us
    all_to_all x1, starting transfers between devices, per_device(): lax.all_to_all(query_normalized_gradient[None], 'ctx', split_axis=1, conc...  13 us
    dot_general x5, matrix products, times_transposed(): lax.dot_general(left, right, (((1,), (1,)), ((), ())), preferred_element_...  12.4 us
  transfers between devices with their start and end apart: 11, of which 9 were waited for; matrix products, arithmetic and copies ran while one was open for 13% of the time, Pallas kernels for 0%

commit v1 on v0

v1 whole, which is shorter than its diff:
```python
import functools

import jax
import jax.numpy as jnp
from jax import lax
from jax.experimental import pallas as pl
from jax.experimental.pallas import tpu as pltpu
from jax.sharding import PartitionSpec as P

HEAD = 128
EPS = 1e-06
F32 = jnp.float32
BF16 = jnp.bfloat16
NT = (((1,), (1,)), ((), ()))
TN = (((0,), (0,)), ((), ()))
NN = (((1,), (0,)), ((), ()))


def dot(a, b, dims=NN):
    return lax.dot_general(a, b, dims, preferred_element_type=F32)


def call(body, out_shape, grid=None, in_specs=None, out_specs=None, scratch=(), flops=0, moved=0, vmem=24):
    extra = {} if grid is None else {"grid": grid, "in_specs": in_specs, "out_specs": out_specs}
    return pl.pallas_call(
        body,
        out_shape=out_shape,
        scratch_shapes=list(scratch),
        compiler_params=pltpu.CompilerParams(vmem_limit_bytes=vmem * 2**20),
        cost_estimate=pl.CostEstimate(flops=flops, bytes_accessed=moved, transcendentals=0),
        **extra,
    )


def shape(dims, dtype):
    return jax.ShapeDtypeStruct(dims, dtype)


def whole(*dims):
    return pl.BlockSpec(dims, lambda i: (0,) * len(dims))


def split_up(up, rank):
    row = lax.broadcasted_iota(jnp.int32, up.shape, 0)
    zero = jnp.zeros_like(up)
    return jnp.where(row < rank, up, zero), jnp.where(row < rank, zero, up)


def unpack_blocks(ref, t, heads):
    groups = ref.shape[0] // heads
    columns = [
        jnp.concatenate([ref[g * heads + h, t] for g in range(groups)], 0) for h in range(heads)
    ]
    return jnp.concatenate(columns, 1)


def normalize(x, mod, upstream, hidden, hidden_t, branch_grad, mean_out, rstd_out):
    values = x[...].astype(F32)
    mean = jnp.mean(values, -1, keepdims=True)
    center = values - mean
    rstd = lax.rsqrt(jnp.mean(center * center, -1, keepdims=True) + EPS)
    mean_out[...] = mean
    rstd_out[...] = rstd
    state = (center * rstd * (1.0 + mod[1:2, :]) + mod[0:1, :]).astype(BF16)
    hidden[...] = state
    hidden_t[...] = state.T
    branch_grad[...] = (upstream[...].astype(F32) * mod[2:3, :]).astype(BF16)


def attended_grads(steps, branch_grad, w, grad_out, acc):
    k = pl.program_id(0)

    @pl.when(k == 0)
    def _():
        acc[...] = jnp.zeros_like(acc)

    acc[...] += dot(branch_grad[...], w[...].reshape(-1, w.shape[2]))

    @pl.when(k == steps - 1)
    def _():
        grad = acc[...].astype(BF16)
        positions = grad_out.shape[2]
        heads = grad.shape[1] // HEAD
        for g in range(grad.shape[0] // positions):
            for h in range(heads):
                grad_out[g * heads + h, 0] = grad[
                    g * positions : (g + 1) * positions, h * HEAD : (h + 1) * HEAD
                ]


def head_scales(x):
    parts = []
    for h in range(x.shape[1] // HEAD):
        v = x[:, h * HEAD : (h + 1) * HEAD]
        parts.append(lax.rsqrt(jnp.mean(v * v, -1, keepdims=True) + EPS))
    return parts


def projections(steps, rank, hidden, w, up, sent, raw, low_out, acc):
    k = pl.program_id(0)

    @pl.when(k == 0)
    def _():
        acc[...] = jnp.zeros_like(acc)

    acc[...] += dot(hidden[...], w[...])

    @pl.when(k == steps - 1)
    def _():
        n = up.shape[1]
        heads = n // HEAD
        up_q, up_v = split_up(up[...], rank)
        low_rows = acc[:, 3 * n :].astype(BF16)
        low_out[...] = low_rows
        q = acc[:, :n] + dot(low_rows, up_q)
        kk = acc[:, n : 2 * n]
        v = acc[:, 2 * n : 3 * n] + dot(low_rows, up_v)
        raw[:, :n] = q
        raw[:, n:] = kk
        positions = sent.shape[2]
        for t, x in enumerate((q, kk, v)):
            scales = head_scales(x) if t < 2 else None
            for h in range(heads):
                rows = x[:, h * HEAD : (h + 1) * HEAD]
                if t < 2:
                    rows = rows * scales[h]
                rows = rows.astype(BF16)
                for g in range(x.shape[0] // positions):
                    sent[g * heads + h, t] = rows[g * positions : (g + 1) * positions]


def attention(rows_in, grad_in, back):
    frames, _, positions, _ = rows_in.shape
    group = 8
    total = frames * group
    row = lax.broadcasted_iota(jnp.int32, (total, total), 0) % group
    col = lax.broadcasted_iota(jnp.int32, (total, total), 1) % group
    same = row == col
    scale = HEAD**-0.5
    halves = []
    for p in range(positions // group):

        def rows_of(ref, t):
            x = ref[:, t].astype(F32)[:, p * group : (p + 1) * group]
            return x.reshape(total, HEAD).astype(BF16)

        q, k, v = (rows_of(rows_in, t) for t in range(3))
        g = rows_of(grad_in, 0)
        s = dot(q, k, NT) * scale
        e = jnp.where(same, jnp.exp(s), 0.0)
        a = e / jnp.sum(e, -1, keepdims=True)
        low = a.astype(BF16)
        attended = dot(low, v)
        dp = dot(g, v, NT)
        dv = dot(low, g, TN)
        inner = jnp.sum(a * dp, -1, keepdims=True)
        ds = (a * (dp - inner) * scale).astype(BF16)
        dq = dot(ds, k)
        dk = dot(ds, q, TN)
        halves.append([x.reshape(frames, group, HEAD) for x in (dq, dk, dv, attended)])
    for t in range(4):
        x = jnp.concatenate([h[t] for h in halves], 1).astype(BF16)
        back[:, t] = x


def norm_back(raw, incoming):
    parts = []
    for h in range(raw.shape[1] // HEAD):
        x = raw[:, h * HEAD : (h + 1) * HEAD]
        u = incoming[:, h * HEAD : (h + 1) * HEAD].astype(F32)
        r = lax.rsqrt(jnp.mean(x * x, -1, keepdims=True) + EPS)
        parts.append(r * u - x * (r * r * r * jnp.mean(x * u, -1, keepdims=True)))
    return jnp.concatenate(parts, 1).astype(BF16)


def adapter_terms(rank, scale, back, raw, low, up, hidden_t, joined, low_grad, sections):
    n = up.shape[1]
    heads = n // HEAD
    dq = norm_back(raw[:, :n], unpack_blocks(back, 0, heads))
    dk = norm_back(raw[:, n:], unpack_blocks(back, 1, heads))
    dv = unpack_blocks(back, 2, heads)
    joined[:, :n] = dq
    joined[:, n : 2 * n] = dk
    joined[:, 2 * n :] = dv
    up_q, up_v = split_up(up[...], rank)
    lg = (dot(dq, up_q, NT) + dot(dv, up_v, NT)).astype(BF16)
    low_grad[...] = lg
    down = dot(hidden_t[...], jnp.concatenate([lg, lg], 1)) * scale
    low_rows = low[...]
    row = lax.broadcasted_iota(jnp.int32, (2 * rank, n), 0)
    up_grad = jnp.where(row < rank, dot(low_rows, dq, TN), dot(low_rows, dv, TN)) * scale
    parts = sections.shape[0]
    per, half = down.shape[0] // parts, down.shape[0] // parts // 2
    own = 2 * rank // parts
    left = lax.broadcasted_iota(jnp.int32, (half, HEAD), 1) < 2 * rank
    for d in range(parts):
        sections[d, :half] = jnp.where(
            left, down[d * per : d * per + half], down[d * per + half : (d + 1) * per]
        ).astype(BF16)
        sections[d, half:] = jnp.concatenate(
            [up_grad[d * own : (d + 1) * own, h * HEAD : (h + 1) * HEAD] for h in range(heads)], 0
        ).astype(BF16)


def finish(
    steps, grad_scale, joined, low_grad, back, w, out_t, x, mean, rstd, mod, upstream,
    tokens_grad, mixed, mod_rows, held, sums, s1, s2, attended,
):
    j = pl.program_id(0)
    width = w.shape[0]
    total = steps * width
    n3 = joined.shape[1]
    at = pl.ds(pl.multiple_of(j * width, width), width)

    @pl.when(j == 0)
    def _():
        s1[...] = jnp.zeros_like(s1)
        s2[...] = jnp.zeros_like(s2)
        attended[...] = unpack_blocks(back, 3, out_t.shape[2] // HEAD)

    hg = dot(joined[...], w[:, :n3], NT) + dot(low_grad[...], w[:, n3:], NT)
    out = dot(attended[...], out_t[...].reshape(-1, out_t.shape[2]), NT)
    values = x[:, at].astype(F32)
    up_rows = upstream[:, at].astype(F32)
    mixed[:, at] = (values + mod[2:3, at] * out).astype(BF16)
    normed = (values - mean[...]) * rstd[...]
    ng = hg * (1.0 + mod[1:2, at])
    sums[0:1, at] = jnp.sum(hg, 0, keepdims=True) * grad_scale
    sums[1:2, at] = jnp.sum(hg * normed, 0, keepdims=True) * grad_scale
    sums[2:3, at] = jnp.sum(up_rows * out, 0, keepdims=True) * grad_scale
    held[:, at] = ng
    s1[...] += jnp.sum(ng, -1, keepdims=True)
    s2[...] += jnp.sum(ng * normed, -1, keepdims=True)

    @pl.when(j == steps - 1)
    def _():
        m1 = s1[...] * (1.0 / total)
        m2 = s2[...] * (1.0 / total)
        for i in range(steps):
            c = slice(i * width, (i + 1) * width)
            nrm = (x[:, c].astype(F32) - mean[...]) * rstd[...]
            tokens_grad[:, c] = (
                upstream[:, c].astype(F32) + rstd[...] * (held[:, c] - m1 - nrm * m2)
            ).astype(BF16)
        tiles = total // HEAD
        for r in range(3):
            for i in range(tiles):
                mod_rows[r * tiles + i : r * tiles + i + 1, :] = sums[
                    r : r + 1, i * HEAD : (i + 1) * HEAD
                ]


def spread(rows_a, rows_b, arrived, mod_rows, both):
    share = jnp.sum(arrived[...].astype(F32), 0)
    for j in range(both.shape[0]):
        parts = []
        for rows, src in ((rows_a, share), (rows_b, mod_rows)):
            if (j + 1) * rows <= src.shape[0]:
                parts.append(src[j * rows : (j + 1) * rows, :])
            else:
                parts.append(jnp.zeros((rows, HEAD), F32))
        left = both.shape[1] - rows_a - rows_b
        if left:
            parts.append(jnp.zeros((left, HEAD), F32))
        both[j] = jnp.concatenate(parts, 0).astype(BF16)


def summed(arrived, out):
    total = jnp.sum(arrived[...].astype(F32), 0).astype(BF16)
    out[...] = jnp.broadcast_to(total[None], out.shape)


def collected(rows_a, rows_b, shares, down_t, up_grad, mod_grad):
    values = shares[...].astype(F32)
    half = down_t.shape[1] // 2
    cols = down_t.shape[0]
    own = up_grad.shape[0]
    blocks = half // rows_a
    a = jnp.concatenate([values[j, :rows_a] for j in range(blocks)], 0)
    down = jnp.concatenate([a[:, :cols], a[:, cols:]], 0)
    down_t[...] = down.T
    for h in range(up_grad.shape[1] // HEAD):
        first = half + h * own
        j, r = first // rows_a, first % rows_a
        up_grad[:, h * HEAD : (h + 1) * HEAD] = values[j, r : r + own]
    tiles = mod_grad.shape[2] // HEAD
    for i in range(3 * tiles):
        j, r = i // rows_b, rows_a + i % rows_b
        mod_grad[i // tiles, :, (i % tiles) * HEAD : (i % tiles + 1) * HEAD] = values[j, r : r + 1]


def per_device(tokens, modulation, qkv, out_w, down_w, up_w, output_gradient):
    dp, ctx = lax.axis_size("dp"), lax.axis_size("ctx")
    m, width = tokens.shape[2], tokens.shape[3]
    n = up_w.shape[1]
    heads = n // HEAD
    rank = down_w.shape[1] // 2
    positions = m // (ctx // heads)
    mod = modulation[0]
    grad_scale = (dp * ctx * m) ** (-0.5)
    own = width // dp

    w = lax.all_gather(jnp.concatenate([qkv, down_w], 1), "dp", axis=0, tiled=True)
    small = jnp.concatenate([out_w.T, up_w, jnp.zeros((8 - up_w.shape[0] % 8, n), BF16)], 0)
    out_up = lax.all_to_all(
        jnp.broadcast_to(small[None], (dp, *small.shape)), "dp", 0, 0, tiled=True
    )
    up = out_up[:, own : own + up_w.shape[0]].reshape(2 * rank, n)

    x = tokens.reshape(m, width)
    upstream = output_gradient.reshape(m, width)
    hidden, hidden_t, branch_grad, mean, rstd = call(
        normalize,
        (
            shape((m, width), BF16),
            shape((width, m), BF16),
            shape((m, width), BF16),
            shape((m, 1), F32),
            shape((m, 1), F32),
        ),
        flops=20 * m * width,
        moved=10 * m * width,
    )(x, mod, upstream)

    per = 4
    steps = dp // per
    grad_sent = call(
        functools.partial(attended_grads, steps),
        shape((ctx, 1, positions, HEAD), BF16),
        grid=(steps,),
        in_specs=[
            pl.BlockSpec((m, per * own), lambda k: (0, k)),
            pl.BlockSpec((per, own, n), lambda k: (k, 0, 0)),
        ],
        out_specs=whole(ctx, 1, positions, HEAD),
        scratch=[pltpu.VMEM((m, n), F32)],
        flops=2 * m * width * n,
        moved=2 * width * n,
    )(branch_grad, out_up)
    grad_in = lax.all_to_all(grad_sent, "ctx", 0, 0, tiled=True)

    steps, kb = 6, width // 6
    cols = w.shape[1]
    sent, raw, low = call(
        functools.partial(projections, steps, rank),
        (
            shape((ctx, 3, positions, HEAD), BF16),
            shape((m, 2 * n), F32),
            shape((m, 2 * rank), BF16),
        ),
        grid=(steps,),
        in_specs=[
            pl.BlockSpec((m, kb), lambda k: (0, k)),
            pl.BlockSpec((kb, cols), lambda k: (k, 0)),
            whole(2 * rank, n),
        ],
        out_specs=(whole(ctx, 3, positions, HEAD), whole(m, 2 * n), whole(m, 2 * rank)),
        scratch=[pltpu.VMEM((m, cols), F32)],
        flops=2 * m * width * cols,
        moved=2 * width * cols,
    )(hidden, w, up)
    rows_in = lax.all_to_all(sent, "ctx", 0, 0, tiled=True)

    back_sent = call(
        attention,
        shape((ctx, 4, positions, HEAD), BF16),
        flops=7 * 2 * 2 * 256 * 256 * 128,
        moved=8 * m * n * 2,
    )(rows_in, grad_in)
    back = lax.all_to_all(back_sent, "ctx", 0, 0, tiled=True)

    own_rows = own // 2 + (2 * rank // dp) * heads
    joined, low_grad, sections = call(
        functools.partial(adapter_terms, rank, grad_scale),
        (
            shape((m, 3 * n), BF16),
            shape((m, 2 * rank), BF16),
            shape((dp, own_rows, HEAD), BF16),
        ),
        flops=2 * m * width * HEAD + 8 * m * n * 64,
        moved=m * width * 2 + m * n * 20,
    )(back, raw, low, up, hidden_t)
    arrived = lax.all_to_all(sections, "dp", 0, 0, tiled=True)

    per = 2
    steps, cb = dp // per, per * own
    tokens_grad, mixed, mod_rows = call(
        functools.partial(finish, steps, grad_scale),
        (
            shape((m, width), BF16),
            shape((m, width), BF16),
            shape((3 * width // HEAD, HEAD), F32),
        ),
        grid=(steps,),
        in_specs=[
            whole(m, 3 * n),
            whole(m, 2 * rank),
            whole(ctx, 4, positions, HEAD),
            pl.BlockSpec((cb, cols), lambda k: (k, 0)),
            pl.BlockSpec((per, own, n), lambda k: (k, 0, 0)),
            whole(m, width),
            whole(m, 1),
            whole(m, 1),
            whole(3, width),
            whole(m, width),
        ],
        out_specs=(whole(m, width), whole(m, width), whole(3 * width // HEAD, HEAD)),
        scratch=[
            pltpu.VMEM((m, width), F32),
            pltpu.VMEM((3, width), F32),
            pltpu.VMEM((m, 1), F32),
            pltpu.VMEM((m, 1), F32),
            pltpu.VMEM((m, n), BF16),
        ],
        flops=2 * m * width * (cols + n),
        moved=2 * width * (cols + n) + 8 * m * width,
    )(joined, low_grad, back, w, out_up, x, mean, rstd, mod, upstream)

    rows_a = -(-own_rows // ctx)
    rows_b = -(-mod_rows.shape[0] // ctx)
    rows = 8 * -(-(rows_a + rows_b) // 8)
    both = call(
        functools.partial(spread, rows_a, rows_b), shape((ctx, rows, HEAD), BF16), moved=2**19
    )(arrived, mod_rows)
    part = call(summed, shape((ctx, rows, HEAD), BF16), moved=2**17)(
        lax.all_to_all(both, "ctx", 0, 0, tiled=True)
    )
    down_t, up_grad, mod_grad = call(
        functools.partial(collected, rows_a, rows_b),
        (
            shape((2 * rank, own), F32),
            shape((2 * rank // dp, n), F32),
            shape((3, 1, width), F32),
        ),
        moved=2**18,
    )(lax.all_to_all(part, "ctx", 0, 0, tiled=True))
    return (
        mixed.reshape(tokens.shape),
        tokens_grad.reshape(tokens.shape),
        mod_grad.reshape(1, 3, width),
        down_t.T,
        up_grad,
    )


def solution(mesh):
    return jax.shard_map(
        per_device,
        mesh=mesh,
        in_specs=(
            P("dp", "ctx", None, None),
            P("dp", None, None),
            P("dp", None),
            P(None, "dp"),
            P("dp", None),
            P("dp", None),
            P("dp", "ctx", None, None),
        ),
        out_specs=(
            P("dp", "ctx", None, None),
            P("dp", "ctx", None, None),
            P("dp", None, None),
            P("dp", None),
            P("dp", None),
        ),
        check_vma=False,
    )
```

time: 473 us -> 280 us (0.59)
  waiting for transfers between devices: 202 us -> 59.2 us
  starting transfers between devices: 76.6 us -> 29.9 us
  matrix products: 39.8 us -> 0 us
  blocking collectives: 82.9 us -> 120 us
  Pallas kernels: 0 us -> 18.1 us
  other arithmetic: 14 us -> 2.99 us
    all_to_all x1 -> x4, blocking collectives: 45.3 us -> 120 us  [the longest x1 44.2 us: per_device(): rows_in = lax.all_to_all(sent, 'ctx', 0, 0, tiled=True)]
    all_gather x2 -> x1, waiting for transfers between devices: 75.6 us -> 4.63 us  [per_device(): lax.all_gather(jnp.concatenate([qkv, down_w], 1), 'dp', axis=0, tiled=True)]
    all_to_all x9 -> x3, waiting for transfers between devices: 125 us -> 54.5 us  [the longest x1 54.1 us: per_device(): lax.all_to_all(jnp.broadcast_to(small[None], (dp, *small.shape)), 'dp', 0...]
    all_to_all x9 -> x3, starting transfers between devices: 76.5 us -> 29.9 us  [the longest x1 18.4 us: per_device(): grad_in = lax.all_to_all(grad_sent, 'ctx', 0, 0, tiled=True)]
    dot_general x19 -> x0, matrix products: 37.9 us -> none  [the longest x5 12.4 us: times_transposed(): lax.dot_general(left, right, (((1,), (1,)), ((), ())), preferred_element_...]
    all_gather x2 -> x0, blocking collectives: 37.6 us -> none  [the longest x1 19.4 us: per_device(): lax.all_gather(adapter_up_maps, 'dp', axis=0, tiled=True)]
    unnamed x58 -> x56, local copies, waits for them, and re-layouts: 2.58 us -> 27.6 us
    pallas_call x0 -> x9, Pallas kernels: none -> 18.1 us  [the longest x1 8.01 us: per_device(): call(functools.partial(finish, steps, grad_scale), (shape((m, width), BF1...]
  transfers between devices with their start and end apart: 11 -> 4, of which waited for: 9 -> 3; matrix products, arithmetic and copies ran while one was open for 13% -> 2% of each run, Pallas kernels for 0% -> 5%
where the time goes in v1:
time: 280 us; the launch traced here: 276 us
  blocking collectives  120 us (43%)
  waiting for transfers between devices  59.2 us (21%)
  local copies, waits for them, and re-layouts  31.2 us (11%)
  starting transfers between devices  29.9 us (11%)
  Pallas kernels  18.1 us (6%)
  between operations  14.2 us (5%)
  other arithmetic  2.99 us (1%)
    all_to_all x1, waiting for transfers between devices, per_device(): lax.all_to_all(jnp.broadcast_to(small[None], (dp, *small.shape)), 'dp', 0...  54.1 us
    all_to_all x1, blocking collectives, per_device(): rows_in = lax.all_to_all(sent, 'ctx', 0, 0, tiled=True)  44.2 us
    all_to_all x1, blocking collectives, per_device(): back = lax.all_to_all(back_sent, 'ctx', 0, 0, tiled=True)  36.5 us
    unnamed x56, local copies, waits for them, and re-layouts  27.6 us
    all_to_all x1, blocking collectives, per_device(): lax.all_to_all(both, 'ctx', 0, 0, tiled=True)  20.8 us
    all_to_all x1, blocking collectives, per_device(): lax.all_to_all(part, 'ctx', 0, 0, tiled=True)  18.7 us
    all_to_all x1, starting transfers between devices, per_device(): grad_in = lax.all_to_all(grad_sent, 'ctx', 0, 0, tiled=True)  18.4 us
    pallas_call x1, Pallas kernels, per_device(): call(functools.partial(finish, steps, grad_scale), (shape((m, width), BF1...  8.01 us
  transfers between devices with their start and end apart: 4, of which 3 were waited for; matrix products, arithmetic and copies ran while one was open for 2% of the time, Pallas kernels for 5%

profile of v1, /device:TPU:24, one launch (start us, length us, event | category | flops | bytes accessed | tf_op | source)
XLA Modules:
  0.0 275.8 jit_solution(8736967270999649702)
XLA Ops:
  8.1 1.9 pad_maximum_fusion
  10.1 1.0 maximum_maximum_fusion
  11.2 2.0 broadcast_in_dim.10
  13.2 5.9 %all-to-all-start = ((bf16[16,200,512]{2,1,0:T(8,128)(2,1)}), bf16[16,200,512]{2,1,0:T(8,128)(2,1)S(1)}, u32[]{:S(2)}, u32[]{:S(2)}) async-start(bf16[16,200,512]{2,1,0:T(8,128)(2,1)} %broadcast_in_dim.10), calls=%async_computation | async-start | bytes 6553600 | tf_op jit(solution)/shard_map/all_to_all | solution.py:305
  19.2 1.1 copy-done.4
  20.3 1.1 copy-done.6
  21.4 1.0 shard_map.110
  22.4 0.9 copy-done.8
  23.3 0.9 copy-done.10
  24.2 0.9 copy-done.12
  26.3 54.1 %all-to-all-done.w.out_t = bf16[16,200,512]{2,1,0:T(8,128)(2,1)S(1)} async-done(((bf16[16,200,512]{2,1,0:T(8,128)(2,1)}), bf16[16,200,512]{2,1,0:T(8,128)(2,1)S(1)}, u32[]{:S(2)}, u32[]{:S(2)}) %all-to-all-start) | async-done | bytes 3276832 | tf_op jit(solution)/shard_map/all_to_all | solution.py:305
  80.4 1.1 copy-done.9
  81.5 2.1 shard_map.112
  83.6 18.4 %all-to-all-start.2 = ((bf16[32,1,16,128]{3,2,1,0:T(8,128)(2,1)}), bf16[32,1,16,128]{3,2,1,0:T(8,128)(2,1)S(1)}, u32[]{:S(2)}, u32[]{:S(2)}) async-start(bf16[32,1,16,128]{3,2,1,0:T(8,128)(2,1)} %shard_map.112), calls=%async_computation.2 | async-start | bytes 262144 | tf_op jit(solution)/shard_map/all_to_all | solution.py:340
  103.6 4.6 %all-gather.2.cloned.1.call-done.w = bf16[3072,1600]{1,0:T(8,128)(2,1)} async-done(((bf16[192,1600]{1,0:T(8,128)(2,1)}), bf16[3072,1600]{1,0:T(8,128)(2,1)}) %all-gather.2.cloned.1.call-update) | async-done | bytes 9830416 | tf_op jit(solution)/shard_map/all_gather | solution.py:303
  108.2 3.9 %copy-done = bf16[3072,1600]{1,0:T(8,128)(2,1)S(1)} copy-done((bf16[3072,1600]{1,0:T(8,128)(2,1)S(1)}, bf16[3072,1600]{1,0:T(8,128)(2,1)}, u32[]{:S(2)}) %copy-start) | copy-done | bytes 9830424
  112.1 1.1 copy-done.13
  113.2 3.0 %shard_map.111 = (bf16[32,3,16,128]{3,2,1,0:T(8,128)(2,1)S(1)}, f32[128,1024]{1,0:T(8,128)S(1)}, bf16[128,64]{1,0:T(8,128)(2,1)S(1)}) custom-call(bf16[128,3072]{1,0:T(8,128)(2,1)S(1)} %copy-done.13, bf16[3072,1600]{1,0:T(8,128)(2,1)S(1)} %copy-done, bf16[64,512]{1,0:T(8,128)(2,1)S(1)} %reshape.31.up), custom_call_target="tpu_custom_call" | custom-call | flops 1258291200 | bytes 9830400 | tf_op jit(solution)/shard_map/pallas_call | solution.py:344
  118.8 44.2 %all_to_all.35.rows_in = bf16[32,3,16,128]{3,2,1,0:T(8,128)(2,1)S(1)} all-to-all(bf16[32,3,16,128]{3,2,1,0:T(8,128)(2,1)} %copy-done.17), channel_id=1, replica_groups=mesh['dp'=16,'ctx'=32] {'ctx'}, dimensions={0} | all-to-all | bytes 786432 | tf_op jit(solution)/shard_map/all_to_all | solution.py:362
  163.0 1.2 shard_map.113
  164.2 36.5 %all_to_all.36.back = bf16[32,4,16,128]{3,2,1,0:T(8,128)(2,1)S(1)} all-to-all(bf16[32,4,16,128]{3,2,1,0:T(8,128)(2,1)S(1)} %shard_map.113), channel_id=1, replica_groups=mesh['dp'=16,'ctx'=32] {'ctx'}, dimensions={0} | all-to-all | bytes 1048576 | tf_op jit(solution)/shard_map/all_to_all | solution.py:370
  200.7 1.0 copy-done.15
  205.7 5.6 %all-to-all-start.4 = ((bf16[16,112,128]{2,1,0:T(8,128)(2,1)}), bf16[16,112,128]{2,1,0:T(8,128)(2,1)}, u32[]{:S(2)}, u32[]{:S(2)}) async-start(bf16[16,112,128]{2,1,0:T(8,128)(2,1)} %copy-done.16), calls=%async_computation.4 | async-start | bytes 917504 | tf_op jit(solution)/shard_map/all_to_all | solution.py:383
  211.3 3.9 %copy-done.1 = bf16[3072,1600]{1,0:T(8,128)(2,1)S(1)} copy-done((bf16[3072,1600]{1,0:T(8,128)(2,1)S(1)}, bf16[3072,1600]{1,0:T(8,128)(2,1)}, u32[]{:S(2)}) %copy-start.1) | copy-done | bytes 9830424
  215.2 1.0 copy-done.3
  216.2 1.1 copy-done.5
  217.4 1.1 copy-done.7
  218.5 1.0 copy-done.19
  219.5 8.0 %shard_map.115 = (bf16[128,3072]{1,0:T(8,128)(2,1)}, bf16[128,3072]{1,0:T(8,128)(2,1)}, f32[72,128]{1,0:T(8,128)S(1)}) custom-call(bf16[128,1536]{1,0:T(8,128)(2,1)S(1)} %copy-done.19, bf16[128,64]{1,0:T(8,128)(2,1)S(1)} %get-tuple-element.29.low_grad, bf16[32,4,16,128]{3,2,1,0:T(8,128)(2,1)S(1)} %copy-done.3, bf16[3072,1600]{1,0:T(8,128)(2,1)S(1)} %copy-done.1, ...), custom_call_target="tpu_custom_call" | custom-call | flops 1660944384 | bytes 16121856 | tf_op jit(solution)/shard_map/pallas_call | solution.py:387
  227.5 1.1 shard_map.116
  228.6 20.8 %all_to_all.37.arrived = bf16[32,8,128]{2,1,0:T(8,128)(2,1)S(1)} all-to-all(bf16[32,8,128]{2,1,0:T(8,128)(2,1)S(1)} %shard_map.116), channel_id=1, replica_groups=mesh['dp'=16,'ctx'=32] {'ctx'}, dimensions={0} | all-to-all | bytes 131072 | tf_op jit(solution)/shard_map/all_to_all | solution.py:426
  249.4 18.7 %all_to_all.38.shares = bf16[32,8,128]{2,1,0:T(8,128)(2,1)S(1)} all-to-all(bf16[32,8,128]{2,1,0:T(8,128)(2,1)S(1)} %shard_map.117), channel_id=1, replica_groups=mesh['dp'=16,'ctx'=32] {'ctx'}, dimensions={0} | all-to-all | bytes 131072 | tf_op jit(solution)/shard_map/all_to_all | solution.py:436
  (53 shorter events, 11.1 us)
Async XLA Ops:
  7.2 101.0 %all-gather.2.cloned.1.call-start = ((), (), s32[]{:S(2)}) async-start(), calls=%async_computation.7 | async-start | bytes 10862592 | tf_op jit(solution)/shard_map/all_gather | solution.py:303
  13.2 5.9 %copy-start.26 = (f32[1,3,3072]{2,0,1:T(1,128)S(1)}, f32[1,3,3072]{2,0,1:T(1,128)}, u32[]{:S(2)}) copy-start(f32[1,3,3072]{2,0,1:T(1,128)} %param.8) | copy-start | bytes 110596
  13.2 67.2 %all-to-all-start = ((bf16[16,200,512]{2,1,0:T(8,128)(2,1)}), bf16[16,200,512]{2,1,0:T(8,128)(2,1)S(1)}, u32[]{:S(2)}, u32[]{:S(2)}) async-start(bf16[16,200,512]{2,1,0:T(8,128)(2,1)} %broadcast_in_dim.10), calls=%async_computation | async-start | bytes 6553600 | tf_op jit(solution)/shard_map/all_to_all | solution.py:305
  19.1 1.1 copy-start.4
  20.3 1.1 copy-start.6
  22.4 0.9 copy-start.8
  23.3 0.9 copy-start.10
  24.2 0.9 copy-start.12
  25.0 0.6 copy-start.20
  25.7 0.6 copy-start.22
  80.4 1.1 copy-start.9
  83.6 35.2 %all-to-all-start.2 = ((bf16[32,1,16,128]{3,2,1,0:T(8,128)(2,1)}), bf16[32,1,16,128]{3,2,1,0:T(8,128)(2,1)S(1)}, u32[]{:S(2)}, u32[]{:S(2)}) async-start(bf16[32,1,16,128]{3,2,1,0:T(8,128)(2,1)} %shard_map.112), calls=%async_computation.2 | async-start | bytes 262144 | tf_op jit(solution)/shard_map/all_to_all | solution.py:340
  108.2 3.9 %copy-start = (bf16[3072,1600]{1,0:T(8,128)(2,1)S(1)}, bf16[3072,1600]{1,0:T(8,128)(2,1)}, u32[]{:S(2)}) copy-start(bf16[3072,1600]{1,0:T(8,128)(2,1)} %all-gather.2.cloned.1.call-done.w) | copy-start | bytes 29491204
  112.1 1.1 copy-start.13
  116.2 0.8 copy-start.14
  117.0 0.7 copy-start.17
  117.8 0.6 copy-start.24
  118.8 81.9 %copy-start.11 = (bf16[3072,128]{1,0:T(8,128)(2,1)S(1)}, bf16[3072,128]{1,0:T(8,128)(2,1)}, u32[]{:S(2)}) copy-start(bf16[3072,128]{1,0:T(8,128)(2,1)} %copy-done.10) | copy-start | bytes 2359300
  164.2 47.1 %copy-start.21 = (f32[128,1]{1,0:T(8,128)S(1)}, f32[128,1]{1,0:T(8,128)}, u32[]{:S(2)}) copy-start(f32[128,1]{1,0:T(8,128)} %copy-done.20) | copy-start | bytes 1540
  164.2 47.1 %copy-start.23 = (f32[128,1]{1,0:T(8,128)S(1)}, f32[128,1]{1,0:T(8,128)}, u32[]{:S(2)}) copy-start(f32[128,1]{1,0:T(8,128)} %copy-done.22) | copy-start | bytes 1540
  200.7 1.0 copy-start.15
  201.8 0.8 copy-start.25
  203.4 0.8 copy-start.2
  204.2 0.8 copy-start.16
  205.0 0.7 copy-start.18
  205.7 21.8 %all-to-all-start.4 = ((bf16[16,112,128]{2,1,0:T(8,128)(2,1)}), bf16[16,112,128]{2,1,0:T(8,128)(2,1)}, u32[]{:S(2)}, u32[]{:S(2)}) async-start(bf16[16,112,128]{2,1,0:T(8,128)(2,1)} %copy-done.16), calls=%async_computation.4 | async-start | bytes 917504 | tf_op jit(solution)/shard_map/all_to_all | solution.py:383
  211.3 3.9 %copy-start.1 = (bf16[3072,1600]{1,0:T(8,128)(2,1)S(1)}, bf16[3072,1600]{1,0:T(8,128)(2,1)}, u32[]{:S(2)}) copy-start(bf16[3072,1600]{1,0:T(8,128)(2,1)} %all-gather.2.cloned.1.call-done.w) | copy-start | bytes 29491204
  215.2 1.0 copy-start.3
  216.2 1.1 copy-start.5
  217.4 1.1 copy-start.7
  218.5 1.0 copy-start.19
Sparse Core Ops, SparseCore 0:
  10.2 97.9 all-gather.1

commit v2 on v1

--- a/solution.py
+++ b/solution.py
@@ -20,7 +20,7 @@
     return lax.dot_general(a, b, dims, preferred_element_type=F32)
 
 
-def call(body, out_shape, grid=None, in_specs=None, out_specs=None, scratch=(), flops=0, moved=0, vmem=24):
+def call(body, out_shape, grid=None, in_specs=None, out_specs=None, scratch=(), flops=0, moved=0, vmem=60):
     extra = {} if grid is None else {"grid": grid, "in_specs": in_specs, "out_specs": out_specs}
     return pl.pallas_call(
         body,
@@ -61,31 +61,17 @@
     rstd = lax.rsqrt(jnp.mean(center * center, -1, keepdims=True) + EPS)
     mean_out[...] = mean
     rstd_out[...] = rstd
-    state = (center * rstd * (1.0 + mod[1:2, :]) + mod[0:1, :]).astype(BF16)
+    state = (center * rstd * (1.0 + mod[1]) + mod[0]).astype(BF16)
     hidden[...] = state
     hidden_t[...] = state.T
-    branch_grad[...] = (upstream[...].astype(F32) * mod[2:3, :]).astype(BF16)
-
-
-def attended_grads(steps, branch_grad, w, grad_out, acc):
-    k = pl.program_id(0)
-
-    @pl.when(k == 0)
-    def _():
-        acc[...] = jnp.zeros_like(acc)
-
-    acc[...] += dot(branch_grad[...], w[...].reshape(-1, w.shape[2]))
-
-    @pl.when(k == steps - 1)
-    def _():
-        grad = acc[...].astype(BF16)
-        positions = grad_out.shape[2]
-        heads = grad.shape[1] // HEAD
-        for g in range(grad.shape[0] // positions):
-            for h in range(heads):
-                grad_out[g * heads + h, 0] = grad[
-                    g * positions : (g + 1) * positions, h * HEAD : (h + 1) * HEAD
-                ]
+    branch_grad[...] = (upstream[...].astype(F32) * mod[2]).astype(BF16)
+
+
+def pack(qkv, out_t, down_t, packed):
+    n, k = out_t.shape[1], qkv.shape[1]
+    packed[:, :k] = qkv[...]
+    packed[:, k : k + n] = out_t[...]
+    packed[:, k + n :] = down_t[...].astype(F32).T.astype(BF16)
 
 
 def head_scales(x):
@@ -96,21 +82,23 @@
     return parts
 
 
-def projections(steps, rank, hidden, w, up, sent, raw, low_out, acc):
+def projections(steps, rank, hidden, branch_grad, w, up, sent, raw, low_out, acc):
     k = pl.program_id(0)
+    n = up.shape[1]
 
     @pl.when(k == 0)
     def _():
         acc[...] = jnp.zeros_like(acc)
 
-    acc[...] += dot(hidden[...], w[...])
+    acc[:, : 3 * n] += dot(hidden[...], w[:, : 3 * n])
+    acc[:, 3 * n : 4 * n] += dot(branch_grad[...], w[:, 3 * n : 4 * n])
+    acc[:, 4 * n :] += dot(hidden[...], w[:, 4 * n :])
 
     @pl.when(k == steps - 1)
     def _():
-        n = up.shape[1]
         heads = n // HEAD
         up_q, up_v = split_up(up[...], rank)
-        low_rows = acc[:, 3 * n :].astype(BF16)
+        low_rows = acc[:, 4 * n :].astype(BF16)
         low_out[...] = low_rows
         q = acc[:, :n] + dot(low_rows, up_q)
         kk = acc[:, n : 2 * n]
@@ -118,7 +106,7 @@
         raw[:, :n] = q
         raw[:, n:] = kk
         positions = sent.shape[2]
-        for t, x in enumerate((q, kk, v)):
+        for t, x in enumerate((q, kk, v, acc[:, 3 * n : 4 * n])):
             scales = head_scales(x) if t < 2 else None
             for h in range(heads):
                 rows = x[:, h * HEAD : (h + 1) * HEAD]
@@ -129,7 +117,7 @@
                     sent[g * heads + h, t] = rows[g * positions : (g + 1) * positions]
 
 
-def attention(rows_in, grad_in, back):
+def attention(rows_in, back):
     frames, _, positions, _ = rows_in.shape
     group = 8
     total = frames * group
@@ -144,8 +132,7 @@
             x = ref[:, t].astype(F32)[:, p * group : (p + 1) * group]
             return x.reshape(total, HEAD).astype(BF16)
 
-        q, k, v = (rows_of(rows_in, t) for t in range(3))
-        g = rows_of(grad_in, 0)
+        q, k, v, g = (rows_of(rows_in, t) for t in range(4))
         s = dot(q, k, NT) * scale
         e = jnp.where(same, jnp.exp(s), 0.0)
         a = e / jnp.sum(e, -1, keepdims=True)
@@ -203,7 +190,7 @@
 
 
 def finish(
-    steps, grad_scale, joined, low_grad, back, w, out_t, x, mean, rstd, mod, upstream,
+    steps, grad_scale, joined, low_grad, back, w, x, mean, rstd, mod, upstream,
     tokens_grad, mixed, mod_rows, held, sums, s1, s2, attended,
 ):
     j = pl.program_id(0)
@@ -216,15 +203,16 @@
     def _():
         s1[...] = jnp.zeros_like(s1)
         s2[...] = jnp.zeros_like(s2)
-        attended[...] = unpack_blocks(back, 3, out_t.shape[2] // HEAD)
-
-    hg = dot(joined[...], w[:, :n3], NT) + dot(low_grad[...], w[:, n3:], NT)
-    out = dot(attended[...], out_t[...].reshape(-1, out_t.shape[2]), NT)
+        attended[...] = unpack_blocks(back, 3, n3 // 3 // HEAD)
+
+    n4 = n3 + n3 // 3
+    hg = dot(joined[...], w[:, :n3], NT) + dot(low_grad[...], w[:, n4:], NT)
+    out = dot(attended[...], w[:, n3:n4], NT)
     values = x[:, at].astype(F32)
     up_rows = upstream[:, at].astype(F32)
-    mixed[:, at] = (values + mod[2:3, at] * out).astype(BF16)
+    mixed[:, at] = (values + mod[2, :, at] * out).astype(BF16)
     normed = (values - mean[...]) * rstd[...]
-    ng = hg * (1.0 + mod[1:2, at])
+    ng = hg * (1.0 + mod[1, :, at])
     sums[0:1, at] = jnp.sum(hg, 0, keepdims=True) * grad_scale
     sums[1:2, at] = jnp.sum(hg * normed, 0, keepdims=True) * grad_scale
     sums[2:3, at] = jnp.sum(up_rows * out, 0, keepdims=True) * grad_scale
@@ -296,16 +284,16 @@
     heads = n // HEAD
     rank = down_w.shape[1] // 2
     positions = m // (ctx // heads)
-    mod = modulation[0]
+    mod = modulation.transpose(1, 0, 2)
     grad_scale = (dp * ctx * m) ** (-0.5)
     own = width // dp
 
-    w = lax.all_gather(jnp.concatenate([qkv, down_w], 1), "dp", axis=0, tiled=True)
-    small = jnp.concatenate([out_w.T, up_w, jnp.zeros((8 - up_w.shape[0] % 8, n), BF16)], 0)
-    out_up = lax.all_to_all(
-        jnp.broadcast_to(small[None], (dp, *small.shape)), "dp", 0, 0, tiled=True
-    )
-    up = out_up[:, own : own + up_w.shape[0]].reshape(2 * rank, n)
+    cols = 4 * n + 2 * rank
+    packed = call(pack, shape((own, cols), BF16), moved=4 * own * cols)(qkv, out_w.T, down_w.T)
+    w = lax.all_gather(packed, "dp", axis=0, tiled=True)
+    up = lax.all_to_all(
+        jnp.broadcast_to(up_w[None], (dp, *up_w.shape)), "dp", 0, 0, tiled=True
+    ).reshape(2 * rank, n)
 
     x = tokens.reshape(m, width)
     upstream = output_gradient.reshape(m, width)
@@ -322,43 +310,26 @@
         moved=10 * m * width,
     )(x, mod, upstream)
 
-    per = 4
-    steps = dp // per
-    grad_sent = call(
-        functools.partial(attended_grads, steps),
-        shape((ctx, 1, positions, HEAD), BF16),
-        grid=(steps,),
-        in_specs=[
-            pl.BlockSpec((m, per * own), lambda k: (0, k)),
-            pl.BlockSpec((per, own, n), lambda k: (k, 0, 0)),
-        ],
-        out_specs=whole(ctx, 1, positions, HEAD),
-        scratch=[pltpu.VMEM((m, n), F32)],
-        flops=2 * m * width * n,
-        moved=2 * width * n,
-    )(branch_grad, out_up)
-    grad_in = lax.all_to_all(grad_sent, "ctx", 0, 0, tiled=True)
-
     steps, kb = 6, width // 6
-    cols = w.shape[1]
     sent, raw, low = call(
         functools.partial(projections, steps, rank),
         (
-            shape((ctx, 3, positions, HEAD), BF16),
+            shape((ctx, 4, positions, HEAD), BF16),
             shape((m, 2 * n), F32),
             shape((m, 2 * rank), BF16),
         ),
         grid=(steps,),
         in_specs=[
+            pl.BlockSpec((m, kb), lambda k: (0, k)),
             pl.BlockSpec((m, kb), lambda k: (0, k)),
             pl.BlockSpec((kb, cols), lambda k: (k, 0)),
             whole(2 * rank, n),
         ],
-        out_specs=(whole(ctx, 3, positions, HEAD), whole(m, 2 * n), whole(m, 2 * rank)),
+        out_specs=(whole(ctx, 4, positions, HEAD), whole(m, 2 * n), whole(m, 2 * rank)),
         scratch=[pltpu.VMEM((m, cols), F32)],
         flops=2 * m * width * cols,
         moved=2 * width * cols,
-    )(hidden, w, up)
+    )(hidden, branch_grad, w, up)
     rows_in = lax.all_to_all(sent, "ctx", 0, 0, tiled=True)
 
     back_sent = call(
@@ -366,7 +337,8 @@
         shape((ctx, 4, positions, HEAD), BF16),
         flops=7 * 2 * 2 * 256 * 256 * 128,
         moved=8 * m * n * 2,
-    )(rows_in, grad_in)
+        vmem=16,
+    )(rows_in)
     back = lax.all_to_all(back_sent, "ctx", 0, 0, tiled=True)
 
     own_rows = own // 2 + (2 * rank // dp) * heads
@@ -397,11 +369,10 @@
             whole(m, 2 * rank),
             whole(ctx, 4, positions, HEAD),
             pl.BlockSpec((cb, cols), lambda k: (k, 0)),
-            pl.BlockSpec((per, own, n), lambda k: (k, 0, 0)),
             whole(m, width),
             whole(m, 1),
             whole(m, 1),
-            whole(3, width),
+            whole(3, 1, width),
             whole(m, width),
         ],
         out_specs=(whole(m, width), whole(m, width), whole(3 * width // HEAD, HEAD)),
@@ -412,17 +383,17 @@
             pltpu.VMEM((m, 1), F32),
             pltpu.VMEM((m, n), BF16),
         ],
-        flops=2 * m * width * (cols + n),
-        moved=2 * width * (cols + n) + 8 * m * width,
-    )(joined, low_grad, back, w, out_up, x, mean, rstd, mod, upstream)
+        flops=2 * m * width * cols,
+        moved=2 * width * cols + 8 * m * width,
+    )(joined, low_grad, back, w, x, mean, rstd, mod, upstream)
 
     rows_a = -(-own_rows // ctx)
     rows_b = -(-mod_rows.shape[0] // ctx)
     rows = 8 * -(-(rows_a + rows_b) // 8)
     both = call(
-        functools.partial(spread, rows_a, rows_b), shape((ctx, rows, HEAD), BF16), moved=2**19
+        functools.partial(spread, rows_a, rows_b), shape((ctx, rows, HEAD), BF16), moved=2**19, vmem=8
     )(arrived, mod_rows)
-    part = call(summed, shape((ctx, rows, HEAD), BF16), moved=2**17)(
+    part = call(summed, shape((ctx, rows, HEAD), BF16), moved=2**17, vmem=8)(
         lax.all_to_all(both, "ctx", 0, 0, tiled=True)
     )
     down_t, up_grad, mod_grad = call(
@@ -433,6 +404,7 @@
             shape((3, 1, width), F32),
         ),
         moved=2**18,
+        vmem=8,
     )(lax.all_to_all(part, "ctx", 0, 0, tiled=True))
     return (
         mixed.reshape(tokens.shape),

time: 280 us -> 264 us (0.943)
  local copies, waits for them, and re-layouts: 31.2 us -> 2.72 us
  starting transfers between devices: 29.9 us -> 11.3 us
  waiting for transfers between devices: 59.2 us -> 77 us
  Pallas kernels: 18.1 us -> 32.7 us
  blocking collectives: 120 us -> 123 us
  other arithmetic: 2.99 us -> 0 us
    all_gather x1, waiting for transfers between devices: 4.63 us -> 75.6 us  [per_device(): w = lax.all_gather(packed, 'dp', axis=0, tiled=True)]
    all_to_all x2 -> x1, waiting for transfers between devices: 54.5 us -> 1.35 us  [per_device(): lax.all_to_all(jnp.broadcast_to(up_w[None], (dp, *up_w.shape)), 'dp', 0,...]
    unnamed x56 -> x2, local copies, waits for them, and re-layouts: 27.6 us -> 0.76 us
    all_to_all x2 -> x1, starting transfers between devices: 24.3 us -> 5.78 us  [per_device(): lax.all_to_all(jnp.broadcast_to(up_w[None], (dp, *up_w.shape)), 'dp', 0,...]
    pallas_call x3, Pallas kernels: 5.16 us -> 11.4 us  [the longest x1 9.16 us: per_device(): call(functools.partial(projections, steps, rank), (shape((ctx, 4, positio...]
    pallas_call x1, Pallas kernels: 8.01 us -> 12.5 us  [per_device(): call(functools.partial(finish, steps, grad_scale), (shape((m, width), BF1...]
    concatenate x2 -> x0, other arithmetic: 2.99 us -> none  [the longest x1 1.95 us: per_device(): jnp.concatenate([qkv, down_w], 1)]
  transfers between devices with their start and end apart: 4 -> 3, of which waited for: 3 -> 2; matrix products, arithmetic and copies ran while one was open for 2% -> 1% of each run, Pallas kernels for 5% -> 6%
where the time goes in v2:
time: 264 us; the launch traced here: 261 us
  blocking collectives  123 us (47%)
  waiting for transfers between devices  77 us (29%)
  Pallas kernels  32.7 us (12%)
  between operations  14.1 us (5%)
  starting transfers between devices  11.3 us (4%)
  local copies, waits for them, and re-layouts  2.72 us (1%)
    all_gather x1, waiting for transfers between devices, per_device(): w = lax.all_gather(packed, 'dp', axis=0, tiled=True)  75.6 us
    all_to_all x1, blocking collectives, per_device(): rows_in = lax.all_to_all(sent, 'ctx', 0, 0, tiled=True)  45.5 us
    all_to_all x1, blocking collectives, per_device(): back = lax.all_to_all(back_sent, 'ctx', 0, 0, tiled=True)  38.3 us
    all_to_all x1, blocking collectives, per_device(): lax.all_to_all(both, 'ctx', 0, 0, tiled=True)  20.6 us
    all_to_all x1, blocking collectives, per_device(): lax.all_to_all(part, 'ctx', 0, 0, tiled=True)  18.6 us
    pallas_call x1, Pallas kernels, per_device(): call(functools.partial(finish, steps, grad_scale), (shape((m, width), BF1...  12.5 us
    pallas_call x1, Pallas kernels, per_device(): call(functools.partial(projections, steps, rank), (shape((ctx, 4, positio...  9.16 us
    all_to_all x1, starting transfers between devices, per_device(): lax.all_to_all(jnp.broadcast_to(up_w[None], (dp, *up_w.shape)), 'dp', 0,...  5.78 us
  transfers between devices with their start and end apart: 3, of which 2 were waited for; matrix products, arithmetic and copies ran while one was open for 1% of the time, Pallas kernels for 6%

profile of v2, /device:TPU:24, one launch (start us, length us, event | category | flops | bytes accessed | tf_op | source)
XLA Modules:
  0.0 260.7 jit_solution(14011299355165987544)
XLA Ops:
  7.2 0.0 all-gather.2.cloned.1.call-start
  7.2 2.2 shard_map.111
  9.4 0.0 all-gather.2.cloned.1.call-update
  9.4 1.3 broadcast_in_dim.2
  10.7 5.8 %all-to-all-start = ((bf16[16,4,512]{2,1,0:T(4,128)(2,1)}), bf16[16,4,512]{2,1,0:T(4,128)(2,1)S(1)}, u32[]{:S(2)}, u32[]{:S(2)}) async-start(bf16[16,4,512]{2,1,0:T(4,128)(2,1)} %broadcast_in_dim.2), calls=%async_computation | async-start | bytes 131072 | tf_op jit(solution)/shard_map/all_to_all | solution.py:294
  16.5 3.5 %shard_map.110 = (bf16[128,3072]{1,0:T(8,128)(2,1)}, bf16[3072,128]{1,0:T(8,128)(2,1)}, bf16[128,3072]{1,0:T(8,128)(2,1)}, f32[128,1]{1,0:T(8,128)}, f32[128,1]{1,0:T(8,128)}) custom-call(bf16[128,3072]{1,0:T(8,128)(2,1)} %bitcast.9, f32[3,1,3072]{2,1,0:T(1,128)} %bitcast.14, bf16[128,3072]{1,0:T(8,128)(2,1)} %bitcast.11), custom_call_target="tpu_custom_call" | custom-call | flops 7864320 | bytes 3932160 | tf_op jit(solution)/shard_map/pallas_call | solution.py:300
  20.0 1.4 all-to-all-done
  21.4 0.6 reshape.31.up
  22.0 75.6 %all-gather.2.cloned.1.call-done.w = bf16[3072,2112]{1,0:T(8,128)(2,1)} async-done(((bf16[192,2112]{1,0:T(8,128)(2,1)}), bf16[3072,2112]{1,0:T(8,128)(2,1)}) %all-gather.2.cloned.1.call-update) | async-done | bytes 12976144 | tf_op jit(solution)/shard_map/all_gather | solution.py:293
  97.6 9.2 %shard_map.112 = (bf16[32,4,16,128]{3,2,1,0:T(8,128)(2,1)}, f32[128,1024]{1,0:T(8,128)}, bf16[128,64]{1,0:T(8,128)(2,1)}) custom-call(bf16[128,3072]{1,0:T(8,128)(2,1)} %get-tuple-element.22.hidden, bf16[128,3072]{1,0:T(8,128)(2,1)} %get-tuple-element.23.branch_grad, bf16[3072,2112]{1,0:T(8,128)(2,1)} %all-gather.2.cloned.1.call-done.w, ...), custom_call_target="tpu_custom_call" | custom-call | flops 1660944384 | bytes 12976128 | tf_op jit(solution)/shard_map/pallas_call | solution.py:314
  106.7 45.5 %all_to_all.30.rows_in = bf16[32,4,16,128]{3,2,1,0:T(8,128)(2,1)S(1)} all-to-all(bf16[32,4,16,128]{3,2,1,0:T(8,128)(2,1)} %get-tuple-element.24), channel_id=1, replica_groups=mesh['dp'=16,'ctx'=32] {'ctx'}, dimensions={0} | all-to-all | bytes 1048576 | tf_op jit(solution)/shard_map/all_to_all | solution.py:333
  152.3 1.2 shard_map.113
  153.5 38.3 %all_to_all.31.back = bf16[32,4,16,128]{3,2,1,0:T(8,128)(2,1)} all-to-all(bf16[32,4,16,128]{3,2,1,0:T(8,128)(2,1)S(1)} %shard_map.113), channel_id=1, replica_groups=mesh['dp'=16,'ctx'=32] {'ctx'}, dimensions={0} | all-to-all | bytes 1048576 | tf_op jit(solution)/shard_map/all_to_all | solution.py:342
  191.8 3.2 %shard_map.114 = (bf16[128,1536]{1,0:T(8,128)(2,1)}, bf16[128,64]{1,0:T(8,128)(2,1)}, bf16[16,112,128]{2,1,0:T(8,128)(2,1)}) custom-call(bf16[32,4,16,128]{3,2,1,0:T(8,128)(2,1)} %all_to_all.31.back, f32[128,1024]{1,0:T(8,128)} %get-tuple-element.25.raw, bf16[128,64]{1,0:T(8,128)(2,1)} %get-tuple-element.26.low, bf16[64,512]{1,0:T(8,128)(2,1)} %reshape.31.up, ...), custom_call_target="tpu_custom_call" | custom-call | flops 134217728 | bytes 2097152 | tf_op jit(solution)/shard_map/pallas_call | solution.py:345
  195.0 5.4 %all-to-all-start.3 = ((bf16[16,112,128]{2,1,0:T(8,128)(2,1)}), bf16[16,112,128]{2,1,0:T(8,128)(2,1)S(1)}, u32[]{:S(2)}, u32[]{:S(2)}) async-start(bf16[16,112,128]{2,1,0:T(8,128)(2,1)} %get-tuple-element.34), calls=%async_computation.3 | async-start | bytes 917504 | tf_op jit(solution)/shard_map/all_to_all | solution.py:355
  200.4 12.5 %shard_map.115 = (bf16[128,3072]{1,0:T(8,128)(2,1)}, bf16[128,3072]{1,0:T(8,128)(2,1)}, f32[72,128]{1,0:T(8,128)}) custom-call(bf16[128,1536]{1,0:T(8,128)(2,1)} %get-tuple-element.28.joined, bf16[128,64]{1,0:T(8,128)(2,1)} %get-tuple-element.29.low_grad, bf16[32,4,16,128]{3,2,1,0:T(8,128)(2,1)} %all_to_all.31.back, ...), custom_call_target="tpu_custom_call" | custom-call | flops 1660944384 | bytes 16121856 | tf_op jit(solution)/shard_map/pallas_call | solution.py:359
  212.9 0.0 all-to-all-done.3.arrived
  213.0 0.0 copy-start
  213.0 0.8 copy-done
  213.7 0.1 shard_map.116
  213.8 20.6 %all_to_all.32.arrived = bf16[32,8,128]{2,1,0:T(8,128)(2,1)S(1)} all-to-all(bf16[32,8,128]{2,1,0:T(8,128)(2,1)S(1)} %shard_map.116), channel_id=1, replica_groups=mesh['dp'=16,'ctx'=32] {'ctx'}, dimensions={0} | all-to-all | bytes 131072 | tf_op jit(solution)/shard_map/all_to_all | solution.py:397
  234.4 18.6 %all_to_all.33.shares = bf16[32,8,128]{2,1,0:T(8,128)(2,1)S(1)} all-to-all(bf16[32,8,128]{2,1,0:T(8,128)(2,1)S(1)} %shard_map.117), channel_id=1, replica_groups=mesh['dp'=16,'ctx'=32] {'ctx'}, dimensions={0} | all-to-all | bytes 131072 | tf_op jit(solution)/shard_map/all_to_all | solution.py:408
  253.0 0.8 shard_map.118
  (1 shorter events, 0.0 us)
Async XLA Ops:
  7.2 90.4 %all-gather.2.cloned.1.call-start = ((), (), s32[]{:S(2)}) async-start(), calls=%async_computation.6 | async-start | bytes 14204928 | tf_op jit(solution)/shard_map/all_gather | solution.py:293
  10.7 10.6 %all-to-all-start = ((bf16[16,4,512]{2,1,0:T(4,128)(2,1)}), bf16[16,4,512]{2,1,0:T(4,128)(2,1)S(1)}, u32[]{:S(2)}, u32[]{:S(2)}) async-start(bf16[16,4,512]{2,1,0:T(4,128)(2,1)} %broadcast_in_dim.2), calls=%async_computation | async-start | bytes 131072 | tf_op jit(solution)/shard_map/all_to_all | solution.py:294
  195.0 18.0 %all-to-all-start.3 = ((bf16[16,112,128]{2,1,0:T(8,128)(2,1)}), bf16[16,112,128]{2,1,0:T(8,128)(2,1)S(1)}, u32[]{:S(2)}, u32[]{:S(2)}) async-start(bf16[16,112,128]{2,1,0:T(8,128)(2,1)} %get-tuple-element.34), calls=%async_computation.3 | async-start | bytes 917504 | tf_op jit(solution)/shard_map/all_to_all | solution.py:355
  213.0 0.8 copy-start
Sparse Core Ops, SparseCore 0:
  10.1 87.3 all-gather.1

commit v3 on v2

--- a/solution.py
+++ b/solution.py
@@ -5,6 +5,7 @@
 from jax import lax
 from jax.experimental import pallas as pl
 from jax.experimental.pallas import tpu as pltpu
+from jax.sharding import Mesh
 from jax.sharding import PartitionSpec as P
 
 HEAD = 128
@@ -13,6 +14,7 @@
 BF16 = jnp.bfloat16
 NT = (((1,), (1,)), ((), ()))
 TN = (((0,), (0,)), ((), ()))
+CTX = ("yh", "far", "near")
 NN = (((1,), (0,)), ((), ()))
 
 
@@ -71,7 +73,8 @@
     n, k = out_t.shape[1], qkv.shape[1]
     packed[:, :k] = qkv[...]
     packed[:, k : k + n] = out_t[...]
-    packed[:, k + n :] = down_t[...].astype(F32).T.astype(BF16)
+    down = down_t[...].astype(F32).T
+    packed[:, k + n :] = jnp.concatenate([down, jnp.zeros_like(down)], 1).astype(BF16)
 
 
 def head_scales(x):
@@ -82,39 +85,44 @@
     return parts
 
 
-def projections(steps, rank, hidden, branch_grad, w, up, sent, raw, low_out, acc):
-    k = pl.program_id(0)
-    n = up.shape[1]
-
-    @pl.when(k == 0)
-    def _():
-        acc[...] = jnp.zeros_like(acc)
-
-    acc[:, : 3 * n] += dot(hidden[...], w[:, : 3 * n])
-    acc[:, 3 * n : 4 * n] += dot(branch_grad[...], w[:, 3 * n : 4 * n])
-    acc[:, 4 * n :] += dot(hidden[...], w[:, 4 * n :])
-
-    @pl.when(k == steps - 1)
-    def _():
-        heads = n // HEAD
-        up_q, up_v = split_up(up[...], rank)
-        low_rows = acc[:, 4 * n :].astype(BF16)
-        low_out[...] = low_rows
-        q = acc[:, :n] + dot(low_rows, up_q)
-        kk = acc[:, n : 2 * n]
-        v = acc[:, 2 * n : 3 * n] + dot(low_rows, up_v)
+def projections(rank, hidden, branch_grad, w, w_down, up, sent, raw, low_out):
+    t = pl.program_id(0)
+    n = w.shape[1]
+    heads = n // HEAD
+    positions = sent.shape[2]
+
+    def store(x, normed):
+        scales = head_scales(x) if normed else None
+        for h in range(heads):
+            rows = x[:, h * HEAD : (h + 1) * HEAD]
+            if normed:
+                rows = rows * scales[h]
+            rows = rows.astype(BF16)
+            for g in range(x.shape[0] // positions):
+                sent[g * heads + h, 0] = rows[g * positions : (g + 1) * positions]
+
+    @pl.when(t == 0)
+    def _():
+        low_out[...] = dot(hidden[...], w_down[...])[:, : 2 * rank].astype(BF16)
+        up_q, _ = split_up(up[...], rank)
+        q = dot(hidden[...], w[...]) + dot(low_out[...], up_q)
         raw[:, :n] = q
-        raw[:, n:] = kk
-        positions = sent.shape[2]
-        for t, x in enumerate((q, kk, v, acc[:, 3 * n : 4 * n])):
-            scales = head_scales(x) if t < 2 else None
-            for h in range(heads):
-                rows = x[:, h * HEAD : (h + 1) * HEAD]
-                if t < 2:
-                    rows = rows * scales[h]
-                rows = rows.astype(BF16)
-                for g in range(x.shape[0] // positions):
-                    sent[g * heads + h, t] = rows[g * positions : (g + 1) * positions]
+        store(q, True)
+
+    @pl.when(t == 1)
+    def _():
+        k = dot(hidden[...], w[...])
+        raw[:, n:] = k
+        store(k, True)
+
+    @pl.when(t == 2)
+    def _():
+        _, up_v = split_up(up[...], rank)
+        store(dot(hidden[...], w[...]) + dot(low_out[...], up_v), False)
+
+    @pl.when(t == 3)
+    def _():
+        store(dot(branch_grad[...], w[...]), False)
 
 
 def attention(rows_in, back):
@@ -206,7 +214,7 @@
         attended[...] = unpack_blocks(back, 3, n3 // 3 // HEAD)
 
     n4 = n3 + n3 // 3
-    hg = dot(joined[...], w[:, :n3], NT) + dot(low_grad[...], w[:, n4:], NT)
+    hg = dot(joined[...], w[:, :n3], NT) + dot(low_grad[...], w[:, n4 : n4 + low_grad.shape[1]], NT)
     out = dot(attended[...], w[:, n3:n4], NT)
     values = x[:, at].astype(F32)
     up_rows = upstream[:, at].astype(F32)
@@ -238,19 +246,22 @@
                 ]
 
 
-def spread(rows_a, rows_b, arrived, mod_rows, both):
-    share = jnp.sum(arrived[...].astype(F32), 0)
-    for j in range(both.shape[0]):
-        parts = []
-        for rows, src in ((rows_a, share), (rows_b, mod_rows)):
-            if (j + 1) * rows <= src.shape[0]:
-                parts.append(src[j * rows : (j + 1) * rows, :])
-            else:
-                parts.append(jnp.zeros((rows, HEAD), F32))
-        left = both.shape[1] - rows_a - rows_b
-        if left:
-            parts.append(jnp.zeros((left, HEAD), F32))
-        both[j] = jnp.concatenate(parts, 0).astype(BF16)
+def spread(arrived, mod_rows, both):
+    share = jnp.sum(arrived[...].astype(F32), 0).astype(BF16)
+    rows = mod_rows[...].astype(BF16)
+    parts = both.shape[0]
+    rows_a, rows_b = share.shape[0] // parts, rows.shape[0] // parts
+    pad = jnp.zeros((both.shape[1] - rows_a - rows_b, HEAD), F32)
+    for j in range(parts):
+        piece = jnp.concatenate(
+            [
+                share[j * rows_a : (j + 1) * rows_a].astype(F32),
+                rows[j * rows_b : (j + 1) * rows_b].astype(F32),
+                pad,
+            ],
+            0,
+        )
+        both[j] = piece.astype(BF16)
 
 
 def summed(arrived, out):
@@ -260,25 +271,22 @@
 
 def collected(rows_a, rows_b, shares, down_t, up_grad, mod_grad):
     values = shares[...].astype(F32)
-    half = down_t.shape[1] // 2
+    parts = values.shape[0]
     cols = down_t.shape[0]
     own = up_grad.shape[0]
-    blocks = half // rows_a
-    a = jnp.concatenate([values[j, :rows_a] for j in range(blocks)], 0)
-    down = jnp.concatenate([a[:, :cols], a[:, cols:]], 0)
-    down_t[...] = down.T
+    half = down_t.shape[1] // 2
+    a = jnp.concatenate([values[j, :rows_a] for j in range(parts)], 0)
+    b = jnp.concatenate([values[j, rows_a : rows_a + rows_b] for j in range(parts)], 0)
+    down_t[...] = jnp.concatenate([a[:half, :cols], a[:half, cols:]], 0).T
     for h in range(up_grad.shape[1] // HEAD):
-        first = half + h * own
-        j, r = first // rows_a, first % rows_a
-        up_grad[:, h * HEAD : (h + 1) * HEAD] = values[j, r : r + own]
+        up_grad[:, h * HEAD : (h + 1) * HEAD] = a[half + h * own : half + (h + 1) * own]
     tiles = mod_grad.shape[2] // HEAD
     for i in range(3 * tiles):
-        j, r = i // rows_b, rows_a + i % rows_b
-        mod_grad[i // tiles, :, (i % tiles) * HEAD : (i % tiles + 1) * HEAD] = values[j, r : r + 1]
+        mod_grad[i // tiles, :, (i % tiles) * HEAD : (i % tiles + 1) * HEAD] = b[i : i + 1]
 
 
 def per_device(tokens, modulation, qkv, out_w, down_w, up_w, output_gradient):
-    dp, ctx = lax.axis_size("dp"), lax.axis_size("ctx")
+    dp, ctx = lax.axis_size("dp"), lax.axis_size(CTX)
     m, width = tokens.shape[2], tokens.shape[3]
     n = up_w.shape[1]
     heads = n // HEAD
@@ -288,7 +296,7 @@
     grad_scale = (dp * ctx * m) ** (-0.5)
     own = width // dp
 
-    cols = 4 * n + 2 * rank
+    cols = 4 * n + HEAD
     packed = call(pack, shape((own, cols), BF16), moved=4 * own * cols)(qkv, out_w.T, down_w.T)
     w = lax.all_gather(packed, "dp", axis=0, tiled=True)
     up = lax.all_to_all(
@@ -310,27 +318,30 @@
         moved=10 * m * width,
     )(x, mod, upstream)
 
-    steps, kb = 6, width // 6
     sent, raw, low = call(
-        functools.partial(projections, steps, rank),
+        functools.partial(projections, rank),
         (
             shape((ctx, 4, positions, HEAD), BF16),
             shape((m, 2 * n), F32),
             shape((m, 2 * rank), BF16),
         ),
-        grid=(steps,),
+        grid=(4,),
         in_specs=[
-            pl.BlockSpec((m, kb), lambda k: (0, k)),
-            pl.BlockSpec((m, kb), lambda k: (0, k)),
-            pl.BlockSpec((kb, cols), lambda k: (k, 0)),
+            whole(m, width),
+            whole(m, width),
+            pl.BlockSpec((width, n), lambda t: (0, t)),
+            pl.BlockSpec((width, HEAD), lambda t: (0, 4 * n // HEAD)),
             whole(2 * rank, n),
         ],
-        out_specs=(whole(ctx, 4, positions, HEAD), whole(m, 2 * n), whole(m, 2 * rank)),
-        scratch=[pltpu.VMEM((m, cols), F32)],
+        out_specs=(
+            pl.BlockSpec((ctx, 1, positions, HEAD), lambda t: (0, t, 0, 0)),
+            whole(m, 2 * n),
+            whole(m, 2 * rank),
+        ),
         flops=2 * m * width * cols,
         moved=2 * width * cols,
-    )(hidden, branch_grad, w, up)
-    rows_in = lax.all_to_all(sent, "ctx", 0, 0, tiled=True)
+    )(hidden, branch_grad, w, w, up)
+    rows_in = lax.all_to_all(sent, CTX, 0, 0, tiled=True)
 
     back_sent = call(
         attention,
@@ -339,7 +350,7 @@
         moved=8 * m * n * 2,
         vmem=16,
     )(rows_in)
-    back = lax.all_to_all(back_sent, "ctx", 0, 0, tiled=True)
+    back = lax.all_to_all(back_sent, CTX, 0, 0, tiled=True)
 
     own_rows = own // 2 + (2 * rank // dp) * heads
     joined, low_grad, sections = call(
@@ -387,14 +398,15 @@
         moved=2 * width * cols + 8 * m * width,
     )(joined, low_grad, back, w, x, mean, rstd, mod, upstream)
 
-    rows_a = -(-own_rows // ctx)
-    rows_b = -(-mod_rows.shape[0] // ctx)
-    rows = 8 * -(-(rows_a + rows_b) // 8)
-    both = call(
-        functools.partial(spread, rows_a, rows_b), shape((ctx, rows, HEAD), BF16), moved=2**19, vmem=8
-    )(arrived, mod_rows)
-    part = call(summed, shape((ctx, rows, HEAD), BF16), moved=2**17, vmem=8)(
-        lax.all_to_all(both, "ctx", 0, 0, tiled=True)
+    near, far = lax.axis_size("near"), lax.axis_size("yh") * lax.axis_size("far")
+    rows_a, rows_b = own_rows // near, mod_rows.shape[0] // near
+    rows = 16 * -(-(rows_a + rows_b) // 16)
+    both = call(spread, shape((near, rows, HEAD), BF16), moved=2**19, vmem=8)(arrived, mod_rows)
+    part = call(summed, shape((far, rows, HEAD), BF16), moved=2**17, vmem=8)(
+        lax.all_to_all(both, "near", 0, 0, tiled=True)
+    )
+    part = call(summed, shape((near, rows, HEAD), BF16), moved=2**17, vmem=8)(
+        lax.all_to_all(part, ("yh", "far"), 0, 0, tiled=True)
     )
     down_t, up_grad, mod_grad = call(
         functools.partial(collected, rows_a, rows_b),
@@ -405,7 +417,7 @@
         ),
         moved=2**18,
         vmem=8,
-    )(lax.all_to_all(part, "ctx", 0, 0, tiled=True))
+    )(lax.all_to_all(part, "near", 0, 0, tiled=True))
     return (
         mixed.reshape(tokens.shape),
         tokens_grad.reshape(tokens.shape),
@@ -416,21 +428,23 @@
 
 
 def solution(mesh):
+    dp, ctx = mesh.devices.shape
+    fine = Mesh(mesh.devices.reshape(dp, 2, ctx // 8, 4), ("dp", *CTX))
     return jax.shard_map(
         per_device,
-        mesh=mesh,
+        mesh=fine,
         in_specs=(
-            P("dp", "ctx", None, None),
+            P("dp", CTX, None, None),
             P("dp", None, None),
             P("dp", None),
             P(None, "dp"),
             P("dp", None),
             P("dp", None),
-            P("dp", "ctx", None, None),
+            P("dp", CTX, None, None),
         ),
         out_specs=(
-            P("dp", "ctx", None, None),
-            P("dp", "ctx", None, None),
+            P("dp", CTX, None, None),
+            P("dp", CTX, None, None),
             P("dp", None, None),
             P("dp", None),
             P("dp", None),

time: 264 us -> 262 us (level)
    pallas_call x3 -> x4, Pallas kernels: 9.28 us -> 8.4 us  [the longest x1 8.29 us: per_device(): call(functools.partial(projections, rank), (shape((ctx, 4, positions, HEA...]
    all_to_all x4 -> x5, blocking collectives: 123 us -> 122 us  [the longest x1 45.5 us: per_device(): rows_in = lax.all_to_all(sent, CTX, 0, 0, tiled=True)]
where the time goes in v3:
time: 262 us; the launch traced here: 259 us
  blocking collectives  122 us (47%)
  waiting for transfers between devices  77 us (29%)
  Pallas kernels  31.8 us (12%)
  between operations  14.1 us (5%)
  starting transfers between devices  11.3 us (4%)
  local copies, waits for them, and re-layouts  2.72 us (1%)
    all_gather x1, waiting for transfers between devices, per_device(): w = lax.all_gather(packed, 'dp', axis=0, tiled=True)  75.6 us
    all_to_all x1, blocking collectives, per_device(): rows_in = lax.all_to_all(sent, CTX, 0, 0, tiled=True)  45.5 us
    all_to_all x1, blocking collectives, per_device(): back = lax.all_to_all(back_sent, CTX, 0, 0, tiled=True)  38.3 us
    all_to_all x1, blocking collectives, per_device(): lax.all_to_all(part, ('yh', 'far'), 0, 0, tiled=True)  20 us
    pallas_call x1, Pallas kernels, per_device(): call(functools.partial(finish, steps, grad_scale), (shape((m, width), BF1...  12.5 us
    all_to_all x1, blocking collectives, per_device(): lax.all_to_all(both, 'near', 0, 0, tiled=True)  9.49 us
    all_to_all x1, blocking collectives, per_device(): lax.all_to_all(part, 'near', 0, 0, tiled=True)  9.02 us
    pallas_call x1, Pallas kernels, per_device(): call(functools.partial(projections, rank), (shape((ctx, 4, positions, HEA...  8.29 us
  transfers between devices with their start and end apart: 3, of which 2 were waited for; matrix products, arithmetic and copies ran while one was open for 1% of the time, Pallas kernels for 6%

profile of v3, /device:TPU:24, one launch (start us, length us, event | category | flops | bytes accessed | tf_op | source)
XLA Modules:
  0.0 259.1 jit_solution(12994583655994215347)
XLA Ops:
  7.2 0.0 all-gather.2.cloned.1.call-start
  7.2 2.2 shard_map.111
  9.4 0.0 all-gather.2.cloned.1.call-update
  9.4 1.3 broadcast_in_dim.2
  10.7 5.8 %all-to-all-start = ((bf16[16,4,512]{2,1,0:T(4,128)(2,1)}), bf16[16,4,512]{2,1,0:T(4,128)(2,1)S(1)}, u32[]{:S(2)}, u32[]{:S(2)}) async-start(bf16[16,4,512]{2,1,0:T(4,128)(2,1)} %broadcast_in_dim.2), calls=%async_computation | async-start | bytes 131072 | tf_op jit(solution)/shard_map/all_to_all | solution.py:302
  16.5 3.5 %shard_map.110 = (bf16[128,3072]{1,0:T(8,128)(2,1)}, bf16[3072,128]{1,0:T(8,128)(2,1)}, bf16[128,3072]{1,0:T(8,128)(2,1)}, f32[128,1]{1,0:T(8,128)}, f32[128,1]{1,0:T(8,128)}) custom-call(bf16[128,3072]{1,0:T(8,128)(2,1)} %bitcast.9, f32[3,1,3072]{2,1,0:T(1,128)} %bitcast.14, bf16[128,3072]{1,0:T(8,128)(2,1)} %bitcast.11), custom_call_target="tpu_custom_call" | custom-call | flops 7864320 | bytes 3932160 | tf_op jit(solution)/shard_map/pallas_call | solution.py:308
  20.0 1.4 all-to-all-done
  21.4 0.6 reshape.31.up
  22.0 75.6 %all-gather.2.cloned.1.call-done.w.w_down = bf16[3072,2176]{1,0:T(8,128)(2,1)} async-done(((bf16[192,2176]{1,0:T(8,128)(2,1)}), bf16[3072,2176]{1,0:T(8,128)(2,1)}) %all-gather.2.cloned.1.call-update) | async-done | bytes 13369360 | tf_op jit(solution)/shard_map/all_gather | solution.py:301
  97.6 8.3 %shard_map.112 = (bf16[32,4,16,128]{3,2,1,0:T(8,128)(2,1)}, f32[128,1024]{1,0:T(8,128)}, bf16[128,64]{1,0:T(8,128)(2,1)}) custom-call(bf16[128,3072]{1,0:T(8,128)(2,1)} %get-tuple-element.22.hidden, bf16[128,3072]{1,0:T(8,128)(2,1)} %get-tuple-element.23.branch_grad, bf16[3072,2176]{1,0:T(8,128)(2,1)} %all-gather.2.cloned.1.call-done.w.w_down, ...), custom_call_target="tpu_custom_call" | custom-call | flops 1711276032 | bytes 13369344 | tf_op jit(solution)/shard_map/pallas_call | solution.py:321
  105.9 45.5 %all_to_all.35.rows_in = bf16[32,4,16,128]{3,2,1,0:T(8,128)(2,1)S(1)} all-to-all(bf16[32,4,16,128]{3,2,1,0:T(8,128)(2,1)} %get-tuple-element.24), channel_id=1, replica_groups=mesh['dp'=16,'yh'=2,'far'=4,'near'=4] {'yh','far','near'}, dimensions={0} | all-to-all | bytes 1048576 | tf_op jit(solution)/shard_map/all_to_all | solution.py:344
  151.4 1.2 shard_map.113
  152.6 38.3 %all_to_all.36.back = bf16[32,4,16,128]{3,2,1,0:T(8,128)(2,1)} all-to-all(bf16[32,4,16,128]{3,2,1,0:T(8,128)(2,1)S(1)} %shard_map.113), channel_id=1, replica_groups=mesh['dp'=16,'yh'=2,'far'=4,'near'=4] {'yh','far','near'}, dimensions={0} | all-to-all | bytes 1048576 | tf_op jit(solution)/shard_map/all_to_all | solution.py:353
  190.9 3.2 %shard_map.114 = (bf16[128,1536]{1,0:T(8,128)(2,1)}, bf16[128,64]{1,0:T(8,128)(2,1)}, bf16[16,112,128]{2,1,0:T(8,128)(2,1)}) custom-call(bf16[32,4,16,128]{3,2,1,0:T(8,128)(2,1)} %all_to_all.36.back, f32[128,1024]{1,0:T(8,128)} %get-tuple-element.25.raw, bf16[128,64]{1,0:T(8,128)(2,1)} %get-tuple-element.26.low, bf16[64,512]{1,0:T(8,128)(2,1)} %reshape.31.up, ...), custom_call_target="tpu_custom_call" | custom-call | flops 134217728 | bytes 2097152 | tf_op jit(solution)/shard_map/pallas_call | solution.py:356
  194.1 5.4 %all-to-all-start.3 = ((bf16[16,112,128]{2,1,0:T(8,128)(2,1)}), bf16[16,112,128]{2,1,0:T(8,128)(2,1)S(1)}, u32[]{:S(2)}, u32[]{:S(2)}) async-start(bf16[16,112,128]{2,1,0:T(8,128)(2,1)} %get-tuple-element.34), calls=%async_computation.3 | async-start | bytes 917504 | tf_op jit(solution)/shard_map/all_to_all | solution.py:366
  199.6 12.5 %shard_map.115 = (bf16[128,3072]{1,0:T(8,128)(2,1)}, bf16[128,3072]{1,0:T(8,128)(2,1)}, f32[72,128]{1,0:T(8,128)}) custom-call(bf16[128,1536]{1,0:T(8,128)(2,1)} %get-tuple-element.28.joined, bf16[128,64]{1,0:T(8,128)(2,1)} %get-tuple-element.29.low_grad, bf16[32,4,16,128]{3,2,1,0:T(8,128)(2,1)} %all_to_all.36.back, ...), custom_call_target="tpu_custom_call" | custom-call | flops 1711276032 | bytes 16515072 | tf_op jit(solution)/shard_map/pallas_call | solution.py:370
  212.1 0.0 all-to-all-done.3.arrived
  212.1 0.0 copy-start
  212.1 0.8 copy-done
  212.9 0.1 shard_map.116
  212.9 9.5 %all_to_all.37.arrived = bf16[4,48,128]{2,1,0:T(8,128)(2,1)S(1)} all-to-all(bf16[4,48,128]{2,1,0:T(8,128)(2,1)S(1)} %shard_map.116), channel_id=1, replica_groups=mesh['dp'=16,'yh'=2,'far'=4,'near'=4] {'near'}, dimensions={0} | all-to-all | bytes 98304 | tf_op jit(solution)/shard_map/all_to_all | solution.py:406
  222.4 20.0 %all_to_all.38.arrived = bf16[8,48,128]{2,1,0:T(8,128)(2,1)S(1)} all-to-all(bf16[8,48,128]{2,1,0:T(8,128)(2,1)S(1)} %shard_map.117), channel_id=1, replica_groups=mesh['dp'=16,'yh'=2,'far'=4,'near'=4] {'yh','far'}, dimensions={0} | all-to-all | bytes 196608 | tf_op jit(solution)/shard_map/all_to_all | solution.py:409
  242.4 9.0 %all_to_all.39.shares = bf16[4,48,128]{2,1,0:T(8,128)(2,1)S(1)} all-to-all(bf16[4,48,128]{2,1,0:T(8,128)(2,1)S(1)} %shard_map.118), channel_id=1, replica_groups=mesh['dp'=16,'yh'=2,'far'=4,'near'=4] {'near'}, dimensions={0} | all-to-all | bytes 98304 | tf_op jit(solution)/shard_map/all_to_all | solution.py:420
  251.5 0.8 shard_map.119
  (2 shorter events, 0.0 us)
Async XLA Ops:
  7.2 90.4 %all-gather.2.cloned.1.call-start = ((), (), s32[]{:S(2)}) async-start(), calls=%async_computation.7 | async-start | bytes 14204928 | tf_op jit(solution)/shard_map/all_gather | solution.py:301
  10.7 10.6 %all-to-all-start = ((bf16[16,4,512]{2,1,0:T(4,128)(2,1)}), bf16[16,4,512]{2,1,0:T(4,128)(2,1)S(1)}, u32[]{:S(2)}, u32[]{:S(2)}) async-start(bf16[16,4,512]{2,1,0:T(4,128)(2,1)} %broadcast_in_dim.2), calls=%async_computation | async-start | bytes 131072 | tf_op jit(solution)/shard_map/all_to_all | solution.py:302
  194.1 18.0 %all-to-all-start.3 = ((bf16[16,112,128]{2,1,0:T(8,128)(2,1)}), bf16[16,112,128]{2,1,0:T(8,128)(2,1)S(1)}, u32[]{:S(2)}, u32[]{:S(2)}) async-start(bf16[16,112,128]{2,1,0:T(8,128)(2,1)} %get-tuple-element.34), calls=%async_computation.3 | async-start | bytes 917504 | tf_op jit(solution)/shard_map/all_to_all | solution.py:366
  212.1 0.8 copy-start
Sparse Core Ops, SparseCore 0:
  10.1 87.3 all-gather.1

commit v4 on v3

--- a/solution.py
+++ b/solution.py
@@ -49,9 +49,12 @@
 
 
 def unpack_blocks(ref, t, heads):
-    groups = ref.shape[0] // heads
+    groups, frames = ref.shape[0] // heads, ref.shape[1]
     columns = [
-        jnp.concatenate([ref[g * heads + h, t] for g in range(groups)], 0) for h in range(heads)
+        jnp.concatenate(
+            [ref[g * heads + h, f, t] for f in range(frames) for g in range(groups)], 0
+        )
+        for h in range(heads)
     ]
     return jnp.concatenate(columns, 1)
 
@@ -89,7 +92,8 @@
     t = pl.program_id(0)
     n = w.shape[1]
     heads = n // HEAD
-    positions = sent.shape[2]
+    frames, positions = sent.shape[1], sent.shape[3]
+    half = hidden.shape[0] // frames
 
     def store(x, normed):
         scales = head_scales(x) if normed else None
@@ -98,8 +102,10 @@
             if normed:
                 rows = rows * scales[h]
             rows = rows.astype(BF16)
-            for g in range(x.shape[0] // positions):
-                sent[g * heads + h, 0] = rows[g * positions : (g + 1) * positions]
+            for f in range(frames):
+                for g in range(half // positions):
+                    at = f * half + g * positions
+                    sent[g * heads + h, f, 0] = rows[at : at + positions]
 
     @pl.when(t == 0)
     def _():
@@ -199,7 +205,7 @@
 
 def finish(
     steps, grad_scale, joined, low_grad, back, w, x, mean, rstd, mod, upstream,
-    tokens_grad, mixed, mod_rows, held, sums, s1, s2, attended,
+    grad_own, grad_other, mixed_own, mixed_other, mod_rows, held, sums, s1, s2, attended,
 ):
     j = pl.program_id(0)
     width = w.shape[0]
@@ -218,7 +224,10 @@
     out = dot(attended[...], w[:, n3:n4], NT)
     values = x[:, at].astype(F32)
     up_rows = upstream[:, at].astype(F32)
-    mixed[:, at] = (values + mod[2, :, at] * out).astype(BF16)
+    half = mixed_own.shape[0]
+    mixed = (values + mod[2, :, at] * out).astype(BF16)
+    mixed_own[:, at] = mixed[:half]
+    mixed_other[:, at] = mixed[half:]
     normed = (values - mean[...]) * rstd[...]
     ng = hg * (1.0 + mod[1, :, at])
     sums[0:1, at] = jnp.sum(hg, 0, keepdims=True) * grad_scale
@@ -235,15 +244,29 @@
         for i in range(steps):
             c = slice(i * width, (i + 1) * width)
             nrm = (x[:, c].astype(F32) - mean[...]) * rstd[...]
-            tokens_grad[:, c] = (
+            grad = (
                 upstream[:, c].astype(F32) + rstd[...] * (held[:, c] - m1 - nrm * m2)
             ).astype(BF16)
+            grad_own[:, c] = grad[:half]
+            grad_other[:, c] = grad[half:]
         tiles = total // HEAD
         for r in range(3):
             for i in range(tiles):
                 mod_rows[r * tiles + i : r * tiles + i + 1, :] = sums[
                     r : r + 1, i * HEAD : (i + 1) * HEAD
                 ]
+
+
+def halves(place, own_a, other_a, own_b, other_b, out_a, out_b):
+    @pl.when(pl.program_id(0) == 0)
+    def _():
+        out_a[...] = own_a[...]
+        out_b[...] = own_b[...]
+
+    @pl.when(pl.program_id(0) == 1)
+    def _():
+        out_a[...] = other_a[...]
+        out_b[...] = other_b[...]
 
 
 def spread(arrived, mod_rows, both):
@@ -291,7 +314,9 @@
     n = up_w.shape[1]
     heads = n // HEAD
     rank = down_w.shape[1] // 2
-    positions = m // (ctx // heads)
+    pair, along = lax.axis_size("yh"), lax.axis_size(("far", "near"))
+    half = m // pair
+    positions = half // (along // heads)
     mod = modulation.transpose(1, 0, 2)
     grad_scale = (dp * ctx * m) ** (-0.5)
     own = width // dp
@@ -303,8 +328,17 @@
         jnp.broadcast_to(up_w[None], (dp, *up_w.shape)), "dp", 0, 0, tiled=True
     ).reshape(2 * rank, n)
 
-    x = tokens.reshape(m, width)
-    upstream = output_gradient.reshape(m, width)
+    side = lax.axis_index("yh")
+    swap = [(0, 1), (1, 0)]
+
+    def by_place(rows):
+        own_rows = lax.dynamic_slice_in_dim(rows, side * half, half, 0)
+        other = lax.dynamic_slice_in_dim(rows, (1 - side) * half, half, 0)
+        return jnp.concatenate([own_rows, lax.ppermute(other, "yh", swap)], 0)
+
+    _, tokens, output_gradient = lax.optimization_barrier((packed, tokens, output_gradient))
+    x = by_place(tokens.reshape(m, width))
+    upstream = by_place(output_gradient.reshape(m, width))
     hidden, hidden_t, branch_grad, mean, rstd = call(
         normalize,
         (
@@ -321,7 +355,7 @@
     sent, raw, low = call(
         functools.partial(projections, rank),
         (
-            shape((ctx, 4, positions, HEAD), BF16),
+            shape((along, pair, 4, positions, HEAD), BF16),
             shape((m, 2 * n), F32),
             shape((m, 2 * rank), BF16),
         ),
@@ -334,14 +368,14 @@
             whole(2 * rank, n),
         ],
         out_specs=(
-            pl.BlockSpec((ctx, 1, positions, HEAD), lambda t: (0, t, 0, 0)),
+            pl.BlockSpec((along, pair, 1, positions, HEAD), lambda t: (0, 0, t, 0, 0)),
             whole(m, 2 * n),
             whole(m, 2 * rank),
         ),
         flops=2 * m * width * cols,
         moved=2 * width * cols,
     )(hidden, branch_grad, w, w, up)
-    rows_in = lax.all_to_all(sent, CTX, 0, 0, tiled=True)
+    rows_in = lax.all_to_all(sent, ("far", "near"), 0, 0, tiled=True)
 
     back_sent = call(
         attention,
@@ -349,8 +383,10 @@
         flops=7 * 2 * 2 * 256 * 256 * 128,
         moved=8 * m * n * 2,
         vmem=16,
-    )(rows_in)
-    back = lax.all_to_all(back_sent, CTX, 0, 0, tiled=True)
+    )(rows_in.reshape(ctx, 4, positions, HEAD))
+    back = lax.all_to_all(
+        back_sent.reshape(along, pair, 4, positions, HEAD), ("far", "near"), 0, 0, tiled=True
+    )
 
     own_rows = own // 2 + (2 * rank // dp) * heads
     joined, low_grad, sections = call(
@@ -367,18 +403,17 @@
 
     per = 2
     steps, cb = dp // per, per * own
-    tokens_grad, mixed, mod_rows = call(
+    grad_own, grad_other, mixed_own, mixed_other, mod_rows = call(
         functools.partial(finish, steps, grad_scale),
         (
-            shape((m, width), BF16),
-            shape((m, width), BF16),
+            *(shape((half, width), BF16),) * 4,
             shape((3 * width // HEAD, HEAD), F32),
         ),
         grid=(steps,),
         in_specs=[
             whole(m, 3 * n),
             whole(m, 2 * rank),
-            whole(ctx, 4, positions, HEAD),
+            whole(along, pair, 4, positions, HEAD),
             pl.BlockSpec((cb, cols), lambda k: (k, 0)),
             whole(m, width),
             whole(m, 1),
@@ -386,7 +421,7 @@
             whole(3, 1, width),
             whole(m, width),
         ],
-        out_specs=(whole(m, width), whole(m, width), whole(3 * width // HEAD, HEAD)),
+        out_specs=(*(whole(half, width),) * 4, whole(3 * width // HEAD, HEAD)),
         scratch=[
             pltpu.VMEM((m, width), F32),
             pltpu.VMEM((3, width), F32),
@@ -397,6 +432,20 @@
         flops=2 * m * width * cols,
         moved=2 * width * cols + 8 * m * width,
     )(joined, low_grad, back, w, x, mean, rstd, mod, upstream)
+
+    grad_other = lax.ppermute(grad_other, "yh", swap)
+    mixed_other = lax.ppermute(mixed_other, "yh", swap)
+    fixed = pl.BlockSpec((half, width), lambda i, s: (0, 0))
+    placed = pl.BlockSpec((half, width), lambda i, s: (i + s[0] - 2 * i * s[0], 0))
+    tokens_grad, mixed = pl.pallas_call(
+        halves,
+        out_shape=(shape((m, width), BF16),) * 2,
+        grid_spec=pltpu.PrefetchScalarGridSpec(
+            num_scalar_prefetch=1, grid=(2,), in_specs=[fixed] * 4, out_specs=(placed, placed)
+        ),
+        compiler_params=pltpu.CompilerParams(vmem_limit_bytes=16 * 2**20),
+        cost_estimate=pl.CostEstimate(flops=0, bytes_accessed=8 * m * width, transcendentals=0),
+    )(side.astype(jnp.int32).reshape(1), grad_own, grad_other, mixed_own, mixed_other)
 
     near, far = lax.axis_size("near"), lax.axis_size("yh") * lax.axis_size("far")
     rows_a, rows_b = own_rows // near, mod_rows.shape[0] // near

time: 262 us -> 267 us (1.019)
  blocking collectives: 122 us -> 86.8 us
  starting transfers between devices: 11.3 us -> 40.2 us
  waiting for transfers between devices: 77 us -> 84.1 us
    all_to_all x4 -> x2, blocking collectives: 113 us -> 77.1 us  [the longest x1 41.5 us: per_device(): rows_in = lax.all_to_all(sent, ('far', 'near'), 0, 0, tiled=True)]
    ppermute x0 -> x4, waiting for transfers between devices: none -> 27.9 us  [the longest x2 22.6 us: by_place(): return jnp.concatenate([own_rows, lax.ppermute(other, 'yh', swap)], 0)]
    all_gather x1, waiting for transfers between devices: 75.6 us -> 51 us  [per_device(): w = lax.all_gather(packed, 'dp', axis=0, tiled=True)]
    ppermute x0 -> x4, starting transfers between devices: none -> 15.8 us  [the longest x2 8.45 us: by_place(): return jnp.concatenate([own_rows, lax.ppermute(other, 'yh', swap)], 0)]
    all_to_all x0 -> x2, starting transfers between devices: none -> 12.7 us  [the longest x1 9.19 us: per_device(): lax.all_to_all(part, ('yh', 'far'), 0, 0, tiled=True)]
    all_to_all x0 -> x2, waiting for transfers between devices: none -> 5.2 us  [the longest x1 5.2 us: per_device(): lax.all_to_all(part, ('yh', 'far'), 0, 0, tiled=True)]
    pallas_call x2 -> x3, Pallas kernels: 20.8 us -> 22.1 us  [the longest x1 12.6 us: per_device(): call(functools.partial(finish, steps, grad_scale), (*(shape((half, width)...]
  transfers between devices with their start and end apart: 3 -> 9, of which waited for: 2 -> 5; matrix products, arithmetic and copies ran while one was open for 1% -> 1% of each run, Pallas kernels for 6% -> 7%
where the time goes in v4:
time: 267 us; the launch traced here: 266 us
  blocking collectives  86.8 us (33%)
  waiting for transfers between devices  84.1 us (31%)
  starting transfers between devices  40.2 us (15%)
  Pallas kernels  34.4 us (13%)
  between operations  14.2 us (5%)
  local copies, waits for them, and re-layouts  4.18 us (2%)
    all_gather x1, waiting for transfers between devices, per_device(): w = lax.all_gather(packed, 'dp', axis=0, tiled=True)  51 us
    all_to_all x1, blocking collectives, per_device(): rows_in = lax.all_to_all(sent, ('far', 'near'), 0, 0, tiled=True)  41.5 us
    all_to_all x1, blocking collectives, per_device(): lax.all_to_all(back_sent.reshape(along, pair, 4, positions, HEAD), ('far'...  35.6 us
    ppermute x2, waiting for transfers between devices, by_place(): return jnp.concatenate([own_rows, lax.ppermute(other, 'yh', swap)], 0)  22.6 us
    pallas_call x1, Pallas kernels, per_device(): call(functools.partial(finish, steps, grad_scale), (*(shape((half, width)...  12.6 us
    all_to_all x1, blocking collectives, per_device(): lax.all_to_all(both, 'near', 0, 0, tiled=True)  9.69 us
    all_to_all x1, starting transfers between devices, per_device(): lax.all_to_all(part, ('yh', 'far'), 0, 0, tiled=True)  9.19 us
    ppermute x2, starting transfers between devices, by_place(): return jnp.concatenate([own_rows, lax.ppermute(other, 'yh', swap)], 0)  8.45 us
  transfers between devices with their start and end apart: 9, of which 5 were waited for; matrix products, arithmetic and copies ran while one was open for 1% of the time, Pallas kernels for 7%

profile of v4, /device:TPU:24, one launch (start us, length us, event | category | flops | bytes accessed | tf_op | source)
XLA Modules:
  0.0 265.6 jit_solution(13956012077363271221)
XLA Ops:
  7.2 2.2 shard_map.110
  9.5 0.6 broadcast_in_dim.2
  10.2 5.8 %all-to-all-start = ((bf16[16,4,512]{2,1,0:T(4,128)(2,1)}), bf16[16,4,512]{2,1,0:T(4,128)(2,1)S(1)}, u32[]{:S(2)}, u32[]{:S(2)}) async-start(bf16[16,4,512]{2,1,0:T(4,128)(2,1)} %broadcast_in_dim.2), calls=%async_computation | async-start | bytes 131072 | tf_op jit(solution)/shard_map/all_to_all | solution.py:327
  16.0 6.5 %collective-permute-start = (bf16[64,3072]{1,0:T(8,128)(2,1)S(1)}, bf16[64,3072]{1,0:T(8,128)(2,1)S(1)}, u32[]{:S(2)}, u32[]{:S(2)}) collective-permute-start(bf16[64,3072]{1,0:T(8,128)(2,1)S(1)} %get-tuple-element.54), channel_id=1, source_target_pairs={{0,16},{16,0},{1,17},{17,1},{2,18},{18,2},{3,19},{19,3},{4,20},{20... | collective-permute-start | bytes 1179656 | tf_op jit(solution)/shard_map/ppermute | solution.py:337
  22.6 1.9 collective-permute-start.1
  24.6 0.6 reshape.39.up
  25.2 7.6 %collective-permute-done = bf16[64,3072]{1,0:T(8,128)(2,1)S(1)} collective-permute-done((bf16[64,3072]{1,0:T(8,128)(2,1)S(1)}, bf16[64,3072]{1,0:T(8,128)(2,1)S(1)}, u32[]{:S(2)}, u32[]{:S(2)}) %collective-permute-start) | collective-permute-done | bytes 393248 | tf_op jit(solution)/shard_map/ppermute | solution.py:337
  32.8 0.9 pad_maximum_fusion.x
  33.7 15.0 %collective-permute-done.1 = bf16[64,3072]{1,0:T(8,128)(2,1)S(1)} collective-permute-done((bf16[64,3072]{1,0:T(8,128)(2,1)S(1)}, bf16[64,3072]{1,0:T(8,128)(2,1)S(1)}, u32[]{:S(2)}, u32[]{:S(2)}) %collective-permute-start.1) | collective-permute-done | bytes 393248 | tf_op jit(solution)/shard_map/ppermute | solution.py:337
  48.7 0.9 pad_maximum_fusion.1.upstream
  49.7 3.5 %shard_map.111 = (bf16[128,3072]{1,0:T(8,128)(2,1)}, bf16[3072,128]{1,0:T(8,128)(2,1)}, bf16[128,3072]{1,0:T(8,128)(2,1)}, f32[128,1]{1,0:T(8,128)}, f32[128,1]{1,0:T(8,128)}) custom-call(bf16[128,3072]{1,0:T(8,128)(2,1)} %pad_maximum_fusion.x, f32[3,1,3072]{2,1,0:T(1,128)} %bitcast.21, bf16[128,3072]{1,0:T(8,128)(2,1)} %pad_maximum_fusion.1.upstream), custom_call_target="tpu_custom_call" | custom-call | flops 7864320 | bytes 3932160 | tf_op jit(solution)/shard_map/pallas_call | solution.py:342
  53.2 51.0 %all-gather.2.cloned.1.call-done.w.w_down = bf16[3072,2176]{1,0:T(8,128)(2,1)} async-done(((bf16[192,2176]{1,0:T(8,128)(2,1)}), bf16[3072,2176]{1,0:T(8,128)(2,1)}) %all-gather.2.cloned.1.call-update) | async-done | bytes 13369360 | tf_op jit(solution)/shard_map/all_gather | solution.py:326
  104.2 8.3 %shard_map.112 = (bf16[16,2,4,16,128]{4,3,2,1,0:T(8,128)(2,1)}, f32[128,1024]{1,0:T(8,128)}, bf16[128,64]{1,0:T(8,128)(2,1)}) custom-call(bf16[128,3072]{1,0:T(8,128)(2,1)} %get-tuple-element.30.hidden, bf16[128,3072]{1,0:T(8,128)(2,1)} %get-tuple-element.31.branch_grad, bf16[3072,2176]{1,0:T(8,128)(2,1)} %all-gather.2.cloned.1.call-done.w.w_down, ...), custom_call_target="tpu_custom_call" | custom-call | flops 1711276032 | bytes 13369344 | tf_op jit(solution)/shard_map/pallas_call | solution.py:355
  112.4 41.5 %all_to_all.35 = bf16[16,2,4,16,128]{4,3,2,1,0:T(8,128)(2,1)S(1)} all-to-all(bf16[16,2,4,16,128]{4,3,2,1,0:T(8,128)(2,1)} %get-tuple-element.32), channel_id=1, replica_groups=mesh['dp'=16,'yh'=2,'far'=4,'near'=4] {'far','near'}, dimensions={0} | all-to-all | bytes 1048576 | tf_op jit(solution)/shard_map/all_to_all | solution.py:378
  153.9 1.2 shard_map.113
  155.1 35.6 %all_to_all.36.back = bf16[16,2,4,16,128]{4,3,2,1,0:T(8,128)(2,1)} all-to-all(bf16[16,2,4,16,128]{4,3,2,1,0:T(8,128)(2,1)S(1)} %bitcast.19), channel_id=1, replica_groups=mesh['dp'=16,'yh'=2,'far'=4,'near'=4] {'far','near'}, dimensions={0} | all-to-all | bytes 1048576 | tf_op jit(solution)/shard_map/all_to_all | solution.py:387
  190.8 3.2 %shard_map.114 = (bf16[128,1536]{1,0:T(8,128)(2,1)}, bf16[128,64]{1,0:T(8,128)(2,1)}, bf16[16,112,128]{2,1,0:T(8,128)(2,1)}) custom-call(bf16[16,2,4,16,128]{4,3,2,1,0:T(8,128)(2,1)} %all_to_all.36.back, f32[128,1024]{1,0:T(8,128)} %get-tuple-element.33.raw, bf16[128,64]{1,0:T(8,128)(2,1)} %get-tuple-element.34.low, bf16[64,512]{1,0:T(8,128)(2,1)} %reshape.39.up, ...), custom_call_target="tpu_custom_call" | custom-call | flops 134217728 | bytes 2097152 | tf_op jit(solution)/shard_map/pallas_call | solution.py:392
  193.9 5.9 %all-to-all-start.3 = ((bf16[16,112,128]{2,1,0:T(8,128)(2,1)}), bf16[16,112,128]{2,1,0:T(8,128)(2,1)S(1)}, u32[]{:S(2)}, u32[]{:S(2)}) async-start(bf16[16,112,128]{2,1,0:T(8,128)(2,1)} %get-tuple-element.46), calls=%async_computation.3 | async-start | bytes 917504 | tf_op jit(solution)/shard_map/all_to_all | solution.py:402
  199.8 12.6 %shard_map.115 = (bf16[64,3072]{1,0:T(8,128)(2,1)}, bf16[64,3072]{1,0:T(8,128)(2,1)}, bf16[64,3072]{1,0:T(8,128)(2,1)}, bf16[64,3072]{1,0:T(8,128)(2,1)}, f32[72,128]{1,0:T(8,128)}) custom-call(bf16[128,1536]{1,0:T(8,128)(2,1)} %get-tuple-element.36.joined, bf16[128,64]{1,0:T(8,128)(2,1)} %get-tuple-element.37.low_grad, ...), custom_call_target="tpu_custom_call" | custom-call | flops 1711276032 | bytes 16515072 | tf_op jit(solution)/shard_map/pallas_call | solution.py:406
  212.4 0.8 copy-done.2
  213.2 9.7 %all_to_all.37.arrived = bf16[4,48,128]{2,1,0:T(8,128)(2,1)S(1)} all-to-all(bf16[4,48,128]{2,1,0:T(8,128)(2,1)S(1)} %shard_map.117), channel_id=1, replica_groups=mesh['dp'=16,'yh'=2,'far'=4,'near'=4] {'near'}, dimensions={0} | all-to-all | bytes 98304 | tf_op jit(solution)/shard_map/all_to_all | solution.py:455
  222.9 0.7 shard_map.118
  223.6 9.2 %all-to-all-start.5 = ((bf16[8,48,128]{2,1,0:T(8,128)(2,1)}), bf16[8,48,128]{2,1,0:T(8,128)(2,1)S(1)}, u32[]{:S(2)}, u32[]{:S(2)}) async-start(bf16[8,48,128]{2,1,0:T(8,128)(2,1)} %shard_map.118), calls=%async_computation.5 | async-start | bytes 196608 | tf_op jit(solution)/shard_map/all_to_all | solution.py:458
  232.8 1.9 collective-permute-start.2
  234.7 5.4 %collective-permute-start.3 = (bf16[64,3072]{1,0:T(8,128)(2,1)}, bf16[64,3072]{1,0:T(8,128)(2,1)S(1)}, u32[]{:S(2)}, u32[]{:S(2)}) collective-permute-start(bf16[64,3072]{1,0:T(8,128)(2,1)} %get-tuple-element.43), channel_id=1, source_target_pairs={{0,16},{16,0},{1,17},{17,1},{2,18},{18,2},{3,19},{19,3},{4,20},{20... | collective-permute-start | bytes 1179656 | tf_op jit(solution)/shard_map/ppermute | solution.py:437
  240.1 5.2 %all-to-all-done.5.arrived = bf16[8,48,128]{2,1,0:T(8,128)(2,1)S(1)} async-done(((bf16[8,48,128]{2,1,0:T(8,128)(2,1)}), bf16[8,48,128]{2,1,0:T(8,128)(2,1)S(1)}, u32[]{:S(2)}, u32[]{:S(2)}) %all-to-all-start.5) | async-done | bytes 98336 | tf_op jit(solution)/shard_map/all_to_all | solution.py:458
  246.0 3.5 %all-to-all-start.6 = ((bf16[4,48,128]{2,1,0:T(8,128)(2,1)}), bf16[4,48,128]{2,1,0:T(8,128)(2,1)S(1)}, u32[]{:S(2)}, u32[]{:S(2)}) async-start(bf16[4,48,128]{2,1,0:T(8,128)(2,1)} %shard_map.119), calls=%async_computation.6 | async-start | bytes 98304 | tf_op jit(solution)/shard_map/all_to_all | solution.py:469
  249.5 5.3 %collective-permute-done.3.other_b = bf16[64,3072]{1,0:T(8,128)(2,1)S(1)} collective-permute-done((bf16[64,3072]{1,0:T(8,128)(2,1)}, bf16[64,3072]{1,0:T(8,128)(2,1)S(1)}, u32[]{:S(2)}, u32[]{:S(2)}) %collective-permute-start.3) | collective-permute-done | bytes 393248 | tf_op jit(solution)/shard_map/ppermute | solution.py:437
  254.8 1.0 copy-done
  255.8 1.0 copy-done.1
  256.8 1.2 shard_map.116
  258.0 0.8 shard_map.120
  (19 shorter events, 0.9 us)
Async XLA Ops:
  7.2 2.3 copy-start.5
  7.2 8.8 %copy-start.3 = (bf16[1,1,128,3072]{3,2,1,0:T(8,128)(2,1)S(1)}, bf16[1,1,128,3072]{3,2,1,0:T(8,128)(2,1)}, u32[]{:S(2)}) copy-start(bf16[1,1,128,3072]{3,2,1,0:T(8,128)(2,1)} %param.7) | copy-start | bytes 2359300
  7.2 97.0 %all-gather.2.cloned.1.call-start = ((), (), s32[]{:S(2)}) async-start(), calls=%async_computation.7 | async-start | bytes 14204928 | tf_op jit(solution)/shard_map/all_gather | solution.py:326
  9.5 13.1 %copy-start.4 = (bf16[1,1,128,3072]{3,2,1,0:T(8,128)(2,1)S(1)}, bf16[1,1,128,3072]{3,2,1,0:T(8,128)(2,1)}, u32[]{:S(2)}) copy-start(bf16[1,1,128,3072]{3,2,1,0:T(8,128)(2,1)} %param.13) | copy-start | bytes 2359300
  10.2 14.4 %all-to-all-start = ((bf16[16,4,512]{2,1,0:T(4,128)(2,1)}), bf16[16,4,512]{2,1,0:T(4,128)(2,1)S(1)}, u32[]{:S(2)}, u32[]{:S(2)}) async-start(bf16[16,4,512]{2,1,0:T(4,128)(2,1)} %broadcast_in_dim.2), calls=%async_computation | async-start | bytes 131072 | tf_op jit(solution)/shard_map/all_to_all | solution.py:327
  16.0 16.7 %collective-permute-start = (bf16[64,3072]{1,0:T(8,128)(2,1)S(1)}, bf16[64,3072]{1,0:T(8,128)(2,1)S(1)}, u32[]{:S(2)}, u32[]{:S(2)}) collective-permute-start(bf16[64,3072]{1,0:T(8,128)(2,1)S(1)} %get-tuple-element.54), channel_id=1, source_target_pairs={{0,16},{16,0},{1,17},{17,1},{2,18},{18,2},{3,19},{19,3},{4,20},{20... | collective-permute-start | bytes 1179656 | tf_op jit(solution)/shard_map/ppermute | solution.py:337
  22.6 26.1 %collective-permute-start.1 = (bf16[64,3072]{1,0:T(8,128)(2,1)S(1)}, bf16[64,3072]{1,0:T(8,128)(2,1)S(1)}, u32[]{:S(2)}, u32[]{:S(2)}) collective-permute-start(bf16[64,3072]{1,0:T(8,128)(2,1)S(1)} %get-tuple-element.52), channel_id=1, source_target_pairs={{0,16},{16,0},{1,17},{17,1},{2,18},{18,2},{3,19},{19,3},{4,20},{20... | collective-permute-start | bytes 1179656 | tf_op jit(solution)/shard_map/ppermute | solution.py:337
  193.9 18.4 %all-to-all-start.3 = ((bf16[16,112,128]{2,1,0:T(8,128)(2,1)}), bf16[16,112,128]{2,1,0:T(8,128)(2,1)S(1)}, u32[]{:S(2)}, u32[]{:S(2)}) async-start(bf16[16,112,128]{2,1,0:T(8,128)(2,1)} %get-tuple-element.46), calls=%async_computation.3 | async-start | bytes 917504 | tf_op jit(solution)/shard_map/all_to_all | solution.py:402
  212.4 0.8 copy-start.2
  223.6 21.7 %all-to-all-start.5 = ((bf16[8,48,128]{2,1,0:T(8,128)(2,1)}), bf16[8,48,128]{2,1,0:T(8,128)(2,1)S(1)}, u32[]{:S(2)}, u32[]{:S(2)}) async-start(bf16[8,48,128]{2,1,0:T(8,128)(2,1)} %shard_map.118), calls=%async_computation.5 | async-start | bytes 196608 | tf_op jit(solution)/shard_map/all_to_all | solution.py:458
  232.8 16.7 %collective-permute-start.2 = (bf16[64,3072]{1,0:T(8,128)(2,1)}, bf16[64,3072]{1,0:T(8,128)(2,1)S(1)}, u32[]{:S(2)}, u32[]{:S(2)}) collective-permute-start(bf16[64,3072]{1,0:T(8,128)(2,1)} %get-tuple-element.41), channel_id=1, source_target_pairs={{0,16},{16,0},{1,17},{17,1},{2,18},{18,2},{3,19},{19,3},{4,20},{20... | collective-permute-start | bytes 1179656 | tf_op jit(solution)/shard_map/ppermute | solution.py:436
  234.7 20.1 %collective-permute-start.3 = (bf16[64,3072]{1,0:T(8,128)(2,1)}, bf16[64,3072]{1,0:T(8,128)(2,1)S(1)}, u32[]{:S(2)}, u32[]{:S(2)}) collective-permute-start(bf16[64,3072]{1,0:T(8,128)(2,1)} %get-tuple-element.43), channel_id=1, source_target_pairs={{0,16},{16,0},{1,17},{17,1},{2,18},{18,2},{3,19},{19,3},{4,20},{20... | collective-permute-start | bytes 1179656 | tf_op jit(solution)/shard_map/ppermute | solution.py:437
  246.0 12.0 %all-to-all-start.6 = ((bf16[4,48,128]{2,1,0:T(8,128)(2,1)}), bf16[4,48,128]{2,1,0:T(8,128)(2,1)S(1)}, u32[]{:S(2)}, u32[]{:S(2)}) async-start(bf16[4,48,128]{2,1,0:T(8,128)(2,1)} %shard_map.119), calls=%async_computation.6 | async-start | bytes 98304 | tf_op jit(solution)/shard_map/all_to_all | solution.py:469
  254.8 1.0 copy-start
  255.8 1.0 copy-start.1
Sparse Core Ops, SparseCore 0:
  10.2 93.9 all-gather.1

commit v5 on v3

--- a/solution.py
+++ b/solution.py
@@ -22,7 +22,7 @@
     return lax.dot_general(a, b, dims, preferred_element_type=F32)
 
 
-def call(body, out_shape, grid=None, in_specs=None, out_specs=None, scratch=(), flops=0, moved=0, vmem=60):
+def call(body, out_shape, grid=None, in_specs=None, out_specs=None, scratch=(), flops=0, moved=0, vmem=20):
     extra = {} if grid is None else {"grid": grid, "in_specs": in_specs, "out_specs": out_specs}
     return pl.pallas_call(
         body,
@@ -85,11 +85,14 @@
     return parts
 
 
-def projections(rank, hidden, branch_grad, w, w_down, up, sent, raw, low_out):
+def projections(rank, hidden, branch_grad, w_top, w_low, w_down, up, sent, raw, low_out):
     t = pl.program_id(0)
-    n = w.shape[1]
+    half, n = w_top.shape
     heads = n // HEAD
     positions = sent.shape[2]
+
+    def product(rows):
+        return dot(rows[:, :half], w_top[...]) + dot(rows[:, half:], w_low[...])
 
     def store(x, normed):
         scales = head_scales(x) if normed else None
@@ -105,24 +108,24 @@
     def _():
         low_out[...] = dot(hidden[...], w_down[...])[:, : 2 * rank].astype(BF16)
         up_q, _ = split_up(up[...], rank)
-        q = dot(hidden[...], w[...]) + dot(low_out[...], up_q)
+        q = product(hidden) + dot(low_out[...], up_q)
         raw[:, :n] = q
         store(q, True)
 
     @pl.when(t == 1)
     def _():
-        k = dot(hidden[...], w[...])
+        k = product(hidden)
         raw[:, n:] = k
         store(k, True)
 
     @pl.when(t == 2)
     def _():
         _, up_v = split_up(up[...], rank)
-        store(dot(hidden[...], w[...]) + dot(low_out[...], up_v), False)
+        store(product(hidden) + dot(low_out[...], up_v), False)
 
     @pl.when(t == 3)
     def _():
-        store(dot(branch_grad[...], w[...]), False)
+        store(product(branch_grad), False)
 
 
 def attention(rows_in, back):
@@ -184,17 +187,19 @@
     low_rows = low[...]
     row = lax.broadcasted_iota(jnp.int32, (2 * rank, n), 0)
     up_grad = jnp.where(row < rank, dot(low_rows, dq, TN), dot(low_rows, dv, TN)) * scale
-    parts = sections.shape[0]
+    near = heads
+    parts = sections.shape[0] // near
     per, half = down.shape[0] // parts, down.shape[0] // parts // 2
-    own = 2 * rank // parts
+    own, rows = 2 * rank // parts, half // near
     left = lax.broadcasted_iota(jnp.int32, (half, HEAD), 1) < 2 * rank
     for d in range(parts):
-        sections[d, :half] = jnp.where(
+        both = jnp.where(
             left, down[d * per : d * per + half], down[d * per + half : (d + 1) * per]
         ).astype(BF16)
-        sections[d, half:] = jnp.concatenate(
-            [up_grad[d * own : (d + 1) * own, h * HEAD : (h + 1) * HEAD] for h in range(heads)], 0
-        ).astype(BF16)
+        mine = up_grad[d * own : (d + 1) * own].astype(BF16)
+        for i in range(near):
+            sections[d * near + i, :rows] = both[i * rows : (i + 1) * rows]
+            sections[d * near + i, rows:] = mine[:, i * HEAD : (i + 1) * HEAD]
 
 
 def finish(
@@ -249,19 +254,11 @@
 def spread(arrived, mod_rows, both):
     share = jnp.sum(arrived[...].astype(F32), 0).astype(BF16)
     rows = mod_rows[...].astype(BF16)
-    parts = both.shape[0]
-    rows_a, rows_b = share.shape[0] // parts, rows.shape[0] // parts
-    pad = jnp.zeros((both.shape[1] - rows_a - rows_b, HEAD), F32)
-    for j in range(parts):
-        piece = jnp.concatenate(
-            [
-                share[j * rows_a : (j + 1) * rows_a].astype(F32),
-                rows[j * rows_b : (j + 1) * rows_b].astype(F32),
-                pad,
-            ],
-            0,
-        )
-        both[j] = piece.astype(BF16)
+    a, b = share.shape[0], rows.shape[0]
+    first = 8 * -(-a // 8)
+    for j in range(both.shape[0]):
+        both[j, :a] = share
+        both[j, first : first + b] = rows
 
 
 def summed(arrived, out):
@@ -269,18 +266,18 @@
     out[...] = jnp.broadcast_to(total[None], out.shape)
 
 
-def collected(rows_a, rows_b, shares, down_t, up_grad, mod_grad):
+def collected(shares, down_t, up_grad, mod_grad):
     values = shares[...].astype(F32)
-    parts = values.shape[0]
-    cols = down_t.shape[0]
-    own = up_grad.shape[0]
-    half = down_t.shape[1] // 2
-    a = jnp.concatenate([values[j, :rows_a] for j in range(parts)], 0)
-    b = jnp.concatenate([values[j, rows_a : rows_a + rows_b] for j in range(parts)], 0)
-    down_t[...] = jnp.concatenate([a[:half, :cols], a[:half, cols:]], 0).T
-    for h in range(up_grad.shape[1] // HEAD):
-        up_grad[:, h * HEAD : (h + 1) * HEAD] = a[half + h * own : half + (h + 1) * own]
+    near = values.shape[0]
+    cols, own = down_t.shape[0], up_grad.shape[0]
+    rows = down_t.shape[1] // 2 // near
+    first = 8 * -(-(rows + own) // 8)
+    a = jnp.concatenate([values[i, :rows] for i in range(near)], 0)
+    down_t[...] = jnp.concatenate([a[:, :cols], a[:, cols:]], 0).T
+    for i in range(near):
+        up_grad[:, i * HEAD : (i + 1) * HEAD] = values[i, rows : rows + own]
     tiles = mod_grad.shape[2] // HEAD
+    b = jnp.sum(values[:, first : first + 3 * tiles], 0)
     for i in range(3 * tiles):
         mod_grad[i // tiles, :, (i % tiles) * HEAD : (i % tiles + 1) * HEAD] = b[i : i + 1]
 
@@ -297,8 +294,9 @@
     own = width // dp
 
     cols = 4 * n + HEAD
-    packed = call(pack, shape((own, cols), BF16), moved=4 * own * cols)(qkv, out_w.T, down_w.T)
+    packed = call(pack, shape((own, cols), BF16), moved=4 * own * cols, vmem=60)(qkv, out_w.T, down_w.T)
     w = lax.all_gather(packed, "dp", axis=0, tiled=True)
+    w = pltpu.with_memory_space_constraint(w, pltpu.HBM)
     up = lax.all_to_all(
         jnp.broadcast_to(up_w[None], (dp, *up_w.shape)), "dp", 0, 0, tiled=True
     ).reshape(2 * rank, n)
@@ -329,7 +327,8 @@
         in_specs=[
             whole(m, width),
             whole(m, width),
-            pl.BlockSpec((width, n), lambda t: (0, t)),
+            pl.BlockSpec((width // 2, n), lambda t: (0, t)),
+            pl.BlockSpec((width // 2, n), lambda t: (1, t)),
             pl.BlockSpec((width, HEAD), lambda t: (0, 4 * n // HEAD)),
             whole(2 * rank, n),
         ],
@@ -340,7 +339,11 @@
         ),
         flops=2 * m * width * cols,
         moved=2 * width * cols,
-    )(hidden, branch_grad, w, w, up)
+    )(
+        pltpu.with_memory_space_constraint(hidden, pltpu.HBM),
+        pltpu.with_memory_space_constraint(branch_grad, pltpu.HBM),
+        w, w, w, up,
+    )
     rows_in = lax.all_to_all(sent, CTX, 0, 0, tiled=True)
 
     back_sent = call(
@@ -352,18 +355,20 @@
     )(rows_in)
     back = lax.all_to_all(back_sent, CTX, 0, 0, tiled=True)
 
-    own_rows = own // 2 + (2 * rank // dp) * heads
+    near, far = lax.axis_size("near"), lax.axis_size("yh") * lax.axis_size("far")
+    assert near == heads
+    own_rows = own // 2 // near + 2 * rank // dp
     joined, low_grad, sections = call(
         functools.partial(adapter_terms, rank, grad_scale),
         (
             shape((m, 3 * n), BF16),
             shape((m, 2 * rank), BF16),
-            shape((dp, own_rows, HEAD), BF16),
+            shape((dp * near, own_rows, HEAD), BF16),
         ),
         flops=2 * m * width * HEAD + 8 * m * n * 64,
         moved=m * width * 2 + m * n * 20,
     )(back, raw, low, up, hidden_t)
-    arrived = lax.all_to_all(sections, "dp", 0, 0, tiled=True)
+    arrived = lax.all_to_all(sections, ("dp", "near"), 0, 0, tiled=True)
 
     per = 2
     steps, cb = dp // per, per * own
@@ -398,18 +403,13 @@
         moved=2 * width * cols + 8 * m * width,
     )(joined, low_grad, back, w, x, mean, rstd, mod, upstream)
 
-    near, far = lax.axis_size("near"), lax.axis_size("yh") * lax.axis_size("far")
-    rows_a, rows_b = own_rows // near, mod_rows.shape[0] // near
-    rows = 16 * -(-(rows_a + rows_b) // 16)
-    both = call(spread, shape((near, rows, HEAD), BF16), moved=2**19, vmem=8)(arrived, mod_rows)
-    part = call(summed, shape((far, rows, HEAD), BF16), moved=2**17, vmem=8)(
-        lax.all_to_all(both, "near", 0, 0, tiled=True)
-    )
-    part = call(summed, shape((near, rows, HEAD), BF16), moved=2**17, vmem=8)(
+    rows = 8 * -(-own_rows // 8) + mod_rows.shape[0]
+    part = call(spread, shape((far, rows, HEAD), BF16), moved=2**20, vmem=8)(arrived, mod_rows)
+    part = call(summed, shape((near, rows, HEAD), BF16), moved=2**18, vmem=8)(
         lax.all_to_all(part, ("yh", "far"), 0, 0, tiled=True)
     )
     down_t, up_grad, mod_grad = call(
-        functools.partial(collected, rows_a, rows_b),
+        collected,
         (
             shape((2 * rank, own), F32),
             shape((2 * rank // dp, n), F32),

time: 262 us -> 260 us (level)
  Pallas kernels: 31.8 us -> 26 us
  blocking collectives: 122 us -> 117 us
  local copies, waits for them, and re-layouts: 2.72 us -> 6.15 us
  waiting for transfers between devices: 77 us -> 79.9 us
  starting transfers between devices: 11.3 us -> 14.2 us
    all_to_all x1 -> x0, blocking collectives: 9.49 us -> none  [per_device(): lax.all_to_all(both, 'near', 0, 0, tiled=True)]
    all_to_all x1, waiting for transfers between devices: 0.01 us -> 4.66 us  [per_device(): arrived = lax.all_to_all(sections, ('dp', 'near'), 0, 0, tiled=True)]
    unnamed x2 -> x16, local copies, waits for them, and re-layouts: 0.76 us -> 4.79 us
    all_to_all x1, blocking collectives: 20 us -> 23.2 us  [per_device(): lax.all_to_all(part, ('yh', 'far'), 0, 0, tiled=True)]
    all_to_all x1, starting transfers between devices: 5.44 us -> 8.43 us  [per_device(): arrived = lax.all_to_all(sections, ('dp', 'near'), 0, 0, tiled=True)]
  transfers between devices with their start and end apart: 3 -> 3, of which waited for: 2 -> 2; matrix products, arithmetic and copies ran while one was open for 1% -> 1% of each run, Pallas kernels for 6% -> 5%
where the time goes in v5:
time: 260 us; the launch traced here: 257 us
  blocking collectives  117 us (45%)
  waiting for transfers between devices  79.9 us (31%)
  Pallas kernels  26 us (10%)
  starting transfers between devices  14.2 us (5%)
  between operations  14.1 us (5%)
  local copies, waits for them, and re-layouts  6.15 us (2%)
    all_gather x1, waiting for transfers between devices, per_device(): w = lax.all_gather(packed, 'dp', axis=0, tiled=True)  75.3 us
    all_to_all x1, blocking collectives, per_device(): rows_in = lax.all_to_all(sent, CTX, 0, 0, tiled=True)  45.3 us
    all_to_all x1, blocking collectives, per_device(): back = lax.all_to_all(back_sent, CTX, 0, 0, tiled=True)  38.3 us
    all_to_all x1, blocking collectives, per_device(): lax.all_to_all(part, ('yh', 'far'), 0, 0, tiled=True)  23.2 us
    pallas_call x1, Pallas kernels, per_device(): call(functools.partial(finish, steps, grad_scale), (shape((m, width), BF1...  11.8 us
    all_to_all x1, blocking collectives, per_device(): lax.all_to_all(part, 'near', 0, 0, tiled=True)  9.79 us
    all_to_all x1, starting transfers between devices, per_device(): arrived = lax.all_to_all(sections, ('dp', 'near'), 0, 0, tiled=True)  8.43 us
    pallas_call x1, Pallas kernels, per_device(): call(functools.partial(projections, rank), (shape((ctx, 4, positions, HEA...  7.35 us
  transfers between devices with their start and end apart: 3, of which 2 were waited for; matrix products, arithmetic and copies ran while one was open for 1% of the time, Pallas kernels for 5%

profile of v5, /device:TPU:24, one launch (start us, length us, event | category | flops | bytes accessed | tf_op | source)
XLA Modules:
  0.0 257.0 jit_solution(9316874221151602193)
XLA Ops:
  7.2 0.0 all-gather.2.cloned.1.call-start
  7.2 2.2 shard_map.111
  9.4 0.0 all-gather.2.cloned.1.call-update
  9.4 1.3 broadcast_in_dim.2
  10.8 5.8 %all-to-all-start = ((bf16[16,4,512]{2,1,0:T(4,128)(2,1)}), bf16[16,4,512]{2,1,0:T(4,128)(2,1)S(1)}, u32[]{:S(2)}, u32[]{:S(2)}) async-start(bf16[16,4,512]{2,1,0:T(4,128)(2,1)} %broadcast_in_dim.2), calls=%async_computation | async-start | bytes 131072 | tf_op jit(solution)/shard_map/all_to_all | solution.py:300
  16.5 0.0 copy-start
  16.5 1.1 copy-done
  17.7 0.0 copy-start.2
  17.7 1.1 copy-done.2
  18.8 0.0 copy-start.6
  18.8 0.8 copy-done.6
  19.6 1.0 shard_map.110
  20.5 0.0 copy-start.4
  20.6 0.9 copy-done.4
  21.4 0.9 copy-done.5
  22.3 0.0 all-to-all-done
  22.3 75.3 %all-gather.2.cloned.1.call-done.w_top.w_low.w_down.w = bf16[3072,2176]{1,0:T(8,128)(2,1)} async-done(((bf16[192,2176]{1,0:T(8,128)(2,1)}), bf16[3072,2176]{1,0:T(8,128)(2,1)}) %all-gather.2.cloned.1.call-update) | async-done | bytes 13369360 | tf_op jit(solution)/shard_map/all_gather | solution.py:298
  97.6 7.4 %shard_map.112 = (bf16[32,4,16,128]{3,2,1,0:T(8,128)(2,1)S(1)}, f32[128,1024]{1,0:T(8,128)S(1)}, bf16[128,64]{1,0:T(8,128)(2,1)S(1)}) custom-call(bf16[128,3072]{1,0:T(8,128)(2,1)} %copy-done.4, bf16[128,3072]{1,0:T(8,128)(2,1)} %copy-done.5, bf16[3072,2176]{1,0:T(8,128)(2,1)} %all-gather.2.cloned.1.call-done.w_top.w_low.w_down.w, ...), custom_call_target="tpu_custom_call" | custom-call | flops 1711276032 | bytes 13369344 | tf_op jit(solution)/shard_map/pallas_call | solution.py:319
  105.0 45.3 %all_to_all.30.rows_in = bf16[32,4,16,128]{3,2,1,0:T(8,128)(2,1)S(1)} all-to-all(bf16[32,4,16,128]{3,2,1,0:T(8,128)(2,1)S(1)} %get-tuple-element.24), channel_id=1, replica_groups=mesh['dp'=16,'yh'=2,'far'=4,'near'=4] {'yh','far','near'}, dimensions={0} | all-to-all | bytes 1048576 | tf_op jit(solution)/shard_map/all_to_all | solution.py:347
  150.2 1.2 shard_map.113
  151.4 38.3 %all_to_all.31.back = bf16[32,4,16,128]{3,2,1,0:T(8,128)(2,1)S(1)} all-to-all(bf16[32,4,16,128]{3,2,1,0:T(8,128)(2,1)S(1)} %shard_map.113), channel_id=1, replica_groups=mesh['dp'=16,'yh'=2,'far'=4,'near'=4] {'yh','far','near'}, dimensions={0} | all-to-all | bytes 1048576 | tf_op jit(solution)/shard_map/all_to_all | solution.py:356
  189.7 1.6 shard_map.114
  191.3 8.4 %all-to-all-start.3 = ((bf16[64,28,128]{2,1,0:T(8,128)(2,1)}), bf16[64,28,128]{2,1,0:T(8,128)(2,1)S(1)}, u32[]{:S(2)}, u32[]{:S(2)}) async-start(bf16[64,28,128]{2,1,0:T(8,128)(2,1)} %get-tuple-element.34), calls=%async_computation.3 | async-start | bytes 1048576 | tf_op jit(solution)/shard_map/all_to_all | solution.py:371
  199.8 0.0 copy-done.1
  199.8 0.0 copy-done.3
  199.8 0.0 copy-done.7
  199.8 11.8 %shard_map.115 = (bf16[128,3072]{1,0:T(8,128)(2,1)}, bf16[128,3072]{1,0:T(8,128)(2,1)}, f32[72,128]{1,0:T(8,128)S(1)}) custom-call(bf16[128,1536]{1,0:T(8,128)(2,1)S(1)} %get-tuple-element.28.joined, bf16[128,64]{1,0:T(8,128)(2,1)S(1)} %get-tuple-element.29.low_grad, bf16[32,4,16,128]{3,2,1,0:T(8,128)(2,1)S(1)} %all_to_all.31.back, ...), custom_call_target="tpu_custom_call" | custom-call | flops 1711276032 | bytes 16515072 | tf_op jit(solution)/shard_map/pallas_call | solution.py:375
  211.5 4.7 %all-to-all-done.3.arrived = bf16[64,28,128]{2,1,0:T(8,128)(2,1)S(1)} async-done(((bf16[64,28,128]{2,1,0:T(8,128)(2,1)}), bf16[64,28,128]{2,1,0:T(8,128)(2,1)S(1)}, u32[]{:S(2)}, u32[]{:S(2)}) %all-to-all-start.3) | async-done | bytes 458784 | tf_op jit(solution)/shard_map/all_to_all | solution.py:371
  216.2 0.1 shard_map.116
  216.3 23.2 %all_to_all.32.arrived = bf16[8,104,128]{2,1,0:T(8,128)(2,1)S(1)} all-to-all(bf16[8,104,128]{2,1,0:T(8,128)(2,1)S(1)} %shard_map.116), channel_id=1, replica_groups=mesh['dp'=16,'yh'=2,'far'=4,'near'=4] {'yh','far'}, dimensions={0} | all-to-all | bytes 425984 | tf_op jit(solution)/shard_map/all_to_all | solution.py:409
  239.5 9.8 %all_to_all.33.shares = bf16[4,104,128]{2,1,0:T(8,128)(2,1)S(1)} all-to-all(bf16[4,104,128]{2,1,0:T(8,128)(2,1)S(1)} %shard_map.117), channel_id=1, replica_groups=mesh['dp'=16,'yh'=2,'far'=4,'near'=4] {'near'}, dimensions={0} | all-to-all | bytes 212992 | tf_op jit(solution)/shard_map/all_to_all | solution.py:420
  249.3 0.8 shard_map.118
  (6 shorter events, 0.1 us)
Async XLA Ops:
  7.2 90.4 %all-gather.2.cloned.1.call-start = ((), (), s32[]{:S(2)}) async-start(), calls=%async_computation.6 | async-start | bytes 14204928 | tf_op jit(solution)/shard_map/all_gather | solution.py:298
  10.8 11.6 %all-to-all-start = ((bf16[16,4,512]{2,1,0:T(4,128)(2,1)}), bf16[16,4,512]{2,1,0:T(4,128)(2,1)S(1)}, u32[]{:S(2)}, u32[]{:S(2)}) async-start(bf16[16,4,512]{2,1,0:T(4,128)(2,1)} %broadcast_in_dim.2), calls=%async_computation | async-start | bytes 131072 | tf_op jit(solution)/shard_map/all_to_all | solution.py:300
  16.5 1.1 copy-start
  17.7 1.1 copy-start.2
  18.8 0.8 copy-start.6
  20.5 0.9 copy-start.4
  21.4 0.9 copy-start.5
  97.6 102.2 %copy-start.1 = (bf16[1,1,128,3072]{3,2,1,0:T(8,128)(2,1)S(1)}, bf16[1,1,128,3072]{3,2,1,0:T(8,128)(2,1)}, u32[]{:S(2)}) copy-start(bf16[1,1,128,3072]{3,2,1,0:T(8,128)(2,1)} %param.7) | copy-start | bytes 2359300
  97.6 102.2 %copy-start.3 = (bf16[1,1,128,3072]{3,2,1,0:T(8,128)(2,1)S(1)}, bf16[1,1,128,3072]{3,2,1,0:T(8,128)(2,1)}, u32[]{:S(2)}) copy-start(bf16[1,1,128,3072]{3,2,1,0:T(8,128)(2,1)} %param.13) | copy-start | bytes 2359300
  97.6 102.2 %copy-start.7 = (f32[1,3,3072]{2,0,1:T(1,128)S(1)}, f32[1,3,3072]{2,0,1:T(1,128)}, u32[]{:S(2)}) copy-start(f32[1,3,3072]{2,0,1:T(1,128)} %param.8) | copy-start | bytes 110596
  191.3 24.9 %all-to-all-start.3 = ((bf16[64,28,128]{2,1,0:T(8,128)(2,1)}), bf16[64,28,128]{2,1,0:T(8,128)(2,1)S(1)}, u32[]{:S(2)}, u32[]{:S(2)}) async-start(bf16[64,28,128]{2,1,0:T(8,128)(2,1)} %get-tuple-element.34), calls=%async_computation.3 | async-start | bytes 1048576 | tf_op jit(solution)/shard_map/all_to_all | solution.py:371
Sparse Core Ops, SparseCore 0:
  10.1 87.3 all-gather.1

commit v6 on v3

--- a/solution.py
+++ b/solution.py
@@ -22,8 +22,10 @@
     return lax.dot_general(a, b, dims, preferred_element_type=F32)
 
 
-def call(body, out_shape, grid=None, in_specs=None, out_specs=None, scratch=(), flops=0, moved=0, vmem=60):
-    extra = {} if grid is None else {"grid": grid, "in_specs": in_specs, "out_specs": out_specs}
+def call(body, out_shape, grid=None, in_specs=None, out_specs=None, scratch=(), flops=0, moved=0, vmem=20):
+    extra = {} if in_specs is None else {"in_specs": in_specs, "out_specs": out_specs}
+    if grid is not None:
+        extra["grid"] = grid
     return pl.pallas_call(
         body,
         out_shape=out_shape,
@@ -85,44 +87,53 @@
     return parts
 
 
-def projections(rank, hidden, branch_grad, w, w_down, up, sent, raw, low_out):
-    t = pl.program_id(0)
-    n = w.shape[1]
+def projections(rank, hidden_at, branch_at, w_at, up, sent, raw, low_out, hidden, branch, w, sems):
+    n = up.shape[1]
     heads = n // HEAD
     positions = sent.shape[2]
 
-    def store(x, normed):
-        scales = head_scales(x) if normed else None
+    def fetch(src, dst, i):
+        return pltpu.make_async_copy(src, dst, sems.at[i])
+
+    def columns(i, start, size):
+        at = pl.ds(start, size)
+        return fetch(w_at.at[:, at], w.at[:, at], i)
+
+    blocks = [columns(i, i * n, n) for i in range(4)]
+    down = columns(4, 4 * n, HEAD)
+    rows = fetch(hidden_at, hidden, 5)
+    grads = fetch(branch_at, branch, 6)
+    for copy in (rows, down, *blocks[:3], grads, blocks[3]):
+        copy.start()
+
+    def store(t, x):
+        scales = head_scales(x) if t < 2 else None
         for h in range(heads):
-            rows = x[:, h * HEAD : (h + 1) * HEAD]
-            if normed:
-                rows = rows * scales[h]
-            rows = rows.astype(BF16)
+            part = x[:, h * HEAD : (h + 1) * HEAD]
+            if t < 2:
+                part = part * scales[h]
+            part = part.astype(BF16)
             for g in range(x.shape[0] // positions):
-                sent[g * heads + h, 0] = rows[g * positions : (g + 1) * positions]
-
-    @pl.when(t == 0)
-    def _():
-        low_out[...] = dot(hidden[...], w_down[...])[:, : 2 * rank].astype(BF16)
-        up_q, _ = split_up(up[...], rank)
-        q = dot(hidden[...], w[...]) + dot(low_out[...], up_q)
-        raw[:, :n] = q
-        store(q, True)
-
-    @pl.when(t == 1)
-    def _():
-        k = dot(hidden[...], w[...])
-        raw[:, n:] = k
-        store(k, True)
-
-    @pl.when(t == 2)
-    def _():
-        _, up_v = split_up(up[...], rank)
-        store(dot(hidden[...], w[...]) + dot(low_out[...], up_v), False)
-
-    @pl.when(t == 3)
-    def _():
-        store(dot(branch_grad[...], w[...]), False)
+                sent[g * heads + h, t] = part[g * positions : (g + 1) * positions]
+
+    up_q, up_v = split_up(up[...], rank)
+    rows.wait()
+    down.wait()
+    low = dot(hidden[...], w[:, 4 * n :])[:, : 2 * rank].astype(BF16)
+    low_out[...] = low
+    blocks[0].wait()
+    q = dot(hidden[...], w[:, :n]) + dot(low, up_q)
+    raw[:, :n] = q
+    store(0, q)
+    blocks[1].wait()
+    k = dot(hidden[...], w[:, n : 2 * n])
+    raw[:, n:] = k
+    store(1, k)
+    blocks[2].wait()
+    store(2, dot(hidden[...], w[:, 2 * n : 3 * n]) + dot(low, up_v))
+    grads.wait()
+    blocks[3].wait()
+    store(3, dot(branch[...], w[:, 3 * n : 4 * n]))
 
 
 def attention(rows_in, back):
@@ -198,52 +209,48 @@
 
 
 def finish(
-    steps, grad_scale, joined, low_grad, back, w, x, mean, rstd, mod, upstream,
-    tokens_grad, mixed, mod_rows, held, sums, s1, s2, attended,
+    steps, grad_scale, joined, low_grad, back, x, mean, rstd, mod, upstream, w_at,
+    tokens_grad, mixed, mod_rows, held, w, sems,
 ):
-    j = pl.program_id(0)
-    width = w.shape[0]
-    total = steps * width
+    width = x.shape[1] // steps
+    total = x.shape[1]
     n3 = joined.shape[1]
-    at = pl.ds(pl.multiple_of(j * width, width), width)
-
-    @pl.when(j == 0)
-    def _():
-        s1[...] = jnp.zeros_like(s1)
-        s2[...] = jnp.zeros_like(s2)
-        attended[...] = unpack_blocks(back, 3, n3 // 3 // HEAD)
-
     n4 = n3 + n3 // 3
-    hg = dot(joined[...], w[:, :n3], NT) + dot(low_grad[...], w[:, n4 : n4 + low_grad.shape[1]], NT)
-    out = dot(attended[...], w[:, n3:n4], NT)
-    values = x[:, at].astype(F32)
-    up_rows = upstream[:, at].astype(F32)
-    mixed[:, at] = (values + mod[2, :, at] * out).astype(BF16)
-    normed = (values - mean[...]) * rstd[...]
-    ng = hg * (1.0 + mod[1, :, at])
-    sums[0:1, at] = jnp.sum(hg, 0, keepdims=True) * grad_scale
-    sums[1:2, at] = jnp.sum(hg * normed, 0, keepdims=True) * grad_scale
-    sums[2:3, at] = jnp.sum(up_rows * out, 0, keepdims=True) * grad_scale
-    held[:, at] = ng
-    s1[...] += jnp.sum(ng, -1, keepdims=True)
-    s2[...] += jnp.sum(ng * normed, -1, keepdims=True)
-
-    @pl.when(j == steps - 1)
-    def _():
-        m1 = s1[...] * (1.0 / total)
-        m2 = s2[...] * (1.0 / total)
-        for i in range(steps):
-            c = slice(i * width, (i + 1) * width)
-            nrm = (x[:, c].astype(F32) - mean[...]) * rstd[...]
-            tokens_grad[:, c] = (
-                upstream[:, c].astype(F32) + rstd[...] * (held[:, c] - m1 - nrm * m2)
-            ).astype(BF16)
-        tiles = total // HEAD
-        for r in range(3):
-            for i in range(tiles):
-                mod_rows[r * tiles + i : r * tiles + i + 1, :] = sums[
-                    r : r + 1, i * HEAD : (i + 1) * HEAD
-                ]
+    tiles = total // HEAD
+    copies = []
+    for j in range(steps):
+        at = pl.ds(j * width, width)
+        copies.append(pltpu.make_async_copy(w_at.at[at], w.at[at], sems.at[j]))
+        copies[j].start()
+    attended = unpack_blocks(back, 3, n3 // 3 // HEAD)
+    s1 = jnp.zeros((x.shape[0], 1), F32)
+    s2 = jnp.zeros((x.shape[0], 1), F32)
+    for j in range(steps):
+        c = slice(j * width, (j + 1) * width)
+        copies[j].wait()
+        hg = dot(joined[...], w[c, :n3], NT) + dot(low_grad[...], w[c, n4 : n4 + low_grad.shape[1]], NT)
+        out = dot(attended, w[c, n3:n4], NT)
+        values = x[:, c].astype(F32)
+        up_rows = upstream[:, c].astype(F32)
+        mixed[:, c] = (values + mod[2, :, c] * out).astype(BF16)
+        normed = (values - mean[...]) * rstd[...]
+        ng = hg * (1.0 + mod[1, :, c])
+        held[:, c] = ng
+        s1 += jnp.sum(ng, -1, keepdims=True)
+        s2 += jnp.sum(ng * normed, -1, keepdims=True)
+        for r, term in enumerate((hg, hg * normed, up_rows * out)):
+            sums = jnp.sum(term, 0, keepdims=True) * grad_scale
+            for i in range(width // HEAD):
+                row = r * tiles + j * (width // HEAD) + i
+                mod_rows[row : row + 1, :] = sums[:, i * HEAD : (i + 1) * HEAD]
+    m1 = s1 * (1.0 / total)
+    m2 = s2 * (1.0 / total)
+    for j in range(steps):
+        c = slice(j * width, (j + 1) * width)
+        normed = (x[:, c].astype(F32) - mean[...]) * rstd[...]
+        tokens_grad[:, c] = (
+            upstream[:, c].astype(F32) + rstd[...] * (held[:, c] - m1 - normed * m2)
+        ).astype(BF16)
 
 
 def spread(arrived, mod_rows, both):
@@ -297,8 +304,9 @@
     own = width // dp
 
     cols = 4 * n + HEAD
-    packed = call(pack, shape((own, cols), BF16), moved=4 * own * cols)(qkv, out_w.T, down_w.T)
+    packed = call(pack, shape((own, cols), BF16), moved=4 * own * cols, vmem=60)(qkv, out_w.T, down_w.T)
     w = lax.all_gather(packed, "dp", axis=0, tiled=True)
+    w = pltpu.with_memory_space_constraint(w, pltpu.HBM)
     up = lax.all_to_all(
         jnp.broadcast_to(up_w[None], (dp, *up_w.shape)), "dp", 0, 0, tiled=True
     ).reshape(2 * rank, n)
@@ -325,22 +333,23 @@
             shape((m, 2 * n), F32),
             shape((m, 2 * rank), BF16),
         ),
-        grid=(4,),
-        in_specs=[
-            whole(m, width),
-            whole(m, width),
-            pl.BlockSpec((width, n), lambda t: (0, t)),
-            pl.BlockSpec((width, HEAD), lambda t: (0, 4 * n // HEAD)),
-            whole(2 * rank, n),
+        in_specs=[pl.BlockSpec(memory_space=pl.ANY)] * 3 + [pl.BlockSpec(memory_space=pltpu.VMEM)],
+        out_specs=(pl.BlockSpec(memory_space=pltpu.VMEM),) * 3,
+        scratch=[
+            pltpu.VMEM((m, width), BF16),
+            pltpu.VMEM((m, width), BF16),
+            pltpu.VMEM((width, cols), BF16),
+            pltpu.SemaphoreType.DMA((7,)),
         ],
-        out_specs=(
-            pl.BlockSpec((ctx, 1, positions, HEAD), lambda t: (0, t, 0, 0)),
-            whole(m, 2 * n),
-            whole(m, 2 * rank),
-        ),
+        vmem=32,
         flops=2 * m * width * cols,
         moved=2 * width * cols,
-    )(hidden, branch_grad, w, w, up)
+    )(
+        pltpu.with_memory_space_constraint(hidden, pltpu.HBM),
+        pltpu.with_memory_space_constraint(branch_grad, pltpu.HBM),
+        w,
+        up,
+    )
     rows_in = lax.all_to_all(sent, CTX, 0, 0, tiled=True)
 
     back_sent = call(
@@ -365,8 +374,7 @@
     )(back, raw, low, up, hidden_t)
     arrived = lax.all_to_all(sections, "dp", 0, 0, tiled=True)
 
-    per = 2
-    steps, cb = dp // per, per * own
+    steps = dp // 2
     tokens_grad, mixed, mod_rows = call(
         functools.partial(finish, steps, grad_scale),
         (
@@ -374,29 +382,17 @@
             shape((m, width), BF16),
             shape((3 * width // HEAD, HEAD), F32),
         ),
-        grid=(steps,),
-        in_specs=[
-            whole(m, 3 * n),
-            whole(m, 2 * rank),
-            whole(ctx, 4, positions, HEAD),
-            pl.BlockSpec((cb, cols), lambda k: (k, 0)),
-            whole(m, width),
-            whole(m, 1),
-            whole(m, 1),
-            whole(3, 1, width),
-            whole(m, width),
-        ],
-        out_specs=(whole(m, width), whole(m, width), whole(3 * width // HEAD, HEAD)),
+        in_specs=[pl.BlockSpec(memory_space=pltpu.VMEM)] * 8 + [pl.BlockSpec(memory_space=pl.ANY)],
+        out_specs=(pl.BlockSpec(memory_space=pltpu.VMEM),) * 3,
         scratch=[
             pltpu.VMEM((m, width), F32),
-            pltpu.VMEM((3, width), F32),
-            pltpu.VMEM((m, 1), F32),
-            pltpu.VMEM((m, 1), F32),
-            pltpu.VMEM((m, n), BF16),
+            pltpu.VMEM((width, cols), BF16),
+            pltpu.SemaphoreType.DMA((steps,)),
         ],
         flops=2 * m * width * cols,
         moved=2 * width * cols + 8 * m * width,
-    )(joined, low_grad, back, w, x, mean, rstd, mod, upstream)
+        vmem=32,
+    )(joined, low_grad, back, x, mean, rstd, mod, upstream, w)
 
     near, far = lax.axis_size("near"), lax.axis_size("yh") * lax.axis_size("far")
     rows_a, rows_b = own_rows // near, mod_rows.shape[0] // near

time: 262 us -> 253 us (0.966)
  Pallas kernels: 31.8 us -> 21.8 us
  local copies, waits for them, and re-layouts: 2.72 us -> 6.16 us
    unnamed x2 -> x16, local copies, waits for them, and re-layouts: 0.76 us -> 4.8 us
    pallas_call x1, Pallas kernels: 12.5 us -> 8.77 us  [per_device(): call(functools.partial(finish, steps, grad_scale), (shape((m, width), BF1...]
  transfers between devices with their start and end apart: 3 -> 3, of which waited for: 2 -> 1; matrix products, arithmetic and copies ran while one was open for 1% -> 1% of each run, Pallas kernels for 6% -> 4%
where the time goes in v6:
time: 253 us; the launch traced here: 251 us
  blocking collectives  122 us (48%)
  waiting for transfers between devices  75.2 us (30%)
  Pallas kernels  21.8 us (9%)
  between operations  14.1 us (6%)
  starting transfers between devices  11.3 us (4%)
  local copies, waits for them, and re-layouts  6.16 us (2%)
    all_gather x1, waiting for transfers between devices, per_device(): w = lax.all_gather(packed, 'dp', axis=0, tiled=True)  75.2 us
    all_to_all x1, blocking collectives, per_device(): rows_in = lax.all_to_all(sent, CTX, 0, 0, tiled=True)  45.3 us
    all_to_all x1, blocking collectives, per_device(): back = lax.all_to_all(back_sent, CTX, 0, 0, tiled=True)  38.3 us
    all_to_all x1, blocking collectives, per_device(): lax.all_to_all(part, ('yh', 'far'), 0, 0, tiled=True)  19.8 us
    all_to_all x1, blocking collectives, per_device(): lax.all_to_all(both, 'near', 0, 0, tiled=True)  9.68 us
    all_to_all x1, blocking collectives, per_device(): lax.all_to_all(part, 'near', 0, 0, tiled=True)  9.02 us
    pallas_call x1, Pallas kernels, per_device(): call(functools.partial(finish, steps, grad_scale), (shape((m, width), BF1...  8.77 us
    pallas_call x1, Pallas kernels, per_device(): call(functools.partial(projections, rank), (shape((ctx, 4, positions, HEA...  6.06 us
  transfers between devices with their start and end apart: 3, of which 1 were waited for; matrix products, arithmetic and copies ran while one was open for 1% of the time, Pallas kernels for 4%

profile of v6, /device:TPU:24, one launch (start us, length us, event | category | flops | bytes accessed | tf_op | source)
XLA Modules:
  0.0 250.5 jit_solution(7554789190833473629)
XLA Ops:
  7.2 0.0 copy-start.3
  7.2 0.0 copy-start.7
  7.2 0.0 copy-start.1
  7.2 0.0 all-gather.2.cloned.1.call-start
  7.2 2.3 shard_map.111
  9.5 0.0 all-gather.2.cloned.1.call-update
  9.5 1.3 broadcast_in_dim.2
  10.9 5.8 %all-to-all-start = ((bf16[16,4,512]{2,1,0:T(4,128)(2,1)}), bf16[16,4,512]{2,1,0:T(4,128)(2,1)S(1)}, u32[]{:S(2)}, u32[]{:S(2)}) async-start(bf16[16,4,512]{2,1,0:T(4,128)(2,1)} %broadcast_in_dim.2), calls=%async_computation | async-start | bytes 131072 | tf_op jit(solution)/shard_map/all_to_all | solution.py:310
  16.7 1.1 copy-done
  17.8 1.1 copy-done.2
  18.9 0.8 copy-done.6
  19.7 1.0 shard_map.110
  20.7 0.0 copy-start.4
  20.7 0.9 copy-done.4
  21.6 0.9 copy-done.5
  22.4 0.0 all-to-all-done
  22.5 75.2 %all-gather.2.cloned.1.call-done.w_at = bf16[3072,2176]{1,0:T(8,128)(2,1)} async-done(((bf16[192,2176]{1,0:T(8,128)(2,1)}), bf16[3072,2176]{1,0:T(8,128)(2,1)}) %all-gather.2.cloned.1.call-update) | async-done | bytes 13369360 | tf_op jit(solution)/shard_map/all_gather | solution.py:308
  97.6 6.1 %shard_map.112 = (bf16[32,4,16,128]{3,2,1,0:T(8,128)(2,1)S(1)}, f32[128,1024]{1,0:T(8,128)S(1)}, bf16[128,64]{1,0:T(8,128)(2,1)S(1)}) custom-call(bf16[128,3072]{1,0:T(8,128)(2,1)} %copy-done.4, bf16[128,3072]{1,0:T(8,128)(2,1)} %copy-done.5, bf16[3072,2176]{1,0:T(8,128)(2,1)} %all-gather.2.cloned.1.call-done.w_at, bf16[64,512]{1,0:T(8,128)(2,1)S(1)} %reshape.31.up), custom_call_target="tpu_custom_call" | custom-call | flops 1711276032 | bytes 13369344 | tf_op jit(solution)/shard_map/pallas_call | solution.py:329
  103.7 45.3 %all_to_all.35.rows_in = bf16[32,4,16,128]{3,2,1,0:T(8,128)(2,1)S(1)} all-to-all(bf16[32,4,16,128]{3,2,1,0:T(8,128)(2,1)S(1)} %get-tuple-element.24), channel_id=1, replica_groups=mesh['dp'=16,'yh'=2,'far'=4,'near'=4] {'yh','far','near'}, dimensions={0} | all-to-all | bytes 1048576 | tf_op jit(solution)/shard_map/all_to_all | solution.py:353
  149.0 1.2 shard_map.113
  150.2 38.3 %all_to_all.36.back = bf16[32,4,16,128]{3,2,1,0:T(8,128)(2,1)S(1)} all-to-all(bf16[32,4,16,128]{3,2,1,0:T(8,128)(2,1)S(1)} %shard_map.113), channel_id=1, replica_groups=mesh['dp'=16,'yh'=2,'far'=4,'near'=4] {'yh','far','near'}, dimensions={0} | all-to-all | bytes 1048576 | tf_op jit(solution)/shard_map/all_to_all | solution.py:362
  188.4 1.6 shard_map.114
  190.0 5.4 %all-to-all-start.3 = ((bf16[16,112,128]{2,1,0:T(8,128)(2,1)}), bf16[16,112,128]{2,1,0:T(8,128)(2,1)S(1)}, u32[]{:S(2)}, u32[]{:S(2)}) async-start(bf16[16,112,128]{2,1,0:T(8,128)(2,1)} %get-tuple-element.34), calls=%async_computation.3 | async-start | bytes 917504 | tf_op jit(solution)/shard_map/all_to_all | solution.py:375
  195.5 0.0 copy-done.3
  195.5 0.0 copy-done.7
  195.5 8.8 %shard_map.115 = (bf16[128,3072]{1,0:T(8,128)(2,1)}, bf16[128,3072]{1,0:T(8,128)(2,1)}, f32[72,128]{1,0:T(8,128)S(1)}) custom-call(bf16[128,1536]{1,0:T(8,128)(2,1)S(1)} %get-tuple-element.28.joined, bf16[128,64]{1,0:T(8,128)(2,1)S(1)} %get-tuple-element.29.low_grad, bf16[32,4,16,128]{3,2,1,0:T(8,128)(2,1)S(1)} %all_to_all.36.back, ...), custom_call_target="tpu_custom_call" | custom-call | flops 1711276032 | bytes 16515072 | tf_op jit(solution)/shard_map/pallas_call | solution.py:378
  204.3 0.0 all-to-all-done.3.arrived
  204.3 0.1 shard_map.116
  204.4 9.7 %all_to_all.37.arrived = bf16[4,48,128]{2,1,0:T(8,128)(2,1)S(1)} all-to-all(bf16[4,48,128]{2,1,0:T(8,128)(2,1)S(1)} %shard_map.116), channel_id=1, replica_groups=mesh['dp'=16,'yh'=2,'far'=4,'near'=4] {'near'}, dimensions={0} | all-to-all | bytes 98304 | tf_op jit(solution)/shard_map/all_to_all | solution.py:402
  214.1 19.8 %all_to_all.38.arrived = bf16[8,48,128]{2,1,0:T(8,128)(2,1)S(1)} all-to-all(bf16[8,48,128]{2,1,0:T(8,128)(2,1)S(1)} %shard_map.117), channel_id=1, replica_groups=mesh['dp'=16,'yh'=2,'far'=4,'near'=4] {'yh','far'}, dimensions={0} | all-to-all | bytes 196608 | tf_op jit(solution)/shard_map/all_to_all | solution.py:405
  233.9 9.0 %all_to_all.39.shares = bf16[4,48,128]{2,1,0:T(8,128)(2,1)S(1)} all-to-all(bf16[4,48,128]{2,1,0:T(8,128)(2,1)S(1)} %shard_map.118), channel_id=1, replica_groups=mesh['dp'=16,'yh'=2,'far'=4,'near'=4] {'near'}, dimensions={0} | all-to-all | bytes 98304 | tf_op jit(solution)/shard_map/all_to_all | solution.py:416
  242.9 0.8 shard_map.119
  (8 shorter events, 0.1 us)
Async XLA Ops:
  7.2 188.3 %copy-start.3 = (bf16[1,1,128,3072]{3,2,1,0:T(8,128)(2,1)S(1)}, bf16[1,1,128,3072]{3,2,1,0:T(8,128)(2,1)}, u32[]{:S(2)}) copy-start(bf16[1,1,128,3072]{3,2,1,0:T(8,128)(2,1)} %param.13) | copy-start | bytes 2359300
  7.2 188.3 %copy-start.7 = (f32[1,3,3072]{2,0,1:T(1,128)S(1)}, f32[1,3,3072]{2,0,1:T(1,128)}, u32[]{:S(2)}) copy-start(f32[1,3,3072]{2,0,1:T(1,128)} %param.8) | copy-start | bytes 110596
  7.2 188.3 %copy-start.1 = (bf16[1,1,128,3072]{3,2,1,0:T(8,128)(2,1)S(1)}, bf16[1,1,128,3072]{3,2,1,0:T(8,128)(2,1)}, u32[]{:S(2)}) copy-start(bf16[1,1,128,3072]{3,2,1,0:T(8,128)(2,1)} %param.7) | copy-start | bytes 2359300
  7.2 90.4 %all-gather.2.cloned.1.call-start = ((), (), s32[]{:S(2)}) async-start(), calls=%async_computation.7 | async-start | bytes 14204928 | tf_op jit(solution)/shard_map/all_gather | solution.py:308
  10.9 11.6 %all-to-all-start = ((bf16[16,4,512]{2,1,0:T(4,128)(2,1)}), bf16[16,4,512]{2,1,0:T(4,128)(2,1)S(1)}, u32[]{:S(2)}, u32[]{:S(2)}) async-start(bf16[16,4,512]{2,1,0:T(4,128)(2,1)} %broadcast_in_dim.2), calls=%async_computation | async-start | bytes 131072 | tf_op jit(solution)/shard_map/all_to_all | solution.py:310
  16.7 1.1 copy-start
  17.8 1.1 copy-start.2
  18.9 0.8 copy-start.6
  20.7 0.9 copy-start.4
  21.6 0.9 copy-start.5
  190.0 14.2 %all-to-all-start.3 = ((bf16[16,112,128]{2,1,0:T(8,128)(2,1)}), bf16[16,112,128]{2,1,0:T(8,128)(2,1)S(1)}, u32[]{:S(2)}, u32[]{:S(2)}) async-start(bf16[16,112,128]{2,1,0:T(8,128)(2,1)} %get-tuple-element.34), calls=%async_computation.3 | async-start | bytes 917504 | tf_op jit(solution)/shard_map/all_to_all | solution.py:375
Sparse Core Ops, SparseCore 0:
  10.2 87.3 all-gather.1

commit v7 on v6

--- a/solution.py
+++ b/solution.py
@@ -71,12 +71,47 @@
     branch_grad[...] = (upstream[...].astype(F32) * mod[2]).astype(BF16)
 
 
-def pack(qkv, out_t, down_t, packed):
-    n, k = out_t.shape[1], qkv.shape[1]
-    packed[:, :k] = qkv[...]
-    packed[:, k : k + n] = out_t[...]
+def pack(qkv, out_t, packed, sems):
+    k, n = qkv.shape[1], out_t.shape[1]
+    copies = [
+        pltpu.make_async_copy(qkv, packed.at[:, pl.ds(0, k)], sems.at[0]),
+        pltpu.make_async_copy(out_t, packed.at[:, pl.ds(k, n)], sems.at[1]),
+    ]
+    for copy in copies:
+        copy.start()
+    for copy in copies:
+        copy.wait()
+
+
+def pack_maps(down_t, up, copies):
+    half = down_t.shape[1] // 2
     down = down_t[...].astype(F32).T
-    packed[:, k + n :] = jnp.concatenate([down, jnp.zeros_like(down)], 1).astype(BF16)
+    both = jnp.concatenate([down[:half], down[half:]], 1).astype(BF16)
+    rows = up.shape[0]
+    values = up[...].astype(F32)
+    ups = jnp.concatenate(
+        [values[:, h * HEAD : (h + 1) * HEAD] for h in range(up.shape[1] // HEAD)], 0
+    ).astype(BF16)
+    for d in range(copies.shape[0]):
+        copies[d, :half] = both
+        copies[d, half:] = ups
+
+
+def unpack_maps(maps, down, up):
+    parts = maps.shape[0]
+    cols, n = up.shape
+    half = down.shape[0] // parts // 2
+    own = cols // parts
+    for d in range(parts):
+        both = maps[d, :half].astype(F32)
+        at = 2 * half * d
+        down[at : at + half, :] = both[:, :cols].astype(BF16)
+        down[at + half : at + 2 * half, :] = both[:, cols:].astype(BF16)
+        rows = maps[d, half:].astype(F32)
+        for h in range(n // HEAD):
+            up[d * own : (d + 1) * own, h * HEAD : (h + 1) * HEAD] = rows[
+                h * own : (h + 1) * own
+            ]
 
 
 def head_scales(x):
@@ -87,7 +122,9 @@
     return parts
 
 
-def projections(rank, hidden_at, branch_at, w_at, up, sent, raw, low_out, hidden, branch, w, sems):
+def projections(
+    hidden_at, branch_at, w_at, down_at, up, sent, raw, low_out, hidden, branch, w, w_down, sems
+):
     n = up.shape[1]
     heads = n // HEAD
     positions = sent.shape[2]
@@ -100,9 +137,9 @@
         return fetch(w_at.at[:, at], w.at[:, at], i)
 
     blocks = [columns(i, i * n, n) for i in range(4)]
-    down = columns(4, 4 * n, HEAD)
-    rows = fetch(hidden_at, hidden, 5)
-    grads = fetch(branch_at, branch, 6)
+    rows = fetch(hidden_at, hidden, 4)
+    grads = fetch(branch_at, branch, 5)
+    down = fetch(down_at, w_down, 6)
     for copy in (rows, down, *blocks[:3], grads, blocks[3]):
         copy.start()
 
@@ -116,10 +153,10 @@
             for g in range(x.shape[0] // positions):
                 sent[g * heads + h, t] = part[g * positions : (g + 1) * positions]
 
-    up_q, up_v = split_up(up[...], rank)
+    up_q, up_v = split_up(up[...], up.shape[0] // 2)
     rows.wait()
     down.wait()
-    low = dot(hidden[...], w[:, 4 * n :])[:, : 2 * rank].astype(BF16)
+    low = dot(hidden[...], w_down[...]).astype(BF16)
     low_out[...] = low
     blocks[0].wait()
     q = dot(hidden[...], w[:, :n]) + dot(low, up_q)
@@ -209,8 +246,8 @@
 
 
 def finish(
-    steps, grad_scale, joined, low_grad, back, x, mean, rstd, mod, upstream, w_at,
-    tokens_grad, mixed, mod_rows, held, w, sems,
+    steps, grad_scale, joined, low_grad, back, x, mean, rstd, mod, upstream, w_at, down_at,
+    tokens_grad, mixed, mod_rows, held, w, w_down, sems,
 ):
     width = x.shape[1] // steps
     total = x.shape[1]
@@ -222,13 +259,17 @@
         at = pl.ds(j * width, width)
         copies.append(pltpu.make_async_copy(w_at.at[at], w.at[at], sems.at[j]))
         copies[j].start()
+    down = pltpu.make_async_copy(down_at, w_down, sems.at[steps])
+    down.start()
     attended = unpack_blocks(back, 3, n3 // 3 // HEAD)
     s1 = jnp.zeros((x.shape[0], 1), F32)
     s2 = jnp.zeros((x.shape[0], 1), F32)
     for j in range(steps):
         c = slice(j * width, (j + 1) * width)
         copies[j].wait()
-        hg = dot(joined[...], w[c, :n3], NT) + dot(low_grad[...], w[c, n4 : n4 + low_grad.shape[1]], NT)
+        if j == 0:
+            down.wait()
+        hg = dot(joined[...], w[c, :n3], NT) + dot(low_grad[...], w_down[c], NT)
         out = dot(attended, w[c, n3:n4], NT)
         values = x[:, c].astype(F32)
         up_rows = upstream[:, c].astype(F32)
@@ -253,43 +294,33 @@
         ).astype(BF16)
 
 
-def spread(arrived, mod_rows, both):
+def spread(arrived, mod_rows, copies):
     share = jnp.sum(arrived[...].astype(F32), 0).astype(BF16)
     rows = mod_rows[...].astype(BF16)
-    parts = both.shape[0]
-    rows_a, rows_b = share.shape[0] // parts, rows.shape[0] // parts
-    pad = jnp.zeros((both.shape[1] - rows_a - rows_b, HEAD), F32)
-    for j in range(parts):
-        piece = jnp.concatenate(
-            [
-                share[j * rows_a : (j + 1) * rows_a].astype(F32),
-                rows[j * rows_b : (j + 1) * rows_b].astype(F32),
-                pad,
-            ],
-            0,
-        )
-        both[j] = piece.astype(BF16)
-
-
-def summed(arrived, out):
+    for j in range(copies.shape[0]):
+        copies[j, : share.shape[0]] = share
+        copies[j, share.shape[0] :] = rows
+
+
+def summed(arrived, copies):
     total = jnp.sum(arrived[...].astype(F32), 0).astype(BF16)
-    out[...] = jnp.broadcast_to(total[None], out.shape)
-
-
-def collected(rows_a, rows_b, shares, down_t, up_grad, mod_grad):
-    values = shares[...].astype(F32)
-    parts = values.shape[0]
-    cols = down_t.shape[0]
-    own = up_grad.shape[0]
+    copies[...] = jnp.broadcast_to(total[None], copies.shape)
+
+
+def collected(arrived, down_t, up_grad, mod_grad):
+    total = jnp.sum(arrived[...].astype(F32), 0)
+    cols, own = down_t.shape[0], up_grad.shape[0]
     half = down_t.shape[1] // 2
-    a = jnp.concatenate([values[j, :rows_a] for j in range(parts)], 0)
-    b = jnp.concatenate([values[j, rows_a : rows_a + rows_b] for j in range(parts)], 0)
-    down_t[...] = jnp.concatenate([a[:half, :cols], a[:half, cols:]], 0).T
-    for h in range(up_grad.shape[1] // HEAD):
-        up_grad[:, h * HEAD : (h + 1) * HEAD] = a[half + h * own : half + (h + 1) * own]
+    down_t[...] = jnp.concatenate([total[:half, :cols], total[:half, cols:]], 0).T
+    heads = up_grad.shape[1] // HEAD
+    for h in range(heads):
+        up_grad[:, h * HEAD : (h + 1) * HEAD] = total[half + h * own : half + (h + 1) * own]
     tiles = mod_grad.shape[2] // HEAD
+    first = half + heads * own
     for i in range(3 * tiles):
-        mod_grad[i // tiles, :, (i % tiles) * HEAD : (i % tiles + 1) * HEAD] = b[i : i + 1]
+        mod_grad[i // tiles, :, (i % tiles) * HEAD : (i % tiles + 1) * HEAD] = total[
+            first + i : first + i + 1
+        ]
 
 
 def per_device(tokens, modulation, qkv, out_w, down_w, up_w, output_gradient):
@@ -303,13 +334,25 @@
     grad_scale = (dp * ctx * m) ** (-0.5)
     own = width // dp
 
-    cols = 4 * n + HEAD
-    packed = call(pack, shape((own, cols), BF16), moved=4 * own * cols, vmem=60)(qkv, out_w.T, down_w.T)
+    cols = 4 * n
+    packed = call(
+        pack,
+        shape((own, cols), BF16),
+        in_specs=[pl.BlockSpec(memory_space=pl.ANY)] * 2,
+        out_specs=pl.BlockSpec(memory_space=pl.ANY),
+        scratch=[pltpu.SemaphoreType.DMA((2,))],
+        moved=4 * own * cols,
+        vmem=60,
+    )(qkv, out_w.T)
     w = lax.all_gather(packed, "dp", axis=0, tiled=True)
     w = pltpu.with_memory_space_constraint(w, pltpu.HBM)
-    up = lax.all_to_all(
-        jnp.broadcast_to(up_w[None], (dp, *up_w.shape)), "dp", 0, 0, tiled=True
-    ).reshape(2 * rank, n)
+    own_rows = own // 2 + (2 * rank // dp) * heads
+    maps = call(pack_maps, shape((dp, own_rows, HEAD), BF16), moved=2**19)(down_w.T, up_w)
+    w_down, up = call(
+        unpack_maps, (shape((width, 2 * rank), BF16), shape((2 * rank, n), F32)), moved=2**21
+    )(lax.all_to_all(maps, "dp", 0, 0, tiled=True))
+    w_down = pltpu.with_memory_space_constraint(w_down, pltpu.HBM)
+    up = up.astype(BF16)
 
     x = tokens.reshape(m, width)
     upstream = output_gradient.reshape(m, width)
@@ -327,18 +370,19 @@
     )(x, mod, upstream)
 
     sent, raw, low = call(
-        functools.partial(projections, rank),
+        projections,
         (
             shape((ctx, 4, positions, HEAD), BF16),
             shape((m, 2 * n), F32),
             shape((m, 2 * rank), BF16),
         ),
-        in_specs=[pl.BlockSpec(memory_space=pl.ANY)] * 3 + [pl.BlockSpec(memory_space=pltpu.VMEM)],
+        in_specs=[pl.BlockSpec(memory_space=pl.ANY)] * 4 + [pl.BlockSpec(memory_space=pltpu.VMEM)],
         out_specs=(pl.BlockSpec(memory_space=pltpu.VMEM),) * 3,
         scratch=[
             pltpu.VMEM((m, width), BF16),
             pltpu.VMEM((m, width), BF16),
             pltpu.VMEM((width, cols), BF16),
+            pltpu.VMEM((width, 2 * rank), BF16),
             pltpu.SemaphoreType.DMA((7,)),
         ],
         vmem=32,
@@ -348,6 +392,7 @@
         pltpu.with_memory_space_constraint(hidden, pltpu.HBM),
         pltpu.with_memory_space_constraint(branch_grad, pltpu.HBM),
         w,
+        w_down,
         up,
     )
     rows_in = lax.all_to_all(sent, CTX, 0, 0, tiled=True)
@@ -361,7 +406,6 @@
     )(rows_in)
     back = lax.all_to_all(back_sent, CTX, 0, 0, tiled=True)
 
-    own_rows = own // 2 + (2 * rank // dp) * heads
     joined, low_grad, sections = call(
         functools.partial(adapter_terms, rank, grad_scale),
         (
@@ -382,38 +426,35 @@
             shape((m, width), BF16),
             shape((3 * width // HEAD, HEAD), F32),
         ),
-        in_specs=[pl.BlockSpec(memory_space=pltpu.VMEM)] * 8 + [pl.BlockSpec(memory_space=pl.ANY)],
+        in_specs=[pl.BlockSpec(memory_space=pltpu.VMEM)] * 8 + [pl.BlockSpec(memory_space=pl.ANY)] * 2,
         out_specs=(pl.BlockSpec(memory_space=pltpu.VMEM),) * 3,
         scratch=[
             pltpu.VMEM((m, width), F32),
             pltpu.VMEM((width, cols), BF16),
-            pltpu.SemaphoreType.DMA((steps,)),
+            pltpu.VMEM((width, 2 * rank), BF16),
+            pltpu.SemaphoreType.DMA((steps + 1,)),
         ],
         flops=2 * m * width * cols,
         moved=2 * width * cols + 8 * m * width,
         vmem=32,
-    )(joined, low_grad, back, x, mean, rstd, mod, upstream, w)
+    )(joined, low_grad, back, x, mean, rstd, mod, upstream, w, w_down)
 
     near, far = lax.axis_size("near"), lax.axis_size("yh") * lax.axis_size("far")
-    rows_a, rows_b = own_rows // near, mod_rows.shape[0] // near
-    rows = 16 * -(-(rows_a + rows_b) // 16)
-    both = call(spread, shape((near, rows, HEAD), BF16), moved=2**19, vmem=8)(arrived, mod_rows)
-    part = call(summed, shape((far, rows, HEAD), BF16), moved=2**17, vmem=8)(
-        lax.all_to_all(both, "near", 0, 0, tiled=True)
-    )
-    part = call(summed, shape((near, rows, HEAD), BF16), moved=2**17, vmem=8)(
-        lax.all_to_all(part, ("yh", "far"), 0, 0, tiled=True)
+    rows = own_rows + mod_rows.shape[0]
+    part = call(spread, shape((near, rows, HEAD), BF16), moved=2**19, vmem=8)(arrived, mod_rows)
+    part = call(summed, shape((far, rows, HEAD), BF16), moved=2**19, vmem=8)(
+        lax.all_to_all(part, "near", 0, 0, tiled=True)
     )
     down_t, up_grad, mod_grad = call(
-        functools.partial(collected, rows_a, rows_b),
+        collected,
         (
             shape((2 * rank, own), F32),
             shape((2 * rank // dp, n), F32),
             shape((3, 1, width), F32),
         ),
-        moved=2**18,
+        moved=2**19,
         vmem=8,
-    )(lax.all_to_all(part, "near", 0, 0, tiled=True))
+    )(lax.all_to_all(part, ("yh", "far"), 0, 0, tiled=True))
     return (
         mixed.reshape(tokens.shape),
         tokens_grad.reshape(tokens.shape),

time: 253 us -> 279 us (1.10)
  the two profiles are of different devices: /device:TPU:24 before, /device:TPU:32 now
where the time goes in v7:
time: 279 us
  blocking collectives  130 us (47%)
  waiting for transfers between devices  68.9 us (25%)
  Pallas kernels  49 us (18%)
  between operations  14.2 us (5%)
  starting transfers between devices  9.69 us (3%)
  local copies, waits for them, and re-layouts  7.24 us (3%)
    all_gather x1, waiting for transfers between devices, per_device(): w = lax.all_gather(packed, 'dp', axis=0, tiled=True)  64.5 us
    all_to_all x1, blocking collectives, per_device(): rows_in = lax.all_to_all(sent, CTX, 0, 0, tiled=True)  49.2 us
    all_to_all x1, blocking collectives, per_device(): back = lax.all_to_all(back_sent, CTX, 0, 0, tiled=True)  37.4 us
    all_to_all x1, blocking collectives, per_device(): lax.all_to_all(part, ('yh', 'far'), 0, 0, tiled=True)  33.5 us
    pallas_call x1, Pallas kernels, per_device(): call(pack, shape((own, cols), BF16), in_specs=[pl.BlockSpec(memory_space=...  24.9 us
    pallas_call x1, Pallas kernels, per_device(): call(functools.partial(finish, steps, grad_scale), (shape((m, width), BF1...  12.1 us
    all_to_all x1, blocking collectives, per_device(): lax.all_to_all(part, 'near', 0, 0, tiled=True)  9.55 us
    unnamed x22, local copies, waits for them, and re-layouts  7.24 us
  transfers between devices with their start and end apart: 3, of which 2 were waited for; matrix products, arithmetic and copies ran while one was open for 0% of the time, Pallas kernels for 5%

profile of v7, /device:TPU:32, one launch (start us, length us, event | category | flops | bytes accessed | tf_op | source)
XLA Modules:
  0.0 278.7 jit_solution(7501060038971020804)
XLA Ops:
  7.2 0.0 all-gather.2.cloned.1.call-start
  7.2 24.9 %shard_map.111 = bf16[192,2048]{1,0:T(8,128)(2,1)} custom-call(bf16[192,1536]{1,0:T(8,128)(2,1)} %qkv.1, bf16[192,512]{1,0:T(8,128)(2,1)} %bitcast.16), custom_call_target="tpu_custom_call" | custom-call | bytes 1572864 | tf_op jit(solution)/shard_map/pallas_call | solution.py:338
  32.2 0.0 copy-start.2
  32.2 0.0 copy-start.8
  32.2 0.0 all-gather.2.cloned.1.call-update
  32.2 0.0 copy-start.9
  32.2 0.9 copy-done.9
  33.1 0.7 copy-done.10
  33.8 0.9 shard_map.112
  34.7 5.4 %all-to-all-start = ((bf16[16,112,128]{2,1,0:T(8,128)(2,1)}), bf16[16,112,128]{2,1,0:T(8,128)(2,1)S(1)}, u32[]{:S(2)}, u32[]{:S(2)}) async-start(bf16[16,112,128]{2,1,0:T(8,128)(2,1)} %shard_map.112), calls=%async_computation | async-start | bytes 917504 | tf_op jit(solution)/shard_map/all_to_all | solution.py:353
  40.1 0.0 copy-start.1
  40.2 1.1 copy-done.1
  41.3 1.1 copy-done.3
  42.4 0.8 copy-done.7
  43.2 1.0 shard_map.110
  44.2 0.9 copy-done.5
  45.0 0.9 copy-done.6
  45.9 4.4 %all-to-all-done.maps = bf16[16,112,128]{2,1,0:T(8,128)(2,1)S(1)} async-done(((bf16[16,112,128]{2,1,0:T(8,128)(2,1)}), bf16[16,112,128]{2,1,0:T(8,128)(2,1)S(1)}, u32[]{:S(2)}, u32[]{:S(2)}) %all-to-all-start) | async-done | bytes 458784 | tf_op jit(solution)/shard_map/all_to_all | solution.py:353
  50.3 0.3 shard_map.113
  50.6 0.9 copy-done
  51.5 64.5 %all-gather.2.cloned.1.call-done.w_at = bf16[3072,2048]{1,0:T(8,128)(2,1)} async-done(((bf16[192,2048]{1,0:T(8,128)(2,1)}), bf16[3072,2048]{1,0:T(8,128)(2,1)}) %all-gather.2.cloned.1.call-update) | async-done | bytes 12582928 | tf_op jit(solution)/shard_map/all_gather | solution.py:347
  116.0 6.0 %shard_map.114 = (bf16[32,4,16,128]{3,2,1,0:T(8,128)(2,1)S(1)}, f32[128,1024]{1,0:T(8,128)S(1)}, bf16[128,64]{1,0:T(8,128)(2,1)S(1)}) custom-call(bf16[128,3072]{1,0:T(8,128)(2,1)} %copy-done.5, bf16[128,3072]{1,0:T(8,128)(2,1)} %copy-done.6, bf16[3072,2048]{1,0:T(8,128)(2,1)} %all-gather.2.cloned.1.call-done.w_at, bf16[3072,64]{1,0:T(8,128)(2,1)} %copy-done, ...), custom_call_target="tpu_custom_call" | custom-call | flops 1610612736 | bytes 12582912 | tf_op jit(solution)/shard_map/pallas_call | solution.py:372
  122.1 49.2 %all_to_all.30.rows_in = bf16[32,4,16,128]{3,2,1,0:T(8,128)(2,1)S(1)} all-to-all(bf16[32,4,16,128]{3,2,1,0:T(8,128)(2,1)S(1)} %get-tuple-element.28), channel_id=1, replica_groups=mesh['dp'=16,'yh'=2,'far'=4,'near'=4] {'yh','far','near'}, dimensions={0} | all-to-all | bytes 1048576 | tf_op jit(solution)/shard_map/all_to_all | solution.py:398
  171.3 1.2 shard_map.115
  172.5 37.4 %all_to_all.31.back = bf16[32,4,16,128]{3,2,1,0:T(8,128)(2,1)S(1)} all-to-all(bf16[32,4,16,128]{3,2,1,0:T(8,128)(2,1)S(1)} %shard_map.115), channel_id=1, replica_groups=mesh['dp'=16,'yh'=2,'far'=4,'near'=4] {'yh','far','near'}, dimensions={0} | all-to-all | bytes 1048576 | tf_op jit(solution)/shard_map/all_to_all | solution.py:407
  209.9 1.7 shard_map.116
  211.6 4.2 %all-to-all-start.3 = ((bf16[16,112,128]{2,1,0:T(8,128)(2,1)}), bf16[16,112,128]{2,1,0:T(8,128)(2,1)S(1)}, u32[]{:S(2)}, u32[]{:S(2)}) async-start(bf16[16,112,128]{2,1,0:T(8,128)(2,1)} %get-tuple-element.38), calls=%async_computation.3 | async-start | bytes 917504 | tf_op jit(solution)/shard_map/all_to_all | solution.py:419
  215.9 12.1 %shard_map.117 = (bf16[128,3072]{1,0:T(8,128)(2,1)}, bf16[128,3072]{1,0:T(8,128)(2,1)}, f32[72,128]{1,0:T(8,128)S(1)}) custom-call(bf16[128,1536]{1,0:T(8,128)(2,1)S(1)} %get-tuple-element.32.joined, bf16[128,64]{1,0:T(8,128)(2,1)S(1)} %get-tuple-element.33.low_grad, bf16[32,4,16,128]{3,2,1,0:T(8,128)(2,1)S(1)} %all_to_all.31.back, ...), custom_call_target="tpu_custom_call" | custom-call | flops 1610612736 | bytes 15728640 | tf_op jit(solution)/shard_map/pallas_call | solution.py:422
  228.0 0.1 shard_map.118
  228.0 9.5 %all_to_all.32.arrived = bf16[4,184,128]{2,1,0:T(8,128)(2,1)S(1)} all-to-all(bf16[4,184,128]{2,1,0:T(8,128)(2,1)S(1)} %shard_map.118), channel_id=1, replica_groups=mesh['dp'=16,'yh'=2,'far'=4,'near'=4] {'near'}, dimensions={0} | all-to-all | bytes 376832 | tf_op jit(solution)/shard_map/all_to_all | solution.py:446
  237.6 33.5 %all_to_all.33.arrived = bf16[8,184,128]{2,1,0:T(8,128)(2,1)S(1)} all-to-all(bf16[8,184,128]{2,1,0:T(8,128)(2,1)S(1)} %shard_map.119), channel_id=1, replica_groups=mesh['dp'=16,'yh'=2,'far'=4,'near'=4] {'yh','far'}, dimensions={0} | all-to-all | bytes 753664 | tf_op jit(solution)/shard_map/all_to_all | solution.py:457
  271.1 0.8 shard_map.120
  (13 shorter events, 0.1 us)
Async XLA Ops:
  7.2 108.8 %all-gather.2.cloned.1.call-start = ((), (), s32[]{:S(2)}) async-start(), calls=%async_computation.6 | async-start | bytes 13369344 | tf_op jit(solution)/shard_map/all_gather | solution.py:347
  32.2 183.7 %copy-start.2 = (bf16[1,1,128,3072]{3,2,1,0:T(8,128)(2,1)S(1)}, bf16[1,1,128,3072]{3,2,1,0:T(8,128)(2,1)}, u32[]{:S(2)}) copy-start(bf16[1,1,128,3072]{3,2,1,0:T(8,128)(2,1)} %param.7) | copy-start | bytes 2359300
  32.2 183.7 %copy-start.4 = (bf16[1,1,128,3072]{3,2,1,0:T(8,128)(2,1)S(1)}, bf16[1,1,128,3072]{3,2,1,0:T(8,128)(2,1)}, u32[]{:S(2)}) copy-start(bf16[1,1,128,3072]{3,2,1,0:T(8,128)(2,1)} %param.13) | copy-start | bytes 2359300
  32.2 183.7 %copy-start.8 = (f32[1,3,3072]{2,0,1:T(1,128)S(1)}, f32[1,3,3072]{2,0,1:T(1,128)}, u32[]{:S(2)}) copy-start(f32[1,3,3072]{2,0,1:T(1,128)} %param.8) | copy-start | bytes 110596
  32.2 0.9 copy-start.9
  33.1 0.7 copy-start.10
  34.7 15.6 %all-to-all-start = ((bf16[16,112,128]{2,1,0:T(8,128)(2,1)}), bf16[16,112,128]{2,1,0:T(8,128)(2,1)S(1)}, u32[]{:S(2)}, u32[]{:S(2)}) async-start(bf16[16,112,128]{2,1,0:T(8,128)(2,1)} %shard_map.112), calls=%async_computation | async-start | bytes 917504 | tf_op jit(solution)/shard_map/all_to_all | solution.py:353
  40.1 1.1 copy-start.1
  41.3 1.1 copy-start.3
  42.4 0.8 copy-start.7
  44.2 0.9 copy-start.5
  45.0 0.9 copy-start.6
  50.6 0.9 copy-start
  211.6 16.4 %all-to-all-start.3 = ((bf16[16,112,128]{2,1,0:T(8,128)(2,1)}), bf16[16,112,128]{2,1,0:T(8,128)(2,1)S(1)}, u32[]{:S(2)}, u32[]{:S(2)}) async-start(bf16[16,112,128]{2,1,0:T(8,128)(2,1)} %get-tuple-element.38), calls=%async_computation.3 | async-start | bytes 917504 | tf_op jit(solution)/shard_map/all_to_all | solution.py:419
Sparse Core Ops, SparseCore 0:
  32.3 83.6 all-gather.1

commit v8 on v7

--- a/solution.py
+++ b/solution.py
@@ -254,13 +254,13 @@
     n3 = joined.shape[1]
     n4 = n3 + n3 // 3
     tiles = total // HEAD
+    down = pltpu.make_async_copy(down_at, w_down, sems.at[steps])
+    down.start()
     copies = []
     for j in range(steps):
         at = pl.ds(j * width, width)
         copies.append(pltpu.make_async_copy(w_at.at[at], w.at[at], sems.at[j]))
         copies[j].start()
-    down = pltpu.make_async_copy(down_at, w_down, sems.at[steps])
-    down.start()
     attended = unpack_blocks(back, 3, n3 // 3 // HEAD)
     s1 = jnp.zeros((x.shape[0], 1), F32)
     s2 = jnp.zeros((x.shape[0], 1), F32)
@@ -339,7 +339,7 @@
         pack,
         shape((own, cols), BF16),
         in_specs=[pl.BlockSpec(memory_space=pl.ANY)] * 2,
-        out_specs=pl.BlockSpec(memory_space=pl.ANY),
+        out_specs=pl.BlockSpec(memory_space=pltpu.VMEM),
         scratch=[pltpu.SemaphoreType.DMA((2,))],
         moved=4 * own * cols,
         vmem=60,

time: 279 us -> 254 us (0.910)
  the two profiles are of different devices: /device:TPU:32 before, /device:TPU:34 now
where the time goes in v8:
time: 254 us; the launch traced here: 253 us
  blocking collectives  129 us (51%)
  waiting for transfers between devices  69 us (27%)
  Pallas kernels  23 us (9%)
  between operations  14.2 us (6%)
  starting transfers between devices  10.6 us (4%)
  local copies, waits for them, and re-layouts  7.24 us (3%)
    all_gather x1, waiting for transfers between devices, per_device(): w = lax.all_gather(packed, 'dp', axis=0, tiled=True)  67.7 us
    all_to_all x1, blocking collectives, per_device(): rows_in = lax.all_to_all(sent, CTX, 0, 0, tiled=True)  49.4 us
    all_to_all x1, blocking collectives, per_device(): back = lax.all_to_all(back_sent, CTX, 0, 0, tiled=True)  37.4 us
    all_to_all x1, blocking collectives, per_device(): lax.all_to_all(part, ('yh', 'far'), 0, 0, tiled=True)  33.2 us
    all_to_all x1, blocking collectives, per_device(): lax.all_to_all(part, 'near', 0, 0, tiled=True)  9.3 us
    pallas_call x1, Pallas kernels, per_device(): call(functools.partial(finish, steps, grad_scale), (shape((m, width), BF1...  8.95 us
    unnamed x22, local copies, waits for them, and re-layouts  7.24 us
    pallas_call x1, Pallas kernels, per_device(): call(projections, (shape((ctx, 4, positions, HEAD), BF16), shape((m, 2 *...  6.04 us
  transfers between devices with their start and end apart: 3, of which 2 were waited for; matrix products, arithmetic and copies ran while one was open for 0% of the time, Pallas kernels for 4%

profile of v8, /device:TPU:34, one launch (start us, length us, event | category | flops | bytes accessed | tf_op | source)
XLA Modules:
  0.0 253.3 jit_solution(112116012308509614)
XLA Ops:
  7.2 0.0 all-gather.2.cloned.1.call-start
  7.2 2.1 shard_map.111
  9.3 0.0 copy-start.2
  9.3 0.0 copy-start.8
  9.3 0.0 all-gather.2.cloned.1.call-update
  9.3 0.0 copy-start.9
  9.4 0.9 copy-done.9
  10.2 0.7 copy-done.10
  10.9 0.9 shard_map.112
  11.8 5.9 %all-to-all-start = ((bf16[16,112,128]{2,1,0:T(8,128)(2,1)}), bf16[16,112,128]{2,1,0:T(8,128)(2,1)S(1)}, u32[]{:S(2)}, u32[]{:S(2)}) async-start(bf16[16,112,128]{2,1,0:T(8,128)(2,1)} %shard_map.112), calls=%async_computation | async-start | bytes 917504 | tf_op jit(solution)/shard_map/all_to_all | solution.py:353
  17.7 1.1 copy-done.1
  18.8 1.1 copy-done.3
  20.0 0.8 copy-done.7
  20.7 1.0 shard_map.110
  21.7 0.0 copy-start.5
  21.7 0.9 copy-done.5
  22.6 0.9 copy-done.6
  23.5 1.3 all-to-all-done.maps
  24.8 0.3 shard_map.113
  25.1 0.9 copy-done
  26.0 67.7 %all-gather.2.cloned.1.call-done.w_at = bf16[3072,2048]{1,0:T(8,128)(2,1)} async-done(((bf16[192,2048]{1,0:T(8,128)(2,1)}), bf16[3072,2048]{1,0:T(8,128)(2,1)}) %all-gather.2.cloned.1.call-update) | async-done | bytes 12582928 | tf_op jit(solution)/shard_map/all_gather | solution.py:347
  93.7 6.0 %shard_map.114 = (bf16[32,4,16,128]{3,2,1,0:T(8,128)(2,1)S(1)}, f32[128,1024]{1,0:T(8,128)S(1)}, bf16[128,64]{1,0:T(8,128)(2,1)S(1)}) custom-call(bf16[128,3072]{1,0:T(8,128)(2,1)} %copy-done.5, bf16[128,3072]{1,0:T(8,128)(2,1)} %copy-done.6, bf16[3072,2048]{1,0:T(8,128)(2,1)} %all-gather.2.cloned.1.call-done.w_at, bf16[3072,64]{1,0:T(8,128)(2,1)} %copy-done, ...), custom_call_target="tpu_custom_call" | custom-call | flops 1610612736 | bytes 12582912 | tf_op jit(solution)/shard_map/pallas_call | solution.py:372
  99.7 49.4 %all_to_all.30.rows_in = bf16[32,4,16,128]{3,2,1,0:T(8,128)(2,1)S(1)} all-to-all(bf16[32,4,16,128]{3,2,1,0:T(8,128)(2,1)S(1)} %get-tuple-element.28), channel_id=1, replica_groups=mesh['dp'=16,'yh'=2,'far'=4,'near'=4] {'yh','far','near'}, dimensions={0} | all-to-all | bytes 1048576 | tf_op jit(solution)/shard_map/all_to_all | solution.py:398
  149.1 1.2 shard_map.115
  150.3 37.4 %all_to_all.31.back = bf16[32,4,16,128]{3,2,1,0:T(8,128)(2,1)S(1)} all-to-all(bf16[32,4,16,128]{3,2,1,0:T(8,128)(2,1)S(1)} %shard_map.115), channel_id=1, replica_groups=mesh['dp'=16,'yh'=2,'far'=4,'near'=4] {'yh','far','near'}, dimensions={0} | all-to-all | bytes 1048576 | tf_op jit(solution)/shard_map/all_to_all | solution.py:407
  187.7 1.7 shard_map.116
  189.4 4.7 %all-to-all-start.3 = ((bf16[16,112,128]{2,1,0:T(8,128)(2,1)}), bf16[16,112,128]{2,1,0:T(8,128)(2,1)S(1)}, u32[]{:S(2)}, u32[]{:S(2)}) async-start(bf16[16,112,128]{2,1,0:T(8,128)(2,1)} %get-tuple-element.38), calls=%async_computation.3 | async-start | bytes 917504 | tf_op jit(solution)/shard_map/all_to_all | solution.py:419
  194.1 8.9 %shard_map.117 = (bf16[128,3072]{1,0:T(8,128)(2,1)}, bf16[128,3072]{1,0:T(8,128)(2,1)}, f32[72,128]{1,0:T(8,128)S(1)}) custom-call(bf16[128,1536]{1,0:T(8,128)(2,1)S(1)} %get-tuple-element.32.joined, bf16[128,64]{1,0:T(8,128)(2,1)S(1)} %get-tuple-element.33.low_grad, bf16[32,4,16,128]{3,2,1,0:T(8,128)(2,1)S(1)} %all_to_all.31.back, ...), custom_call_target="tpu_custom_call" | custom-call | flops 1610612736 | bytes 15728640 | tf_op jit(solution)/shard_map/pallas_call | solution.py:422
  203.0 0.1 shard_map.118
  203.1 9.3 %all_to_all.32.arrived = bf16[4,184,128]{2,1,0:T(8,128)(2,1)S(1)} all-to-all(bf16[4,184,128]{2,1,0:T(8,128)(2,1)S(1)} %shard_map.118), channel_id=1, replica_groups=mesh['dp'=16,'yh'=2,'far'=4,'near'=4] {'near'}, dimensions={0} | all-to-all | bytes 376832 | tf_op jit(solution)/shard_map/all_to_all | solution.py:446
  212.5 33.2 %all_to_all.33.arrived = bf16[8,184,128]{2,1,0:T(8,128)(2,1)S(1)} all-to-all(bf16[8,184,128]{2,1,0:T(8,128)(2,1)S(1)} %shard_map.119), channel_id=1, replica_groups=mesh['dp'=16,'yh'=2,'far'=4,'near'=4] {'yh','far'}, dimensions={0} | all-to-all | bytes 753664 | tf_op jit(solution)/shard_map/all_to_all | solution.py:457
  245.7 0.8 shard_map.120
  (13 shorter events, 0.1 us)
Async XLA Ops:
  7.2 86.5 %all-gather.2.cloned.1.call-start = ((), (), s32[]{:S(2)}) async-start(), calls=%async_computation.6 | async-start | bytes 13369344 | tf_op jit(solution)/shard_map/all_gather | solution.py:347
  9.3 184.8 %copy-start.2 = (bf16[1,1,128,3072]{3,2,1,0:T(8,128)(2,1)S(1)}, bf16[1,1,128,3072]{3,2,1,0:T(8,128)(2,1)}, u32[]{:S(2)}) copy-start(bf16[1,1,128,3072]{3,2,1,0:T(8,128)(2,1)} %param.7) | copy-start | bytes 2359300
  9.3 184.8 %copy-start.4 = (bf16[1,1,128,3072]{3,2,1,0:T(8,128)(2,1)S(1)}, bf16[1,1,128,3072]{3,2,1,0:T(8,128)(2,1)}, u32[]{:S(2)}) copy-start(bf16[1,1,128,3072]{3,2,1,0:T(8,128)(2,1)} %param.13) | copy-start | bytes 2359300
  9.3 184.8 %copy-start.8 = (f32[1,3,3072]{2,0,1:T(1,128)S(1)}, f32[1,3,3072]{2,0,1:T(1,128)}, u32[]{:S(2)}) copy-start(f32[1,3,3072]{2,0,1:T(1,128)} %param.8) | copy-start | bytes 110596
  9.3 0.9 copy-start.9
  10.2 0.7 copy-start.10
  11.8 13.0 %all-to-all-start = ((bf16[16,112,128]{2,1,0:T(8,128)(2,1)}), bf16[16,112,128]{2,1,0:T(8,128)(2,1)S(1)}, u32[]{:S(2)}, u32[]{:S(2)}) async-start(bf16[16,112,128]{2,1,0:T(8,128)(2,1)} %shard_map.112), calls=%async_computation | async-start | bytes 917504 | tf_op jit(solution)/shard_map/all_to_all | solution.py:353
  17.7 1.1 copy-start.1
  18.8 1.1 copy-start.3
  20.0 0.8 copy-start.7
  21.7 0.9 copy-start.5
  22.6 0.9 copy-start.6
  25.1 0.9 copy-start
  189.4 13.7 %all-to-all-start.3 = ((bf16[16,112,128]{2,1,0:T(8,128)(2,1)}), bf16[16,112,128]{2,1,0:T(8,128)(2,1)S(1)}, u32[]{:S(2)}, u32[]{:S(2)}) async-start(bf16[16,112,128]{2,1,0:T(8,128)(2,1)} %get-tuple-element.38), calls=%async_computation.3 | async-start | bytes 917504 | tf_op jit(solution)/shard_map/all_to_all | solution.py:419
Sparse Core Ops, SparseCore 0:
  10.1 83.4 all-gather.1

commit v9 on v8

--- a/solution.py
+++ b/solution.py
@@ -294,33 +294,43 @@
         ).astype(BF16)
 
 
-def spread(arrived, mod_rows, copies):
+def spread(arrived, mod_rows, both):
     share = jnp.sum(arrived[...].astype(F32), 0).astype(BF16)
     rows = mod_rows[...].astype(BF16)
-    for j in range(copies.shape[0]):
-        copies[j, : share.shape[0]] = share
-        copies[j, share.shape[0] :] = rows
-
-
-def summed(arrived, copies):
+    parts = both.shape[0]
+    rows_a, rows_b = share.shape[0] // parts, rows.shape[0] // parts
+    pad = jnp.zeros((both.shape[1] - rows_a - rows_b, HEAD), F32)
+    for j in range(parts):
+        piece = jnp.concatenate(
+            [
+                share[j * rows_a : (j + 1) * rows_a].astype(F32),
+                rows[j * rows_b : (j + 1) * rows_b].astype(F32),
+                pad,
+            ],
+            0,
+        )
+        both[j] = piece.astype(BF16)
+
+
+def summed(arrived, out):
     total = jnp.sum(arrived[...].astype(F32), 0).astype(BF16)
-    copies[...] = jnp.broadcast_to(total[None], copies.shape)
-
-
-def collected(arrived, down_t, up_grad, mod_grad):
-    total = jnp.sum(arrived[...].astype(F32), 0)
-    cols, own = down_t.shape[0], up_grad.shape[0]
+    out[...] = jnp.broadcast_to(total[None], out.shape)
+
+
+def collected(rows_a, rows_b, shares, down_t, up_grad, mod_grad):
+    values = shares[...].astype(F32)
+    parts = values.shape[0]
+    cols = down_t.shape[0]
+    own = up_grad.shape[0]
     half = down_t.shape[1] // 2
-    down_t[...] = jnp.concatenate([total[:half, :cols], total[:half, cols:]], 0).T
-    heads = up_grad.shape[1] // HEAD
-    for h in range(heads):
-        up_grad[:, h * HEAD : (h + 1) * HEAD] = total[half + h * own : half + (h + 1) * own]
+    a = jnp.concatenate([values[j, :rows_a] for j in range(parts)], 0)
+    b = jnp.concatenate([values[j, rows_a : rows_a + rows_b] for j in range(parts)], 0)
+    down_t[...] = jnp.concatenate([a[:half, :cols], a[:half, cols:]], 0).T
+    for h in range(up_grad.shape[1] // HEAD):
+        up_grad[:, h * HEAD : (h + 1) * HEAD] = a[half + h * own : half + (h + 1) * own]
     tiles = mod_grad.shape[2] // HEAD
-    first = half + heads * own
     for i in range(3 * tiles):
-        mod_grad[i // tiles, :, (i % tiles) * HEAD : (i % tiles + 1) * HEAD] = total[
-            first + i : first + i + 1
-        ]
+        mod_grad[i // tiles, :, (i % tiles) * HEAD : (i % tiles + 1) * HEAD] = b[i : i + 1]
 
 
 def per_device(tokens, modulation, qkv, out_w, down_w, up_w, output_gradient):
@@ -440,21 +450,25 @@
     )(joined, low_grad, back, x, mean, rstd, mod, upstream, w, w_down)
 
     near, far = lax.axis_size("near"), lax.axis_size("yh") * lax.axis_size("far")
-    rows = own_rows + mod_rows.shape[0]
-    part = call(spread, shape((near, rows, HEAD), BF16), moved=2**19, vmem=8)(arrived, mod_rows)
-    part = call(summed, shape((far, rows, HEAD), BF16), moved=2**19, vmem=8)(
-        lax.all_to_all(part, "near", 0, 0, tiled=True)
+    rows_a, rows_b = own_rows // near, mod_rows.shape[0] // near
+    rows = 16 * -(-(rows_a + rows_b) // 16)
+    both = call(spread, shape((near, rows, HEAD), BF16), moved=2**19, vmem=8)(arrived, mod_rows)
+    part = call(summed, shape((far, rows, HEAD), BF16), moved=2**17, vmem=8)(
+        lax.all_to_all(both, "near", 0, 0, tiled=True)
+    )
+    part = call(summed, shape((near, rows, HEAD), BF16), moved=2**17, vmem=8)(
+        lax.all_to_all(part, ("yh", "far"), 0, 0, tiled=True)
     )
     down_t, up_grad, mod_grad = call(
-        collected,
+        functools.partial(collected, rows_a, rows_b),
         (
             shape((2 * rank, own), F32),
             shape((2 * rank // dp, n), F32),
             shape((3, 1, width), F32),
         ),
-        moved=2**19,
+        moved=2**18,
         vmem=8,
-    )(lax.all_to_all(part, ("yh", "far"), 0, 0, tiled=True))
+    )(lax.all_to_all(part, "near", 0, 0, tiled=True))
     return (
         mixed.reshape(tokens.shape),
         tokens_grad.reshape(tokens.shape),

time: 254 us -> 249 us (0.980)
  the two profiles are of different devices: /device:TPU:34 before, /device:TPU:24 now
where the time goes in v9:
time: 249 us; the launch traced here: 247 us
  blocking collectives  122 us (49%)
  waiting for transfers between devices  69.3 us (28%)
  Pallas kernels  23 us (9%)
  between operations  14.2 us (6%)
  starting transfers between devices  11.3 us (5%)
  local copies, waits for them, and re-layouts  7.24 us (3%)
    all_gather x1, waiting for transfers between devices, per_device(): w = lax.all_gather(packed, 'dp', axis=0, tiled=True)  66.3 us
    all_to_all x1, blocking collectives, per_device(): rows_in = lax.all_to_all(sent, CTX, 0, 0, tiled=True)  45.3 us
    all_to_all x1, blocking collectives, per_device(): back = lax.all_to_all(back_sent, CTX, 0, 0, tiled=True)  38.3 us
    all_to_all x1, blocking collectives, per_device(): lax.all_to_all(part, ('yh', 'far'), 0, 0, tiled=True)  19.8 us
    all_to_all x1, blocking collectives, per_device(): lax.all_to_all(both, 'near', 0, 0, tiled=True)  9.68 us
    all_to_all x1, blocking collectives, per_device(): lax.all_to_all(part, 'near', 0, 0, tiled=True)  9.02 us
    pallas_call x1, Pallas kernels, per_device(): call(functools.partial(finish, steps, grad_scale), (shape((m, width), BF1...  8.95 us
    unnamed x22, local copies, waits for them, and re-layouts  7.24 us
  transfers between devices with their start and end apart: 3, of which 2 were waited for; matrix products, arithmetic and copies ran while one was open for 0% of the time, Pallas kernels for 5%

profile of v9, /device:TPU:24, one launch (start us, length us, event | category | flops | bytes accessed | tf_op | source)
XLA Modules:
  0.0 247.0 jit_solution(1461244627654035606)
XLA Ops:
  7.2 0.0 all-gather.2.cloned.1.call-start
  7.2 2.1 shard_map.111
  9.3 0.0 copy-start.2
  9.3 0.0 copy-start.8
  9.3 0.0 all-gather.2.cloned.1.call-update
  9.3 0.0 copy-start.9
  9.4 0.9 copy-done.9
  10.2 0.7 copy-done.10
  10.9 0.9 shard_map.112
  11.8 5.8 %all-to-all-start = ((bf16[16,112,128]{2,1,0:T(8,128)(2,1)}), bf16[16,112,128]{2,1,0:T(8,128)(2,1)S(1)}, u32[]{:S(2)}, u32[]{:S(2)}) async-start(bf16[16,112,128]{2,1,0:T(8,128)(2,1)} %shard_map.112), calls=%async_computation | async-start | bytes 917504 | tf_op jit(solution)/shard_map/all_to_all | solution.py:363
  17.6 1.1 copy-done.1
  18.8 1.1 copy-done.3
  19.9 0.8 copy-done.7
  20.7 1.0 shard_map.110
  21.6 0.9 copy-done.5
  22.5 0.9 copy-done.6
  23.4 3.0 %all-to-all-done.maps = bf16[16,112,128]{2,1,0:T(8,128)(2,1)S(1)} async-done(((bf16[16,112,128]{2,1,0:T(8,128)(2,1)}), bf16[16,112,128]{2,1,0:T(8,128)(2,1)S(1)}, u32[]{:S(2)}, u32[]{:S(2)}) %all-to-all-start) | async-done | bytes 458784 | tf_op jit(solution)/shard_map/all_to_all | solution.py:363
  26.4 0.3 shard_map.113
  26.7 0.9 copy-done
  27.6 66.3 %all-gather.2.cloned.1.call-done.w_at = bf16[3072,2048]{1,0:T(8,128)(2,1)} async-done(((bf16[192,2048]{1,0:T(8,128)(2,1)}), bf16[3072,2048]{1,0:T(8,128)(2,1)}) %all-gather.2.cloned.1.call-update) | async-done | bytes 12582928 | tf_op jit(solution)/shard_map/all_gather | solution.py:357
  93.9 6.0 %shard_map.114 = (bf16[32,4,16,128]{3,2,1,0:T(8,128)(2,1)S(1)}, f32[128,1024]{1,0:T(8,128)S(1)}, bf16[128,64]{1,0:T(8,128)(2,1)S(1)}) custom-call(bf16[128,3072]{1,0:T(8,128)(2,1)} %copy-done.5, bf16[128,3072]{1,0:T(8,128)(2,1)} %copy-done.6, bf16[3072,2048]{1,0:T(8,128)(2,1)} %all-gather.2.cloned.1.call-done.w_at, bf16[3072,64]{1,0:T(8,128)(2,1)} %copy-done, ...), custom_call_target="tpu_custom_call" | custom-call | flops 1610612736 | bytes 12582912 | tf_op jit(solution)/shard_map/pallas_call | solution.py:382
  99.9 45.3 %all_to_all.35.rows_in = bf16[32,4,16,128]{3,2,1,0:T(8,128)(2,1)S(1)} all-to-all(bf16[32,4,16,128]{3,2,1,0:T(8,128)(2,1)S(1)} %get-tuple-element.28), channel_id=1, replica_groups=mesh['dp'=16,'yh'=2,'far'=4,'near'=4] {'yh','far','near'}, dimensions={0} | all-to-all | bytes 1048576 | tf_op jit(solution)/shard_map/all_to_all | solution.py:408
  145.2 1.2 shard_map.115
  146.4 38.3 %all_to_all.36.back = bf16[32,4,16,128]{3,2,1,0:T(8,128)(2,1)S(1)} all-to-all(bf16[32,4,16,128]{3,2,1,0:T(8,128)(2,1)S(1)} %shard_map.115), channel_id=1, replica_groups=mesh['dp'=16,'yh'=2,'far'=4,'near'=4] {'yh','far','near'}, dimensions={0} | all-to-all | bytes 1048576 | tf_op jit(solution)/shard_map/all_to_all | solution.py:417
  184.7 1.7 shard_map.116
  186.4 5.4 %all-to-all-start.3 = ((bf16[16,112,128]{2,1,0:T(8,128)(2,1)}), bf16[16,112,128]{2,1,0:T(8,128)(2,1)S(1)}, u32[]{:S(2)}, u32[]{:S(2)}) async-start(bf16[16,112,128]{2,1,0:T(8,128)(2,1)} %get-tuple-element.38), calls=%async_computation.3 | async-start | bytes 917504 | tf_op jit(solution)/shard_map/all_to_all | solution.py:429
  191.8 8.9 %shard_map.117 = (bf16[128,3072]{1,0:T(8,128)(2,1)}, bf16[128,3072]{1,0:T(8,128)(2,1)}, f32[72,128]{1,0:T(8,128)S(1)}) custom-call(bf16[128,1536]{1,0:T(8,128)(2,1)S(1)} %get-tuple-element.32.joined, bf16[128,64]{1,0:T(8,128)(2,1)S(1)} %get-tuple-element.33.low_grad, bf16[32,4,16,128]{3,2,1,0:T(8,128)(2,1)S(1)} %all_to_all.36.back, ...), custom_call_target="tpu_custom_call" | custom-call | flops 1610612736 | bytes 15728640 | tf_op jit(solution)/shard_map/pallas_call | solution.py:432
  200.8 0.1 shard_map.118
  200.9 9.7 %all_to_all.37.arrived = bf16[4,48,128]{2,1,0:T(8,128)(2,1)S(1)} all-to-all(bf16[4,48,128]{2,1,0:T(8,128)(2,1)S(1)} %shard_map.118), channel_id=1, replica_groups=mesh['dp'=16,'yh'=2,'far'=4,'near'=4] {'near'}, dimensions={0} | all-to-all | bytes 98304 | tf_op jit(solution)/shard_map/all_to_all | solution.py:457
  210.6 19.8 %all_to_all.38.arrived = bf16[8,48,128]{2,1,0:T(8,128)(2,1)S(1)} all-to-all(bf16[8,48,128]{2,1,0:T(8,128)(2,1)S(1)} %shard_map.119), channel_id=1, replica_groups=mesh['dp'=16,'yh'=2,'far'=4,'near'=4] {'yh','far'}, dimensions={0} | all-to-all | bytes 196608 | tf_op jit(solution)/shard_map/all_to_all | solution.py:460
  230.4 9.0 %all_to_all.39.shares = bf16[4,48,128]{2,1,0:T(8,128)(2,1)S(1)} all-to-all(bf16[4,48,128]{2,1,0:T(8,128)(2,1)S(1)} %shard_map.120), channel_id=1, replica_groups=mesh['dp'=16,'yh'=2,'far'=4,'near'=4] {'near'}, dimensions={0} | all-to-all | bytes 98304 | tf_op jit(solution)/shard_map/all_to_all | solution.py:471
  239.4 0.8 shard_map.121
  (15 shorter events, 0.1 us)
Async XLA Ops:
  7.2 86.7 %all-gather.2.cloned.1.call-start = ((), (), s32[]{:S(2)}) async-start(), calls=%async_computation.7 | async-start | bytes 13369344 | tf_op jit(solution)/shard_map/all_gather | solution.py:357
  9.3 182.5 %copy-start.2 = (bf16[1,1,128,3072]{3,2,1,0:T(8,128)(2,1)S(1)}, bf16[1,1,128,3072]{3,2,1,0:T(8,128)(2,1)}, u32[]{:S(2)}) copy-start(bf16[1,1,128,3072]{3,2,1,0:T(8,128)(2,1)} %param.7) | copy-start | bytes 2359300
  9.3 182.5 %copy-start.4 = (bf16[1,1,128,3072]{3,2,1,0:T(8,128)(2,1)S(1)}, bf16[1,1,128,3072]{3,2,1,0:T(8,128)(2,1)}, u32[]{:S(2)}) copy-start(bf16[1,1,128,3072]{3,2,1,0:T(8,128)(2,1)} %param.13) | copy-start | bytes 2359300
  9.3 182.5 %copy-start.8 = (f32[1,3,3072]{2,0,1:T(1,128)S(1)}, f32[1,3,3072]{2,0,1:T(1,128)}, u32[]{:S(2)}) copy-start(f32[1,3,3072]{2,0,1:T(1,128)} %param.8) | copy-start | bytes 110596
  9.3 0.9 copy-start.9
  10.2 0.7 copy-start.10
  11.8 14.6 %all-to-all-start = ((bf16[16,112,128]{2,1,0:T(8,128)(2,1)}), bf16[16,112,128]{2,1,0:T(8,128)(2,1)S(1)}, u32[]{:S(2)}, u32[]{:S(2)}) async-start(bf16[16,112,128]{2,1,0:T(8,128)(2,1)} %shard_map.112), calls=%async_computation | async-start | bytes 917504 | tf_op jit(solution)/shard_map/all_to_all | solution.py:363
  17.6 1.1 copy-start.1
  18.8 1.1 copy-start.3
  19.9 0.8 copy-start.7
  21.6 0.9 copy-start.5
  22.5 0.9 copy-start.6
  26.7 0.9 copy-start
  186.4 14.4 %all-to-all-start.3 = ((bf16[16,112,128]{2,1,0:T(8,128)(2,1)}), bf16[16,112,128]{2,1,0:T(8,128)(2,1)S(1)}, u32[]{:S(2)}, u32[]{:S(2)}) async-start(bf16[16,112,128]{2,1,0:T(8,128)(2,1)} %get-tuple-element.38), calls=%async_computation.3 | async-start | bytes 917504 | tf_op jit(solution)/shard_map/all_to_all | solution.py:429
Sparse Core Ops, SparseCore 0:
  10.1 83.6 all-gather.1

commit v10 on v9

--- a/solution.py
+++ b/solution.py
@@ -71,15 +71,26 @@
     branch_grad[...] = (upstream[...].astype(F32) * mod[2]).astype(BF16)
 
 
-def pack(qkv, out_t, packed, sems):
+def pack(chunks, qkv, out_t, packed, held, sems):
     k, n = qkv.shape[1], out_t.shape[1]
-    copies = [
-        pltpu.make_async_copy(qkv, packed.at[:, pl.ds(0, k)], sems.at[0]),
-        pltpu.make_async_copy(out_t, packed.at[:, pl.ds(k, n)], sems.at[1]),
-    ]
-    for copy in copies:
-        copy.start()
-    for copy in copies:
+    rows = qkv.shape[0] // chunks
+    landing, leaving = [], []
+    for i in range(chunks):
+        at = pl.ds(i * rows, rows)
+        landing.append(
+            (
+                pltpu.make_async_copy(qkv.at[at], held.at[at, pl.ds(0, k)], sems.at[0, i]),
+                pltpu.make_async_copy(out_t.at[at], held.at[at, pl.ds(k, n)], sems.at[1, i]),
+            )
+        )
+        leaving.append(pltpu.make_async_copy(held.at[at], packed.at[at], sems.at[2, i]))
+        for copy in landing[i]:
+            copy.start()
+    for i in range(chunks):
+        for copy in landing[i]:
+            copy.wait()
+        leaving[i].start()
+    for copy in leaving:
         copy.wait()
 
 
@@ -346,11 +357,11 @@
 
     cols = 4 * n
     packed = call(
-        pack,
+        functools.partial(pack, 4),
         shape((own, cols), BF16),
         in_specs=[pl.BlockSpec(memory_space=pl.ANY)] * 2,
-        out_specs=pl.BlockSpec(memory_space=pltpu.VMEM),
-        scratch=[pltpu.SemaphoreType.DMA((2,))],
+        out_specs=pl.BlockSpec(memory_space=pl.ANY),
+        scratch=[pltpu.VMEM((own, cols), BF16), pltpu.SemaphoreType.DMA((3, 4))],
         moved=4 * own * cols,
         vmem=60,
     )(qkv, out_w.T)

time: 249 us -> 249 us (level)
  no operation moved by 1% of the time
where the time goes in v10:
time: 249 us; the launch traced here: 247 us
  blocking collectives  122 us (49%)
  waiting for transfers between devices  69.4 us (28%)
  Pallas kernels  22.9 us (9%)
  between operations  14.2 us (6%)
  starting transfers between devices  11.3 us (5%)
  local copies, waits for them, and re-layouts  7.24 us (3%)
    all_gather x1, waiting for transfers between devices, per_device(): w = lax.all_gather(packed, 'dp', axis=0, tiled=True)  66.4 us
    all_to_all x1, blocking collectives, per_device(): rows_in = lax.all_to_all(sent, CTX, 0, 0, tiled=True)  45.3 us
    all_to_all x1, blocking collectives, per_device(): back = lax.all_to_all(back_sent, CTX, 0, 0, tiled=True)  38.3 us
    all_to_all x1, blocking collectives, per_device(): lax.all_to_all(part, ('yh', 'far'), 0, 0, tiled=True)  19.8 us
    all_to_all x1, blocking collectives, per_device(): lax.all_to_all(both, 'near', 0, 0, tiled=True)  9.68 us
    all_to_all x1, blocking collectives, per_device(): lax.all_to_all(part, 'near', 0, 0, tiled=True)  9.02 us
    pallas_call x1, Pallas kernels, per_device(): call(functools.partial(finish, steps, grad_scale), (shape((m, width), BF1...  8.95 us
    unnamed x22, local copies, waits for them, and re-layouts  7.24 us
  transfers between devices with their start and end apart: 3, of which 2 were waited for; matrix products, arithmetic and copies ran while one was open for 0% of the time, Pallas kernels for 5%

profile of v10, /device:TPU:24, one launch (start us, length us, event | category | flops | bytes accessed | tf_op | source)
XLA Modules:
  0.0 247.0 jit_solution(17877921816490907358)
XLA Ops:
  7.2 0.0 all-gather.2.cloned.1.call-start
  7.2 2.0 shard_map.111
  9.2 0.0 copy-start.2
  9.2 0.0 copy-start.8
  9.2 0.0 all-gather.2.cloned.1.call-update
  9.3 0.0 copy-start.9
  9.3 0.9 copy-done.9
  10.1 0.7 copy-done.10
  10.8 0.9 shard_map.112
  11.8 5.8 %all-to-all-start = ((bf16[16,112,128]{2,1,0:T(8,128)(2,1)}), bf16[16,112,128]{2,1,0:T(8,128)(2,1)S(1)}, u32[]{:S(2)}, u32[]{:S(2)}) async-start(bf16[16,112,128]{2,1,0:T(8,128)(2,1)} %shard_map.112), calls=%async_computation | async-start | bytes 917504 | tf_op jit(solution)/shard_map/all_to_all | solution.py:374
  17.5 1.1 copy-done.1
  18.7 1.1 copy-done.3
  19.8 0.8 copy-done.7
  20.6 1.0 shard_map.110
  21.6 0.9 copy-done.5
  22.4 0.9 copy-done.6
  23.3 3.0 %all-to-all-done.maps = bf16[16,112,128]{2,1,0:T(8,128)(2,1)S(1)} async-done(((bf16[16,112,128]{2,1,0:T(8,128)(2,1)}), bf16[16,112,128]{2,1,0:T(8,128)(2,1)S(1)}, u32[]{:S(2)}, u32[]{:S(2)}) %all-to-all-start) | async-done | bytes 458784 | tf_op jit(solution)/shard_map/all_to_all | solution.py:374
  26.3 0.3 shard_map.113
  26.6 0.9 copy-done
  27.5 66.4 %all-gather.2.cloned.1.call-done.w_at = bf16[3072,2048]{1,0:T(8,128)(2,1)} async-done(((bf16[192,2048]{1,0:T(8,128)(2,1)}), bf16[3072,2048]{1,0:T(8,128)(2,1)}) %all-gather.2.cloned.1.call-update) | async-done | bytes 12582928 | tf_op jit(solution)/shard_map/all_gather | solution.py:368
  93.9 6.0 %shard_map.114 = (bf16[32,4,16,128]{3,2,1,0:T(8,128)(2,1)S(1)}, f32[128,1024]{1,0:T(8,128)S(1)}, bf16[128,64]{1,0:T(8,128)(2,1)S(1)}) custom-call(bf16[128,3072]{1,0:T(8,128)(2,1)} %copy-done.5, bf16[128,3072]{1,0:T(8,128)(2,1)} %copy-done.6, bf16[3072,2048]{1,0:T(8,128)(2,1)} %all-gather.2.cloned.1.call-done.w_at, bf16[3072,64]{1,0:T(8,128)(2,1)} %copy-done, ...), custom_call_target="tpu_custom_call" | custom-call | flops 1610612736 | bytes 12582912 | tf_op jit(solution)/shard_map/pallas_call | solution.py:393
  99.9 45.3 %all_to_all.35.rows_in = bf16[32,4,16,128]{3,2,1,0:T(8,128)(2,1)S(1)} all-to-all(bf16[32,4,16,128]{3,2,1,0:T(8,128)(2,1)S(1)} %get-tuple-element.28), channel_id=1, replica_groups=mesh['dp'=16,'yh'=2,'far'=4,'near'=4] {'yh','far','near'}, dimensions={0} | all-to-all | bytes 1048576 | tf_op jit(solution)/shard_map/all_to_all | solution.py:419
  145.2 1.2 shard_map.115
  146.4 38.3 %all_to_all.36.back = bf16[32,4,16,128]{3,2,1,0:T(8,128)(2,1)S(1)} all-to-all(bf16[32,4,16,128]{3,2,1,0:T(8,128)(2,1)S(1)} %shard_map.115), channel_id=1, replica_groups=mesh['dp'=16,'yh'=2,'far'=4,'near'=4] {'yh','far','near'}, dimensions={0} | all-to-all | bytes 1048576 | tf_op jit(solution)/shard_map/all_to_all | solution.py:428
  184.7 1.7 shard_map.116
  186.4 5.4 %all-to-all-start.3 = ((bf16[16,112,128]{2,1,0:T(8,128)(2,1)}), bf16[16,112,128]{2,1,0:T(8,128)(2,1)S(1)}, u32[]{:S(2)}, u32[]{:S(2)}) async-start(bf16[16,112,128]{2,1,0:T(8,128)(2,1)} %get-tuple-element.38), calls=%async_computation.3 | async-start | bytes 917504 | tf_op jit(solution)/shard_map/all_to_all | solution.py:440
  191.8 8.9 %shard_map.117 = (bf16[128,3072]{1,0:T(8,128)(2,1)}, bf16[128,3072]{1,0:T(8,128)(2,1)}, f32[72,128]{1,0:T(8,128)S(1)}) custom-call(bf16[128,1536]{1,0:T(8,128)(2,1)S(1)} %get-tuple-element.32.joined, bf16[128,64]{1,0:T(8,128)(2,1)S(1)} %get-tuple-element.33.low_grad, bf16[32,4,16,128]{3,2,1,0:T(8,128)(2,1)S(1)} %all_to_all.36.back, ...), custom_call_target="tpu_custom_call" | custom-call | flops 1610612736 | bytes 15728640 | tf_op jit(solution)/shard_map/pallas_call | solution.py:443
  200.8 0.1 shard_map.118
  200.9 9.7 %all_to_all.37.arrived = bf16[4,48,128]{2,1,0:T(8,128)(2,1)S(1)} all-to-all(bf16[4,48,128]{2,1,0:T(8,128)(2,1)S(1)} %shard_map.118), channel_id=1, replica_groups=mesh['dp'=16,'yh'=2,'far'=4,'near'=4] {'near'}, dimensions={0} | all-to-all | bytes 98304 | tf_op jit(solution)/shard_map/all_to_all | solution.py:468
  210.6 19.8 %all_to_all.38.arrived = bf16[8,48,128]{2,1,0:T(8,128)(2,1)S(1)} all-to-all(bf16[8,48,128]{2,1,0:T(8,128)(2,1)S(1)} %shard_map.119), channel_id=1, replica_groups=mesh['dp'=16,'yh'=2,'far'=4,'near'=4] {'yh','far'}, dimensions={0} | all-to-all | bytes 196608 | tf_op jit(solution)/shard_map/all_to_all | solution.py:471
  230.4 9.0 %all_to_all.39.shares = bf16[4,48,128]{2,1,0:T(8,128)(2,1)S(1)} all-to-all(bf16[4,48,128]{2,1,0:T(8,128)(2,1)S(1)} %shard_map.120), channel_id=1, replica_groups=mesh['dp'=16,'yh'=2,'far'=4,'near'=4] {'near'}, dimensions={0} | all-to-all | bytes 98304 | tf_op jit(solution)/shard_map/all_to_all | solution.py:482
  239.4 0.8 shard_map.121
  (15 shorter events, 0.1 us)
Async XLA Ops:
  7.2 86.7 %all-gather.2.cloned.1.call-start = ((), (), s32[]{:S(2)}) async-start(), calls=%async_computation.7 | async-start | bytes 13369344 | tf_op jit(solution)/shard_map/all_gather | solution.py:368
  9.2 182.6 %copy-start.2 = (bf16[1,1,128,3072]{3,2,1,0:T(8,128)(2,1)S(1)}, bf16[1,1,128,3072]{3,2,1,0:T(8,128)(2,1)}, u32[]{:S(2)}) copy-start(bf16[1,1,128,3072]{3,2,1,0:T(8,128)(2,1)} %param.7) | copy-start | bytes 2359300
  9.2 182.6 %copy-start.4 = (bf16[1,1,128,3072]{3,2,1,0:T(8,128)(2,1)S(1)}, bf16[1,1,128,3072]{3,2,1,0:T(8,128)(2,1)}, u32[]{:S(2)}) copy-start(bf16[1,1,128,3072]{3,2,1,0:T(8,128)(2,1)} %param.13) | copy-start | bytes 2359300
  9.2 182.6 %copy-start.8 = (f32[1,3,3072]{2,0,1:T(1,128)S(1)}, f32[1,3,3072]{2,0,1:T(1,128)}, u32[]{:S(2)}) copy-start(f32[1,3,3072]{2,0,1:T(1,128)} %param.8) | copy-start | bytes 110596
  9.3 0.9 copy-start.9
  10.1 0.7 copy-start.10
  11.8 14.6 %all-to-all-start = ((bf16[16,112,128]{2,1,0:T(8,128)(2,1)}), bf16[16,112,128]{2,1,0:T(8,128)(2,1)S(1)}, u32[]{:S(2)}, u32[]{:S(2)}) async-start(bf16[16,112,128]{2,1,0:T(8,128)(2,1)} %shard_map.112), calls=%async_computation | async-start | bytes 917504 | tf_op jit(solution)/shard_map/all_to_all | solution.py:374
  17.5 1.1 copy-start.1
  18.7 1.1 copy-start.3
  19.8 0.8 copy-start.7
  21.6 0.9 copy-start.5
  22.4 0.9 copy-start.6
  26.6 0.9 copy-start
  186.4 14.4 %all-to-all-start.3 = ((bf16[16,112,128]{2,1,0:T(8,128)(2,1)}), bf16[16,112,128]{2,1,0:T(8,128)(2,1)S(1)}, u32[]{:S(2)}, u32[]{:S(2)}) async-start(bf16[16,112,128]{2,1,0:T(8,128)(2,1)} %get-tuple-element.38), calls=%async_computation.3 | async-start | bytes 917504 | tf_op jit(solution)/shard_map/all_to_all | solution.py:440
Sparse Core Ops, SparseCore 0:
  10.1 83.6 all-gather.1
